TPU v7x, 32 devices: a whole 2x2x4 slice. The times are simulated.
32 devices in a mesh: grp: 2 (over x), ctx: 4 (over z), wsh: 4 (over y, core).
Axes of the slice: x: 2, y: 2, z: 4, core: 2. Of those that a mesh axis runs over, the one named last changes fastest.
Arguments:
- inputs: bfloat16 [2, 4, 2048, 1024], P('grp', 'wsh', 'ctx'), may hold values from -6 to 6
- w_qkv: bfloat16 [1024, 3072], P('wsh'), may hold values from -0.1875 to 0.1875
- w_out: bfloat16 [1024, 1024], P('wsh'), may hold values from -0.1875 to 0.1875
- w_up: bfloat16 [1024, 4096], P('wsh'), may hold values from -0.1875 to 0.1875
- w_down: bfloat16 [4096, 1024], P('wsh'), may hold values from -0.09375 to 0.09375
- norm_gains: float32 [4, 1024], replicated, may hold values from 0.5 to 1.5
- norm_biases: float32 [4, 1024], replicated, may hold values from -2 to 2
- block_map: int32 [2, 4, 4, 2], P('grp', 'wsh', 'ctx'), may hold values from 0 to 1024, as said below
- out_grad: bfloat16 [2, 4, 2048, 1024], P('grp', 'wsh', 'ctx'), may hold values from -6 to 6
Outputs:
- output: bfloat16 [2, 4, 2048, 1024], P('grp', 'wsh', 'ctx')
- input_grad: float32 [2, 4, 2048, 1024], P('grp', 'wsh', 'ctx')
- grad_qkv: float32 [1024, 3072], P('wsh')
- grad_attn_out: float32 [1024, 1024], P('wsh')
- grad_up: float32 [1024, 4096], P('wsh')
- grad_down: float32 [4096, 1024], P('wsh')
- grad_gains: float32 [4, 1024], replicated
- grad_biases: float32 [4, 1024], replicated
Inputs may be any that keep to these rules, and one draw needn't show every extreme that they name: `block_map`: for each grp and wsh index the 4 context blocks are the 2 prompt blocks (sequence 0, first positions 0, 512, 1024 and so on) and one block of each continuation 1 to 4 // 2 (first position 1024), in an order drawn for each family.
All inputs are finite; a program needn't handle non-finite values.
Results may differ from a plain program's by a relative error of at most 0.017.
Values may be sent and summed in bfloat16 or wider, within the bound.
A program may use at most 384 MiB of HBM per device.

v0:
```python
import math

import jax
import jax.numpy as jnp
from jax import lax
from jax.sharding import PartitionSpec as P

D = 1024
HEADS = 16
DH = 64
BLK = 512


EPS = 1e-05
ALPHA = 32.0
NEG = -1e30


def layer_norm(values, gain_row, bias_row):
    centre = values - jnp.mean(values, axis=-1, keepdims=True)
    spread = jnp.mean(centre * centre, axis=-1, keepdims=True)
    return centre * lax.rsqrt(spread + EPS) * gain_row + bias_row


def gelu_tanh(values):
    return jax.nn.gelu(values, approximate=True)


def contract_last(left_side, right_side):
    return lax.dot_general(
        left_side, right_side, (((1,), (1,)), ((), ())), preferred_element_type=jnp.float32
    )


def contract_rows(left_side, right_side):
    return lax.dot_general(
        left_side, right_side, (((0,), (0,)), ((), ())), preferred_element_type=jnp.float32
    )


def allowed(query_tags, key_tags):
    same_doc = (key_tags[None, :, 0] == query_tags[:, None, 0]) | (key_tags[None, :, 0] == 0)
    return same_doc & (key_tags[None, :, 1] <= query_tags[:, None, 1])


def scores(queries, key_block, permit):
    raw_scores = jnp.einsum("qhd,khd->hqk", queries, key_block, preferred_element_type=jnp.float32)
    return jnp.where(permit[None], raw_scores * ALPHA, NEG)


def no_output(step_rows):
    return None


def zero_terms(step_rows):
    zero_rows = jnp.zeros((step_rows, HEADS, DH), jnp.float32)
    return (zero_rows, zero_rows)


def sweep_blocks(members, query_tags, state, update, blank):
    total_rows = members[0].shape[0]
    limit_rows = max(query_tags.shape[0], 512)
    block_count = total_rows // limit_rows
    stacked = tuple(
        (member.reshape((block_count, limit_rows) + member.shape[1:]) for member in members)
    )

    def advance(held_state, pieces):
        permit = allowed(query_tags, pieces[-1])

        def active(inner_state):
            return update(inner_state, pieces, permit)

        def passive(inner_state):
            return (inner_state, blank(limit_rows))

        return lax.cond(jnp.any(permit), active, passive, held_state)

    return lax.scan(advance, state, stacked)


def normaliser_update(queries):

    def update(held_state, pieces, permit):
        top_score, exp_total = held_state
        logits = scores(queries, pieces[0], permit)
        new_top = jnp.maximum(top_score, jnp.max(logits, axis=-1))
        kept_exp = jnp.where(permit[None], jnp.exp(logits - new_top[..., None]), 0.0)
        exp_total = exp_total * jnp.exp(top_score - new_top) + jnp.sum(kept_exp, axis=-1)
        return ((new_top, exp_total), None)

    return update


def output_update(queries, log_total):

    def update(held_state, pieces, permit):
        logits = scores(queries, pieces[0], permit)
        weights_low = jnp.where(permit[None], jnp.exp(logits - log_total[..., None]), 0.0).astype(
            jnp.bfloat16
        )
        return (
            held_state
            + jnp.einsum(
                "hqk,khd->qhd", weights_low, pieces[1], preferred_element_type=jnp.float32
            ),
            None,
        )

    return update


def inner_update(queries, log_total, grad_out_low):

    def update(held_state, pieces, permit):
        logits = scores(queries, pieces[0], permit)
        probs_full = jnp.where(permit[None], jnp.exp(logits - log_total[..., None]), 0.0)
        grad_probs = jnp.einsum(
            "qhd,khd->hqk", grad_out_low, pieces[1], preferred_element_type=jnp.float32
        )
        return (held_state + jnp.sum(probs_full * grad_probs, axis=-1), None)

    return update


def gradient_update(queries, log_total, grad_out_low, inner_sum):

    def update(held_state, pieces, permit):
        logits = scores(queries, pieces[0], permit)
        probs_full = jnp.where(permit[None], jnp.exp(logits - log_total[..., None]), 0.0)
        grad_probs = jnp.einsum(
            "qhd,khd->hqk", grad_out_low, pieces[1], preferred_element_type=jnp.float32
        )
        grad_logits = (probs_full * (grad_probs - inner_sum[..., None]) * ALPHA).astype(
            jnp.bfloat16
        )
        new_state = held_state + jnp.einsum(
            "hqk,khd->qhd", grad_logits, pieces[0], preferred_element_type=jnp.float32
        )
        key_term = jnp.einsum(
            "hqk,qhd->khd", grad_logits, queries, preferred_element_type=jnp.float32
        )
        value_term = jnp.einsum(
            "hqk,qhd->khd",
            probs_full.astype(jnp.bfloat16),
            grad_out_low,
            preferred_element_type=jnp.float32,
        )
        return (new_state, (key_term, value_term))

    return update


def per_device(inputs, w_qkv, w_out, w_up, w_down, norm_gains, norm_biases, block_map, out_grad):
    query_scale = 1.0 / (ALPHA * math.sqrt(DH))
    tokens = inputs.reshape(BLK, D).astype(jnp.float32)
    full_qkv, full_out, full_up, full_down = (
        lax.all_gather(w_qkv, "wsh", axis=0, tiled=True),
        lax.all_gather(w_out, "wsh", axis=0, tiled=True),
        lax.all_gather(w_up, "wsh", axis=0, tiled=True),
        lax.all_gather(w_down, "wsh", axis=0, tiled=True),
    )
    block_entry = block_map.reshape(2)
    local_tags = jnp.stack(
        [
            jnp.full((BLK,), block_entry[0], jnp.int32),
            block_entry[1] + jnp.arange(BLK, dtype=jnp.int32),
        ],
        axis=1,
    )
    first_norm, first_back = jax.vjp(layer_norm, tokens, norm_gains[0], norm_biases[0])
    normed_low = first_norm.astype(jnp.bfloat16)
    projected = jnp.dot(normed_low, full_qkv, preferred_element_type=jnp.float32)
    queries = (projected[:, :D] * query_scale).astype(jnp.bfloat16).reshape(BLK, HEADS, DH)
    key_local = projected[:, D : 2 * D].astype(jnp.bfloat16)
    value_local = projected[:, 2 * D :].astype(jnp.bfloat16)
    start_top = (jnp.full((HEADS, BLK), NEG, jnp.float32), jnp.zeros((HEADS, BLK), jnp.float32))
    start_out = jnp.zeros((BLK, HEADS, DH), jnp.float32)
    key_all, value_all, tag_all = (
        lax.all_gather(key_local, "ctx", axis=0, tiled=True),
        lax.all_gather(value_local, "ctx", axis=0, tiled=True),
        lax.all_gather(local_tags, "ctx", axis=0, tiled=True),
    )
    key_heads = key_all.reshape(-1, HEADS, DH)
    value_heads = value_all.reshape(-1, HEADS, DH)
    top_score, exp_total = sweep_blocks(
        (key_heads, tag_all), local_tags, start_top, normaliser_update(queries), no_output
    )[0]
    log_total = top_score + jnp.log(exp_total)
    attended = sweep_blocks(
        (key_heads, value_heads, tag_all),
        local_tags,
        start_out,
        output_update(queries, log_total),
        no_output,
    )[0]
    attn_low = attended.reshape(BLK, D).astype(jnp.bfloat16)
    branch = jnp.dot(attn_low, full_out, preferred_element_type=jnp.float32)
    post_attn, attn_back = jax.vjp(layer_norm, branch, norm_gains[1], norm_biases[1])
    hidden = tokens + post_attn
    pre_ffn, ffn_back = jax.vjp(layer_norm, hidden, norm_gains[2], norm_biases[2])
    ffn_low = pre_ffn.astype(jnp.bfloat16)
    upward = jnp.dot(ffn_low, full_up, preferred_element_type=jnp.float32)
    activated, gelu_back = jax.vjp(gelu_tanh, upward)
    active_low = activated.astype(jnp.bfloat16)
    downward = jnp.dot(active_low, full_down, preferred_element_type=jnp.float32)
    post_ffn, post_back = jax.vjp(layer_norm, downward, norm_gains[3], norm_biases[3])
    result = (hidden + post_ffn).astype(jnp.bfloat16).reshape(1, 1, BLK, D)
    seed_grad = out_grad.reshape(BLK, D).astype(jnp.float32)
    grad_down_in, gain_grad3, bias_grad3 = post_back(seed_grad)
    down_low = grad_down_in.astype(jnp.bfloat16)
    grad_active = contract_last(down_low, full_down)
    up_low = gelu_back(grad_active)[0].astype(jnp.bfloat16)
    grad_pre_ffn, gain_grad2, bias_grad2 = ffn_back(contract_last(up_low, full_up))
    grad_hidden = seed_grad + grad_pre_ffn
    grad_branch, gain_grad1, bias_grad1 = attn_back(grad_hidden)
    branch_low = grad_branch.astype(jnp.bfloat16)
    grad_out_low = contract_last(branch_low, full_out).astype(jnp.bfloat16).reshape(BLK, HEADS, DH)
    members = (key_heads, value_heads, tag_all)
    inner_sum = sweep_blocks(
        members,
        local_tags,
        jnp.zeros((HEADS, BLK), jnp.float32),
        inner_update(queries, log_total, grad_out_low),
        no_output,
    )[0]
    grad_queries, key_value_terms = sweep_blocks(
        members,
        local_tags,
        start_out,
        gradient_update(queries, log_total, grad_out_low, inner_sum),
        zero_terms,
    )
    key_terms = key_value_terms[0].reshape(-1, D)
    value_terms = key_value_terms[1].reshape(-1, D)
    key_grad, value_grad = (
        lax.psum_scatter(
            key_terms.astype(jnp.bfloat16), "ctx", scatter_dimension=0, tiled=True
        ).astype(jnp.float32),
        lax.psum_scatter(
            value_terms.astype(jnp.bfloat16), "ctx", scatter_dimension=0, tiled=True
        ).astype(jnp.float32),
    )
    qkv_low = jnp.concatenate(
        [
            grad_queries.reshape(BLK, D).astype(jnp.bfloat16) * query_scale,
            key_grad.astype(jnp.bfloat16),
            value_grad.astype(jnp.bfloat16),
        ],
        axis=1,
    )
    grad_tokens, gain_grad0, bias_grad0 = first_back(contract_last(qkv_low, full_qkv))
    grad_input = (grad_hidden + grad_tokens).reshape(1, 1, BLK, D)
    term_qkv = contract_rows(normed_low, qkv_low)
    term_out = contract_rows(attn_low, branch_low)
    term_up = contract_rows(ffn_low, up_low)
    term_down = contract_rows(active_low, down_low)
    shard_qkv, shard_out, shard_up, shard_down = (
        lax.psum_scatter(
            term_qkv.astype(jnp.bfloat16), "wsh", scatter_dimension=0, tiled=True
        ).astype(jnp.float32),
        lax.psum_scatter(
            term_out.astype(jnp.bfloat16), "wsh", scatter_dimension=0, tiled=True
        ).astype(jnp.float32),
        lax.psum_scatter(
            term_up.astype(jnp.bfloat16), "wsh", scatter_dimension=0, tiled=True
        ).astype(jnp.float32),
        lax.psum_scatter(
            term_down.astype(jnp.bfloat16), "wsh", scatter_dimension=0, tiled=True
        ).astype(jnp.float32),
    )
    summed_qkv, summed_out, summed_up, summed_down = (
        lax.psum(shard_qkv.astype(jnp.bfloat16), ("grp", "ctx")).astype(jnp.float32),
        lax.psum(shard_out.astype(jnp.bfloat16), ("grp", "ctx")).astype(jnp.float32),
        lax.psum(shard_up.astype(jnp.bfloat16), ("grp", "ctx")).astype(jnp.float32),
        lax.psum(shard_down.astype(jnp.bfloat16), ("grp", "ctx")).astype(jnp.float32),
    )
    gain_stack = jnp.stack([gain_grad0, gain_grad1, gain_grad2, gain_grad3])
    bias_stack = jnp.stack([bias_grad0, bias_grad1, bias_grad2, bias_grad3])
    gain_total, bias_total = lax.psum((gain_stack, bias_stack), ("grp", "ctx", "wsh"))
    return (
        result,
        grad_input,
        summed_qkv,
        summed_out,
        summed_up,
        summed_down,
        gain_total,
        bias_total,
    )


def solution(mesh):
    return jax.shard_map(
        per_device,
        mesh=mesh,
        in_specs=(
            P("grp", "wsh", "ctx", None),
            P("wsh", None),
            P("wsh", None),
            P("wsh", None),
            P("wsh", None),
            P(),
            P(),
            P("grp", "wsh", "ctx", None),
            P("grp", "wsh", "ctx", None),
        ),
        out_specs=(
            P("grp", "wsh", "ctx", None),
            P("grp", "wsh", "ctx", None),
            P("wsh", None),
            P("wsh", None),
            P("wsh", None),
            P("wsh", None),
            P(),
            P(),
        ),
        check_vma=False,
    )
```

profile of v0, /device:TPU:0, one launch (start us, length us, event | category | flops | bytes accessed | tf_op | source)
XLA Modules:
  0.0 1250.6 jit_solution(280551970439620946)
XLA Ops:
  10.9 47.8 %all-gather.7.cloned.1.call-done = bf16[1024,3072]{1,0:T(8,128)(2,1)} async-done(((bf16[256,3072]{1,0:T(8,128)(2,1)}), bf16[1024,3072]{1,0:T(8,128)(2,1)}) %all-gather.7.cloned.1.call-update) | async-done | bytes 6291472 | tf_op jit(solution)/shard_map/all_gather | solution.py:158
  73.1 13.6 %all_gather.21 = s32[2048,2]{0,1:T(2,128)S(1)} all-gather(s32[512,2]{0,1:T(2,128)S(1)} %stack.6), channel_id=1, replica_groups=mesh['grp'=2,'ctx'=4,'wsh'=4] {'ctx'}, dimensions={0}, use_global_device_ids=true | all-gather | bytes 20480 | tf_op jit(solution)/shard_map/all_gather | solution.py:182
  92.0 57.6 %all-gather.9.cloned.1.call-done = bf16[2048,1024]{1,0:T(8,128)(2,1)} async-done(((bf16[512,1024]{1,0:T(8,128)(2,1)}), bf16[2048,1024]{1,0:T(8,128)(2,1)}) %all-gather.9.cloned.1.call-update) | async-done | bytes 4194320 | tf_op jit(solution)/shard_map/all_gather | solution.py:180
  179.2 52.0 %all-gather.11.cloned.1.call-done = bf16[2048,1024]{1,0:T(8,128)(2,1)} async-done(((bf16[512,1024]{1,0:T(8,128)(2,1)}), bf16[2048,1024]{1,0:T(8,128)(2,1)}) %all-gather.11.cloned.1.call-update) | async-done | bytes 4194320 | tf_op jit(solution)/shard_map/all_gather | solution.py:181
  231.1 11.7 reshape.274
  252.7 35.8 %while.59 = (s32[]{:T(128)}, f32[16,512]{1,0:T(8,128)S(1)}, f32[16,512]{1,0:T(8,128)S(1)}, s32[4,512,2]{1,2,0:T(2,128)S(1)}, s32[]{:T(128)}, /*index=5*/bf16[4,5...) while((s32[]{:T(128)}, f32[16,512]{1,0:T(8,128)S(1)}, ...), condition=%wide.region_8.9_spmd.clone, body=%wide.region_2.8_spmd.clone.sunk | while | flops 571230208 | bytes 36886224 | solution.py:79
  290.0 49.3 %while.60 = (s32[]{:T(128)}, f32[512,16,64]{0,2,1:T(8,128)}, s32[4,512,2]{1,2,0:T(2,128)S(1)}, s32[]{:T(128)}, bf16[4,512,16,64]{3,2,1,0:T(8,128)(2,1)}, /*index...) while((s32[]{:T(128)}, f32[512,16,64]{0,2,1:T(8,128)}, ...), condition=%wide.region_13.14_spmd.clone, body=%wide.region_9.13_spmd.clone.sunk | while | flops 1096026112 | bytes 11065027 | solution.py:79
  293.5 12.3 conditional.13
  308.7 12.3 conditional.13
  326.9 12.4 conditional.13
  349.0 11.9 fusion.115
  361.0 12.2 all-gather.17.cloned.1.call-done
  388.4 15.7 %fusion.80 = bf16[512,4096]{1,0:T(8,128)(2,1)} fusion(f32[512,4096]{1,0:T(8,128)} %fusion.115, bf16[4096,1024]{1,0:T(8,128)(2,1)} %all-gather.17.cloned.1.call-done, f32[512,1024]{1,0:T(8,128)S(1)} %get-tuple-element.761, f32[512]{0:T(512)S(1)} %negate_multiply_fusion.3), kind=kOutput, calls=%fused_computation.97 | convolution fusion | flops 4337958912 | bytes 23070720 | tf_op jit(solution)/shard_map/dot_general | solution.py:30
  419.2 43.8 %while.61 = (s32[]{:T(128)}, f32[16,512]{1,0:T(8,128)S(1)}, s32[4,512,2]{1,2,0:T(2,128)S(1)}, s32[]{:T(128)}, bf16[4,512,16,64]{1,3,2,0:T(8,128)(2,1)}, /*index=...) while((s32[]{:T(128)}, f32[16,512]{1,0:T(8,128)S(1)}, ...), condition=%wide.region_31.32_spmd.clone, body=%wide.region_26.31_spmd.clone.sunk | while | flops 1099696128 | bytes 38459600 | solution.py:79
  435.8 10.7 conditional.14
  464.3 139.4 %while.62 = (s32[]{:T(128)}, f32[512,16,64]{0,2,1:T(8,128)S(1)}, bf16[4,512,16,64]{1,3,2,0:T(8,128)(2,1)}, bf16[4,512,16,64]{1,3,2,0:T(8,128)(2,1)}, s32[4,512,2...) while((s32[]{:T(128)}, f32[512,16,64]{0,2,1:T(8,128)S(1)}, ...), condition=%wide.region_36.37_spmd.clone, body=%wide.region_32.0_spmd.clone.sunk | while | flops 2740193280 | bytes 94231808 | solution.py:79
  467.7 37.5 %conditional.15 = (f32[512,16,64]{0,2,1:T(8,128)S(1)}, bf16[1,512,16,64]{1,3,2,0:T(8,128)(2,1)}, bf16[1,512,16,64]{1,3,2,0:T(8,128)(2,1)}) conditional(s32[]{:T(128)} %convert_element_type.266, f32[512,16,64]{0,2,1:T(8,128)S(1)} %get-tuple-element.1188, (pred[512,512]{0,1:T(8,128)(4,1)S(1)}, bf16[4,512,16,64]{1,3,2,0:T(8,128)(2,1)}, s32[]{:T(128)}, ...), branch_computations={%region_34.34_spmd, %region_35.35_spmd} | conditional | flops 2739404800 | bytes 89753112 | solution.py:77
  477.0 11.3 fusion.54
  511.3 37.5 %conditional.15 = (f32[512,16,64]{0,2,1:T(8,128)S(1)}, bf16[1,512,16,64]{1,3,2,0:T(8,128)(2,1)}, bf16[1,512,16,64]{1,3,2,0:T(8,128)(2,1)}) conditional(s32[]{:T(128)} %convert_element_type.266, f32[512,16,64]{0,2,1:T(8,128)S(1)} %get-tuple-element.1188, (pred[512,512]{0,1:T(8,128)(4,1)S(1)}, bf16[4,512,16,64]{1,3,2,0:T(8,128)(2,1)}, s32[]{:T(128)}, ...), branch_computations={%region_34.34_spmd, %region_35.35_spmd} | conditional | flops 2739404800 | bytes 89753112 | solution.py:77
  520.6 11.3 fusion.54
  563.0 37.5 %conditional.15 = (f32[512,16,64]{0,2,1:T(8,128)S(1)}, bf16[1,512,16,64]{1,3,2,0:T(8,128)(2,1)}, bf16[1,512,16,64]{1,3,2,0:T(8,128)(2,1)}) conditional(s32[]{:T(128)} %convert_element_type.266, f32[512,16,64]{0,2,1:T(8,128)S(1)} %get-tuple-element.1188, (pred[512,512]{0,1:T(8,128)(4,1)S(1)}, bf16[4,512,16,64]{1,3,2,0:T(8,128)(2,1)}, s32[]{:T(128)}, ...), branch_computations={%region_34.34_spmd, %region_35.35_spmd} | conditional | flops 2739404800 | bytes 89753112 | solution.py:77
  572.3 11.3 fusion.54
  628.2 11.1 convolution_convert_fusion
  640.0 10.8 convolution_convert_fusion.1
  652.0 37.8 %reduce-scatter.9.cloned.1.call-done = bf16[512,1024]{0,1:T(8,128)(2,1)} async-done(((bf16[2048,1024]{0,1:T(8,128)(2,1)}), bf16[512,1024]{0,1:T(8,128)(2,1)}) %reduce-scatter.9.cloned.1.call-update) | async-done | bytes 1048592 | tf_op jit(solution)/shard_map/reduce_scatter | solution.py:240
  689.8 80.3 %reduce-scatter.7.cloned.1.call-done = bf16[512,1024]{0,1:T(8,128)(2,1)} async-done(((bf16[2048,1024]{0,1:T(8,128)(2,1)}), bf16[512,1024]{0,1:T(8,128)(2,1)}) %reduce-scatter.7.cloned.1.call-update) | async-done | bytes 1048592 | tf_op jit(solution)/shard_map/reduce_scatter | solution.py:237
  778.8 25.8 %reduce-scatter.13.cloned.1.call-done = bf16[256,1024]{1,0:T(8,128)(2,1)} async-done(((bf16[1024,1024]{1,0:T(8,128)(2,1)}), bf16[256,1024]{1,0:T(8,128)(2,1)}) %reduce-scatter.13.cloned.1.call-update) | async-done | bytes 524304 | tf_op jit(solution)/shard_map/reduce_scatter | solution.py:262
  804.6 74.4 %reduce-scatter.17.cloned.1.call-done = bf16[1024,1024]{1,0:T(8,128)(2,1)} async-done(((bf16[4096,1024]{1,0:T(8,128)(2,1)}), bf16[1024,1024]{1,0:T(8,128)(2,1)}) %reduce-scatter.17.cloned.1.call-update) | async-done | bytes 2097168 | tf_op jit(solution)/shard_map/reduce_scatter | solution.py:268
  878.9 74.4 %reduce-scatter.15.cloned.1.call-done = bf16[256,4096]{1,0:T(8,128)(2,1)} async-done(((bf16[1024,4096]{1,0:T(8,128)(2,1)}), bf16[256,4096]{1,0:T(8,128)(2,1)}) %reduce-scatter.15.cloned.1.call-update) | async-done | bytes 2097168 | tf_op jit(solution)/shard_map/reduce_scatter | solution.py:265
  953.3 60.9 %reduce-scatter.11.cloned.1.call-done = bf16[256,3072]{1,0:T(8,128)(2,1)} async-done(((bf16[1024,3072]{1,0:T(8,128)(2,1)}), bf16[256,3072]{1,0:T(8,128)(2,1)}) %reduce-scatter.11.cloned.1.call-update) | async-done | bytes 1572880 | tf_op jit(solution)/shard_map/reduce_scatter | solution.py:259
  1025.5 43.2 %all-reduce.1 = (f32[4,1024]{1,0:T(4,128)}, f32[4,1024]{1,0:T(4,128)}) all-reduce(f32[4,1024]{1,0:T(4,128)S(1)} %get-tuple-element.797, f32[4,1024]{1,0:T(4,128)S(1)} %get-tuple-element.798), channel_id=1, replica_groups=mesh['grp'=2,'ctx'=4,'wsh'=4] {'grp','ctx','wsh'}, use_global_device_ids=true, to_apply=%region_53.54 | all-reduce | flops 8192 | bytes 65536 | tf_op jit(solution)/shard_map/psum | solution.py:280
  1072.3 162.1 %all-reduce.5.cloned.1.call-done = (bf16[256,3072]{1,0:T(8,128)(2,1)}, bf16[256,1024]{1,0:T(8,128)(2,1)}, bf16[256,4096]{1,0:T(8,128)(2,1)}, bf16[1024,1024]{1,0:T(8,128)(2,1)}) async-done(((bf16[256,3072]{1,0:T(8,128)(2,1)}, bf16[256,1024]{1,0:T(8,128)(2,1)}, bf16[256,4096]{1,0:T(8,128)(2,1)}, bf16[1024,1024]{1,0:T(8,128)(2,1)}), (bf16[256,3072]{1,0:T(8,128)(2,1)}, bf16[256,1024]{1,0:T(8,128)(2,1)}, ...) | async-done | bytes 6291472 | tf_op jit(solution)/shard_map/psum | solution.py:273
  (344 shorter events, 433.7 us)
Async XLA Ops:
  7.2 3.1 copy-start.35
  7.2 51.5 %all-gather.7.cloned.1.call-start = ((), (), s32[]{:S(2)}) async-start(), calls=%async_computation.6 | async-start | bytes 7864320 | tf_op jit(solution)/shard_map/all_gather | solution.py:158
  7.9 141.7 %all-gather.9.cloned.1.call-start = ((), (), s32[]{:S(2)}) async-start(), calls=%async_computation.7 | async-start | bytes 5242880 | tf_op jit(solution)/shard_map/all_gather | solution.py:180
  8.6 58.4 %copy-start.22 = (f32[512]{0:T(512)}, f32[512]{0:T(512)S(1)}, u32[]{:S(2)}) copy-start(f32[512]{0:T(512)S(1)} %broadcast_multiply_fusion.3) | copy-start | bytes 6148
  9.6 57.4 %copy-start.28 = (f32[512]{0:T(512)}, f32[512]{0:T(512)S(1)}, u32[]{:S(2)}) copy-start(f32[512]{0:T(512)S(1)} %fusion.104) | copy-start | bytes 6148
  10.3 56.8 %copy-start.19 = (f32[1,1024]{1,0:T(1,128)}, f32[1,1024]{1,0:T(1,128)S(1)}, u32[]{:S(2)}) copy-start(f32[1,1024]{1,0:T(1,128)S(1)} %get-tuple-element.781) | copy-start | bytes 12292
  10.9 56.2 %copy-start.42 = (f32[1,1024]{1,0:T(1,128)}, f32[1,1024]{1,0:T(1,128)S(1)}, u32[]{:S(2)}) copy-start(f32[1,1024]{1,0:T(1,128)S(1)} %get-tuple-element.785) | copy-start | bytes 12292
  68.6 162.5 %all-gather.11.cloned.1.call-start = ((), (), s32[]{:S(2)}) async-start(), calls=%async_computation.8 | async-start | bytes 5242880 | tf_op jit(solution)/shard_map/all_gather | solution.py:181
  69.3 272.8 %all-gather.13.cloned.1.call-start = ((), (), s32[]{:S(2)}) async-start(), calls=%async_computation.9 | async-start | bytes 2621440 | tf_op jit(solution)/shard_map/all_gather | solution.py:159
  69.9 279.1 %all-gather.15.cloned.1.call-start = ((), (), s32[]{:S(2)}) async-start(), calls=%async_computation.10 | async-start | bytes 10485760 | tf_op jit(solution)/shard_map/all_gather | solution.py:160
  70.5 302.7 %all-gather.17.cloned.1.call-start = ((), (), s32[]{:S(2)}) async-start(), calls=%async_computation.11 | async-start | bytes 10485760 | tf_op jit(solution)/shard_map/all_gather | solution.py:161
  71.1 618.7 %reduce-scatter.9.cloned.1.call-start = ((), (), s32[]{:S(2)}) async-start(), calls=%async_computation.13 | async-start | bytes 5242880 | tf_op jit(solution)/shard_map/reduce_scatter | solution.py:240
  347.3 65.0 %copy-start.26 = (f32[512]{0:T(512)}, f32[512]{0:T(512)S(1)}, u32[]{:S(2)}) copy-start(f32[512]{0:T(512)S(1)} %broadcast_multiply_fusion.1) | copy-start | bytes 6148
  349.0 63.3 %copy-start.38 = (f32[512]{0:T(512)}, f32[512]{0:T(512)S(1)}, u32[]{:S(2)}) copy-start(f32[512]{0:T(512)S(1)} %fusion.106) | copy-start | bytes 6148
  386.4 17.6 %slice-start = ((s8[8388608]{0:T(1024)(128)(4,1)}), s8[4194304]{0:T(1024)(128)(4,1)S(1)}, s32[]{:S(2)}) async-start(s8[8388608]{0:T(1024)(128)(4,1)} %bitcast.301), calls=%async_computation.19 | async-start | bytes 8388608
  388.3 15.7 %copy-start.16 = (f32[512,1024]{1,0:T(8,128)}, f32[512,1024]{1,0:T(8,128)S(1)}, u32[]{:S(2)}) copy-start(f32[512,1024]{1,0:T(8,128)S(1)} %get-tuple-element.761) | copy-start | bytes 6291460
  388.3 15.7 %copy-start.46 = (f32[512]{0:T(512)}, f32[512]{0:T(512)S(1)}, u32[]{:S(2)}) copy-start(f32[512]{0:T(512)S(1)} %negate_multiply_fusion.3) | copy-start | bytes 6148
  388.3 15.7 %slice-start.1 = ((s8[8388608]{0:T(1024)(128)(4,1)}), s8[4194304]{0:T(1024)(128)(4,1)S(1)}, s32[]{:S(2)}) async-start(s8[8388608]{0:T(1024)(128)(4,1)} %bitcast.301), calls=%async_computation.20 | async-start | bytes 8388608
  414.7 2.6 copy-start.12
  612.9 157.2 %reduce-scatter.7.cloned.1.call-start = ((), (), s32[]{:S(2)}) async-start(), calls=%async_computation.12 | async-start | bytes 5242880 | tf_op jit(solution)/shard_map/reduce_scatter | solution.py:237
  622.1 182.5 %reduce-scatter.13.cloned.1.call-start = ((), (), s32[]{:S(2)}) async-start(), calls=%async_computation.15 | async-start | bytes 2621440 | tf_op jit(solution)/shard_map/reduce_scatter | solution.py:262
  627.5 251.4 %reduce-scatter.17.cloned.1.call-start = ((), (), s32[]{:S(2)}) async-start(), calls=%async_computation.17 | async-start | bytes 10485760 | tf_op jit(solution)/shard_map/reduce_scatter | solution.py:268
  639.4 314.0 %reduce-scatter.15.cloned.1.call-start = ((), (), s32[]{:S(2)}) async-start(), calls=%async_computation.16 | async-start | bytes 10485760 | tf_op jit(solution)/shard_map/reduce_scatter | solution.py:265
  650.8 119.3 %copy-start.5 = (bf16[1,1,512,1024]{3,2,1,0:T(8,128)(2,1)S(1)}, bf16[1,1,512,1024]{3,2,1,0:T(8,128)(2,1)}, u32[]{:S(2)}) copy-start(bf16[1,1,512,1024]{3,2,1,0:T(8,128)(2,1)} %param.25) | copy-start | bytes 3145732
  650.8 119.2 %copy-start.20 = (f32[1,1024]{1,0:T(1,128)S(1)}, f32[1,1024]{1,0:T(1,128)}, u32[]{:S(2)}) copy-start(f32[1,1024]{1,0:T(1,128)} %copy-done.19) | copy-start | bytes 12292
  650.8 119.2 %copy-start.23 = (f32[512]{0:T(512)S(1)}, f32[512]{0:T(512)}, u32[]{:S(2)}) copy-start(f32[512]{0:T(512)} %copy-done.22) | copy-start | bytes 6148
  650.9 119.2 %copy-start.29 = (f32[512]{0:T(512)S(1)}, f32[512]{0:T(512)}, u32[]{:S(2)}) copy-start(f32[512]{0:T(512)} %copy-done.28) | copy-start | bytes 6148
  650.9 119.2 %copy-start.43 = (f32[1,1024]{1,0:T(1,128)S(1)}, f32[1,1024]{1,0:T(1,128)}, u32[]{:S(2)}) copy-start(f32[1,1024]{1,0:T(1,128)} %copy-done.42) | copy-start | bytes 12292
  650.9 363.4 %reduce-scatter.11.cloned.1.call-start = ((), (), s32[]{:S(2)}) async-start(), calls=%async_computation.14 | async-start | bytes 7864320 | tf_op jit(solution)/shard_map/reduce_scatter | solution.py:259
  778.4 455.9 %all-reduce.5.cloned.1.call-start = ((), (), s32[]{:S(2)}) async-start(), calls=%async_computation.18 | async-start | bytes 12582912 | tf_op jit(solution)/shard_map/psum | solution.py:273
  1015.8 7.3 copy-start.25
  1023.1 45.6 %copy-start.7 = (f32[512,1024]{1,0:T(8,128)S(1)}, f32[512,1024]{1,0:T(8,128)}, u32[]{:S(2)}) copy-start(f32[512,1024]{1,0:T(8,128)} %copy-done.6) | copy-start | bytes 6291460
  (34 other events, 53.3 us)
Sparse Core Ops, SparseCore 0:
  9.6 49.0 all-gather.6
  68.7 80.8 all-gather.8
  151.8 79.3 all-gather.10
  232.5 21.1 all-gather.12
  255.1 58.2 all-gather.14
  314.8 58.3 all-gather.16
  613.0 76.7 reduce-scatter.8
  692.8 77.2 reduce-scatter.6
  772.6 31.9 reduce-scatter.12
  807.2 71.7 reduce-scatter.16
  881.5 71.7 reduce-scatter.14
  955.9 58.3 reduce-scatter.10
  1018.7 215.5 all-reduce.4
where the time goes:
time: 1260 us; the launch traced here: 1250 us
  waiting for transfers between devices  688 us (55%)
  matrix products  288 us (23%)
  local copies, waits for them, and re-layouts  112 us (9%)
  other arithmetic  77.6 us (6%)
  blocking collectives  56.8 us (5%)
  between operations  14.8 us (1%)
    psum x1, waiting for transfers between devices, per_device(): lax.psum(shard_qkv.astype(jnp.bfloat16), ('grp', 'ctx')).astype(jnp.float32)  162 us
    reduce_scatter x1, waiting for transfers between devices, per_device(): lax.psum_scatter(key_terms.astype(jnp.bfloat16), 'ctx', scatter_dimension...  80.3 us
    reduce_scatter x1, waiting for transfers between devices, per_device(): lax.psum_scatter(term_down.astype(jnp.bfloat16), 'wsh', scatter_dimension...  74.4 us
    reduce_scatter x1, waiting for transfers between devices, per_device(): lax.psum_scatter(term_up.astype(jnp.bfloat16), 'wsh', scatter_dimension=0...  74.4 us
    reduce_scatter x1, waiting for transfers between devices, per_device(): lax.psum_scatter(term_qkv.astype(jnp.bfloat16), 'wsh', scatter_dimension=...  60.9 us
    dot_general x9, matrix products, scores(): jnp.einsum('qhd,khd->hqk', queries, key_block, preferred_element_type=jnp...  60.7 us
    all_gather x1, waiting for transfers between devices, per_device(): lax.all_gather(key_local, 'ctx', axis=0, tiled=True)  57.6 us
    all_gather x1, waiting for transfers between devices, per_device(): lax.all_gather(value_local, 'ctx', axis=0, tiled=True)  52 us
  transfers between devices with their start and end apart: 13, of which 11 were waited for; matrix products, arithmetic and copies ran while one was open for 17% of the time, Pallas kernels for 0%

commit v1 on v0

v1 whole, which is shorter than its diff:
```python
import functools
import math

import jax
import jax.numpy as jnp
from jax import lax
from jax.experimental import pallas as pl
from jax.experimental.pallas import tpu as pltpu
from jax.sharding import PartitionSpec as P

D = 1024
HEADS = 16
DH = 64
BLK = 512
PAIRS = HEADS // 2
QT = 256

EPS = 1e-05
ALPHA = 32.0
NEG = -1e30
LOG2E = 1.4426950408889634
C2 = ALPHA * LOG2E
QSCALE = 1.0 / (ALPHA * math.sqrt(DH))


def layer_norm(values, gain_row, bias_row):
    centre = values - jnp.mean(values, axis=-1, keepdims=True)
    spread = jnp.mean(centre * centre, axis=-1, keepdims=True)
    return centre * lax.rsqrt(spread + EPS) * gain_row + bias_row


def gelu_tanh(values):
    return jax.nn.gelu(values, approximate=True)


def dot_dims(left_side, right_side, left_dim, right_dim):
    return lax.dot_general(
        left_side,
        right_side,
        (((left_dim,), (right_dim,)), ((), ())),
        preferred_element_type=jnp.float32,
    )


def contract_last(left_side, right_side):
    return dot_dims(left_side, right_side, 1, 1)


def contract_rows(left_side, right_side):
    return dot_dims(left_side, right_side, 0, 0)


def head_lanes(head, rows):
    lane = lax.broadcasted_iota(jnp.int32, (rows, 128), 1)
    return (lane >= DH) if head else (lane < DH)


def causal_tile():
    row = lax.broadcasted_iota(jnp.int32, (QT, QT), 0)
    col = lax.broadcasted_iota(jnp.int32, (QT, QT), 1)
    return col <= row


def attn_fwd_kernel(slots, slot_ref, q_ref, k_ref, v_ref, o_ref, lse_ref):
    own_slot = slot_ref[0]
    causal = causal_tile()
    for tile in range(BLK // QT):
        rows = pl.ds(tile * QT, QT)
        own_keys = (tile + 1) * QT
        q_pair = q_ref[rows, :]
        outs, lses = [], []
        for head in range(2):
            q_head = jnp.where(head_lanes(head, QT), q_pair, jnp.zeros_like(q_pair))
            diag = contract_last(q_head, k_ref[pl.ds(tile * QT, QT), :])
            diag = jnp.where(causal, diag, NEG)
            parts = [(diag, tile * QT, QT, None)]
            top = jnp.max(diag, axis=-1, keepdims=True)
            if tile:
                low_part = contract_last(q_head, k_ref[pl.ds(0, tile * QT), :])
                parts.append((low_part, 0, tile * QT, None))
                top = jnp.maximum(top, jnp.max(low_part, axis=-1, keepdims=True))
            for slot in range(slots):
                visible = slot < own_slot
                part = contract_last(q_head, k_ref[pl.ds((slot + 1) * BLK, BLK), :])
                parts.append((part, (slot + 1) * BLK, BLK, visible))
                slot_top = jnp.max(part, axis=-1, keepdims=True)
                top = jnp.maximum(top, jnp.where(visible, slot_top, NEG))
            shift = top * C2
            total = jnp.zeros((QT, 1), jnp.float32)
            acc = jnp.zeros((QT, 128), jnp.float32)
            for part, start, size, visible in parts:
                row_shift = shift if visible is None else shift + jnp.where(visible, 0.0, 1e30)
                expo = jnp.exp2(part * C2 - row_shift)
                total = total + jnp.sum(expo, axis=-1, keepdims=True)
                acc = acc + dot_dims(expo.astype(jnp.bfloat16), v_ref[pl.ds(start, size), :], 1, 0)
            outs.append(acc / total)
            lses.append(jnp.broadcast_to(shift + jnp.log2(total), (QT, 128)))
        first = head_lanes(0, QT)
        o_ref[rows, :] = jnp.where(first, outs[0], outs[1]).astype(jnp.bfloat16)
        lse_ref[0, rows, :] = jnp.where(first, lses[0], lses[1])


def attention_forward(own_slot, queries, keys_values, slots):
    keys = (slots + 1) * BLK
    return pl.pallas_call(
        functools.partial(attn_fwd_kernel, slots),
        out_shape=(
            jax.ShapeDtypeStruct((BLK, D), jnp.bfloat16),
            jax.ShapeDtypeStruct((PAIRS, BLK, 128), jnp.float32),
        ),
        grid_spec=pltpu.PrefetchScalarGridSpec(
            num_scalar_prefetch=1,
            grid=(PAIRS,),
            in_specs=[
                pl.BlockSpec((BLK, 128), lambda i, s: (0, i)),
                pl.BlockSpec((keys, 128), lambda i, s: (0, i)),
                pl.BlockSpec((keys, 128), lambda i, s: (0, i + PAIRS)),
            ],
            out_specs=(
                pl.BlockSpec((BLK, 128), lambda i, s: (0, i)),
                pl.BlockSpec((1, BLK, 128), lambda i, s: (i, 0, 0)),
            ),
        ),
        compiler_params=pltpu.CompilerParams(vmem_limit_bytes=48 << 20),
        cost_estimate=pl.CostEstimate(
            flops=4 * BLK * keys * D, bytes_accessed=16 << 20, transcendentals=BLK * keys * HEADS
        ),
        name="attn_fwd",
    )(own_slot, queries, keys_values, keys_values)


def attn_bwd_kernel(
    slots, slot_ref, q_ref, k_ref, v_ref, o_ref, do_ref, lse_ref, dq_ref, dk_ref, dv_ref, dk_acc, dv_acc
):
    own_slot = slot_ref[0]
    causal = causal_tile()
    dk_acc[...] = jnp.zeros_like(dk_acc)
    dv_acc[...] = jnp.zeros_like(dv_acc)
    for tile in range(BLK // QT):
        rows = pl.ds(tile * QT, QT)
        q_pair = q_ref[rows, :]
        do_pair = do_ref[rows, :]
        q_turned = q_pair.T
        do_turned = do_pair.T
        prod = do_pair.astype(jnp.float32) * o_ref[rows, :].astype(jnp.float32)
        lse_pair = lse_ref[0, rows, :]
        dqs = []
        for head in range(2):
            lanes = head_lanes(head, QT)
            turned = slice(head * DH, (head + 1) * DH)
            q_head = jnp.where(lanes, q_pair, jnp.zeros_like(q_pair))
            do_head = jnp.where(lanes, do_pair, jnp.zeros_like(do_pair))
            delta = jnp.sum(jnp.where(lanes, prod, 0.0), axis=-1, keepdims=True)
            lse = lse_pair[:, head * DH : head * DH + 1]
            spans = [(tile * QT, QT, None, True)]
            if tile:
                spans.append((0, tile * QT, None, False))
            spans += [((s + 1) * BLK, BLK, s < own_slot, False) for s in range(slots)]
            dq = jnp.zeros((QT, 128), jnp.float32)
            for start, size, visible, diagonal in spans:
                keys = pl.ds(start, size)
                k_part = k_ref[keys, :]
                row_shift = lse if visible is None else lse + jnp.where(visible, 0.0, 1e30)
                prob = jnp.exp2(contract_last(q_head, k_part) * C2 - row_shift)
                if diagonal:
                    prob = jnp.where(causal, prob, 0.0)
                dprob = contract_last(do_head, v_ref[keys, :])
                dlogit = (prob * (dprob - delta)).astype(jnp.bfloat16)
                dq = dq + dot_dims(dlogit, k_part, 1, 0)
                dk_acc[turned, keys] += dot_dims(q_turned[turned, :], dlogit, 1, 0)
                dv_acc[turned, keys] += dot_dims(
                    do_turned[turned, :], prob.astype(jnp.bfloat16), 1, 0
                )
            dqs.append(dq)
        dq_ref[rows, :] = (
            jnp.where(head_lanes(0, QT), dqs[0], dqs[1]) * ALPHA
        ).astype(jnp.bfloat16) * jnp.bfloat16(QSCALE)
    dk_ref[...] = (dk_acc[...] * ALPHA).astype(jnp.bfloat16)
    dv_ref[...] = dv_acc[...].astype(jnp.bfloat16)


def attention_backward(own_slot, queries, keys_values, attended, grad_out, lse, slots):
    keys = (slots + 1) * BLK
    pair = pl.BlockSpec((BLK, 128), lambda i, s: (0, i))
    turned = pl.BlockSpec((128, keys), lambda i, s: (i, 0))
    return pl.pallas_call(
        functools.partial(attn_bwd_kernel, slots),
        out_shape=(
            jax.ShapeDtypeStruct((BLK, D), jnp.bfloat16),
            jax.ShapeDtypeStruct((D, keys), jnp.bfloat16),
            jax.ShapeDtypeStruct((D, keys), jnp.bfloat16),
        ),
        grid_spec=pltpu.PrefetchScalarGridSpec(
            num_scalar_prefetch=1,
            grid=(PAIRS,),
            in_specs=[
                pair,
                pl.BlockSpec((keys, 128), lambda i, s: (0, i)),
                pl.BlockSpec((keys, 128), lambda i, s: (0, i + PAIRS)),
                pair,
                pair,
                pl.BlockSpec((1, BLK, 128), lambda i, s: (i, 0, 0)),
            ],
            out_specs=(pair, turned, turned),
            scratch_shapes=[pltpu.VMEM((128, keys), jnp.float32)] * 2,
        ),
        compiler_params=pltpu.CompilerParams(vmem_limit_bytes=48 << 20),
        cost_estimate=pl.CostEstimate(
            flops=10 * BLK * keys * D, bytes_accessed=24 << 20, transcendentals=BLK * keys * HEADS
        ),
        name="attn_bwd",
    )(own_slot, queries, keys_values, keys_values, attended, grad_out, lse)


def per_device(n_ctx, inputs, w_qkv, w_out, w_up, w_down, norm_gains, norm_biases, block_map, out_grad):
    slots = n_ctx // 2
    raw = inputs.reshape(BLK, D)
    tokens = raw.astype(jnp.float32)
    block_entry = block_map.reshape(2)
    own_slot = block_entry[1] // BLK
    own_tag = jnp.where(block_entry[0] == 0, own_slot, n_ctx)
    tag_rows = jnp.full((16, D), own_tag.astype(jnp.bfloat16))
    full_qkv = lax.all_gather(w_qkv, "wsh", axis=0, tiled=True)
    shared = lax.all_gather(jnp.concatenate([raw, tag_rows], axis=0), "ctx", axis=0)
    full_out, full_up, full_down = (
        lax.all_gather(w_out, "wsh", axis=0, tiled=True),
        lax.all_gather(w_up, "wsh", axis=0, tiled=True),
        lax.all_gather(w_down, "wsh", axis=0, tiled=True),
    )
    tags = shared[:, BLK, 0].astype(jnp.int32)
    prompt = [
        lax.dynamic_index_in_dim(shared, jnp.argmax(tags == slot), 0, keepdims=False)[:BLK]
        for slot in range(slots)
    ]
    slot_vec = own_slot.reshape(1)

    first_norm, first_back = jax.vjp(layer_norm, tokens, norm_gains[0], norm_biases[0])
    normed_low = first_norm.astype(jnp.bfloat16)
    prompt_low = layer_norm(
        jnp.concatenate(prompt, axis=0).astype(jnp.float32), norm_gains[0], norm_biases[0]
    ).astype(jnp.bfloat16)
    every_low = jnp.concatenate([normed_low, prompt_low], axis=0)
    queries = (
        jnp.dot(normed_low, full_qkv[:, :D], preferred_element_type=jnp.float32) * QSCALE
    ).astype(jnp.bfloat16)
    keys_values = jnp.dot(
        every_low, full_qkv[:, D:], preferred_element_type=jnp.float32
    ).astype(jnp.bfloat16)
    attn_low, lse = attention_forward(slot_vec, queries, keys_values, slots)

    branch = jnp.dot(attn_low, full_out, preferred_element_type=jnp.float32)
    post_attn, attn_back = jax.vjp(layer_norm, branch, norm_gains[1], norm_biases[1])
    hidden = tokens + post_attn
    pre_ffn, ffn_back = jax.vjp(layer_norm, hidden, norm_gains[2], norm_biases[2])
    ffn_low = pre_ffn.astype(jnp.bfloat16)
    upward = jnp.dot(ffn_low, full_up, preferred_element_type=jnp.float32)
    activated, gelu_back = jax.vjp(gelu_tanh, upward)
    active_low = activated.astype(jnp.bfloat16)
    downward = jnp.dot(active_low, full_down, preferred_element_type=jnp.float32)
    post_ffn, post_back = jax.vjp(layer_norm, downward, norm_gains[3], norm_biases[3])
    result = (hidden + post_ffn).astype(jnp.bfloat16).reshape(1, 1, BLK, D)
    seed_grad = out_grad.reshape(BLK, D).astype(jnp.float32)
    grad_down_in, gain_grad3, bias_grad3 = post_back(seed_grad)
    down_low = grad_down_in.astype(jnp.bfloat16)
    term_down = contract_rows(active_low, down_low).astype(jnp.bfloat16)
    grad_active = contract_last(down_low, full_down)
    up_low = gelu_back(grad_active)[0].astype(jnp.bfloat16)
    term_up = contract_rows(ffn_low, up_low).astype(jnp.bfloat16)
    grad_pre_ffn, gain_grad2, bias_grad2 = ffn_back(contract_last(up_low, full_up))
    grad_hidden = seed_grad + grad_pre_ffn
    grad_branch, gain_grad1, bias_grad1 = attn_back(grad_hidden)
    branch_low = grad_branch.astype(jnp.bfloat16)
    term_out = contract_rows(attn_low, branch_low).astype(jnp.bfloat16)
    grad_out_low = contract_last(branch_low, full_out).astype(jnp.bfloat16)

    grad_q, grad_k, grad_v = attention_backward(
        slot_vec, queries, keys_values, attn_low, grad_out_low, lse, slots
    )
    grad_kv = jnp.concatenate([grad_k, grad_v], axis=0)
    grad_normed_kv = dot_dims(grad_kv, full_qkv[:, D:], 0, 1)
    partial = grad_normed_kv[BLK:].astype(jnp.bfloat16)
    totals = lax.psum(partial, "ctx").reshape(slots, BLK, D)
    from_others = lax.dynamic_index_in_dim(
        totals, jnp.minimum(own_slot, slots - 1), 0, keepdims=False
    ).astype(jnp.float32)
    from_others = jnp.where(own_slot < slots, from_others, 0.0)
    grad_normed = contract_last(grad_q, full_qkv[:, :D]) + grad_normed_kv[:BLK] + from_others
    term_qkv = jnp.concatenate(
        [
            contract_rows(normed_low, grad_q).astype(jnp.bfloat16),
            dot_dims(every_low, grad_kv, 0, 1).astype(jnp.bfloat16),
        ],
        axis=1,
    )
    grad_tokens, gain_grad0, bias_grad0 = first_back(grad_normed)
    grad_input = (grad_hidden + grad_tokens).reshape(1, 1, BLK, D)

    def reduced(term):
        shard = lax.psum_scatter(term, "wsh", scatter_dimension=0, tiled=True)
        return lax.psum(shard, ("grp", "ctx")).astype(jnp.float32)

    summed_down, summed_up, summed_out, summed_qkv = (
        reduced(term_down),
        reduced(term_up),
        reduced(term_out),
        reduced(term_qkv),
    )
    gain_stack = jnp.stack([gain_grad0, gain_grad1, gain_grad2, gain_grad3])
    bias_stack = jnp.stack([bias_grad0, bias_grad1, bias_grad2, bias_grad3])
    gain_total, bias_total = lax.psum((gain_stack, bias_stack), ("grp", "ctx", "wsh"))
    return (
        result,
        grad_input,
        summed_qkv,
        summed_out,
        summed_up,
        summed_down,
        gain_total,
        bias_total,
    )


def solution(mesh):
    rows = P("wsh", None)
    blocks = P("grp", "wsh", "ctx", None)
    return jax.shard_map(
        functools.partial(per_device, mesh.shape["ctx"]),
        mesh=mesh,
        in_specs=(blocks, rows, rows, rows, rows, P(), P(), blocks, blocks),
        out_specs=(blocks, blocks, rows, rows, rows, rows, P(), P()),
        check_vma=False,
    )
```

time: 1260 us -> 948 us (0.75)
  matrix products: 288 us -> 113 us
  local copies, waits for them, and re-layouts: 112 us -> 36.3 us
  Pallas kernels: 0 us -> 66.3 us
  waiting for transfers between devices: 688 us -> 627 us
  other arithmetic: 77.6 us -> 31.8 us
  blocking collectives: 56.8 us -> 43.6 us
    reduce_scatter x6 -> x4, waiting for transfers between devices: 354 us -> 169 us  [reduced(): shard = lax.psum_scatter(term, 'wsh', scatter_dimension=0, tiled=True)]
    dot_general x36 -> x12, matrix products: 262 us -> 86.3 us  [the longest x10 74.5 us: dot_dims(): lax.dot_general(left_side, right_side, (((left_dim,), (right_dim,)), ((),...]
    psum x1 -> x2, waiting for transfers between devices: 162 us -> 253 us  [the longest x1 165 us: reduced(): return lax.psum(shard, ('grp', 'ctx')).astype(jnp.float32)]
    pallas_call x0 -> x2, Pallas kernels: none -> 66.3 us  [the longest x1 42.1 us: attention_backward(): pl.pallas_call(functools.partial(attn_bwd_kernel, slots), out_shape=(jax....]
    all_gather x3 -> x2, waiting for transfers between devices: 157 us -> 116 us  [the longest x1 81.3 us: per_device(): lax.all_gather(jnp.concatenate([raw, tag_rows], axis=0), 'ctx', axis=0)]
    all_gather x1, waiting for transfers between devices: 0.02 us -> 39.6 us  [per_device(): lax.all_gather(w_up, 'wsh', axis=0, tiled=True)]
    all_gather x1, waiting for transfers between devices: 12.2 us -> 46.6 us  [per_device(): lax.all_gather(w_down, 'wsh', axis=0, tiled=True)]
    another operation x7 -> x0, local copies, waits for them, and re-layouts: 22.2 us -> none  [the longest x2 19.7 us: sweep_blocks(): member.reshape((block_count, limit_rows) + member.shape[1:])]
  transfers between devices with their start and end apart: 13 -> 11, of which waited for: 11 -> 9; matrix products, arithmetic and copies ran while one was open for 17% -> 11% of each run, Pallas kernels for 0% -> 7%
where the time goes in v1:
time: 948 us; the launch traced here: 940 us
  waiting for transfers between devices  627 us (66%)
  matrix products  113 us (12%)
  Pallas kernels  66.3 us (7%)
  blocking collectives  43.6 us (5%)
  local copies, waits for them, and re-layouts  36.3 us (4%)
  other arithmetic  31.8 us (3%)
  between operations  21.9 us (2%)
    reduce_scatter x4, waiting for transfers between devices, reduced(): shard = lax.psum_scatter(term, 'wsh', scatter_dimension=0, tiled=True)  169 us
    psum x1, waiting for transfers between devices, reduced(): return lax.psum(shard, ('grp', 'ctx')).astype(jnp.float32)  165 us
    psum x1, waiting for transfers between devices, per_device(): totals = lax.psum(partial, 'ctx').reshape(slots, BLK, D)  87.9 us
    all_gather x1, waiting for transfers between devices, per_device(): lax.all_gather(jnp.concatenate([raw, tag_rows], axis=0), 'ctx', axis=0)  81.3 us
    dot_general x10, matrix products, dot_dims(): lax.dot_general(left_side, right_side, (((left_dim,), (right_dim,)), ((),...  74.5 us
    all_gather x1, waiting for transfers between devices, per_device(): lax.all_gather(w_down, 'wsh', axis=0, tiled=True)  46.6 us
    psum x1, blocking collectives, per_device(): lax.psum((gain_stack, bias_stack), ('grp', 'ctx', 'wsh'))  43.6 us
    pallas_call x1, Pallas kernels, attention_backward(): pl.pallas_call(functools.partial(attn_bwd_kernel, slots), out_shape=(jax....  42.1 us
  transfers between devices with their start and end apart: 11, of which 9 were waited for; matrix products, arithmetic and copies ran while one was open for 11% of the time, Pallas kernels for 7%

profile of v1, /device:TPU:0, one launch (start us, length us, event | category | flops | bytes accessed | tf_op | source)
XLA Modules:
  0.0 940.1 jit_solution(8773519172055803372)
XLA Ops:
  18.6 81.3 %all-gather.15.cloned.1.call-done = bf16[2112,1024]{1,0:T(8,128)(2,1)} async-done(((bf16[528,1024]{1,0:T(8,128)(2,1)}), bf16[2112,1024]{1,0:T(8,128)(2,1)}) %all-gather.15.cloned.1.call-update) | async-done | bytes 4325392 | tf_op jit(solution)/shard_map/all_gather | solution.py:224
  109.0 2.8 fusion.12
  111.7 34.6 %all-gather.7.cloned.1.call-done = bf16[1024,3072]{1,0:T(8,128)(2,1)} async-done(((bf16[256,3072]{1,0:T(8,128)(2,1)}), bf16[1024,3072]{1,0:T(8,128)(2,1)}) %all-gather.7.cloned.1.call-update) | async-done | bytes 6291472 | tf_op jit(solution)/shard_map/all_gather | solution.py:223
  146.4 3.0 multiply_convert_fusion.1.q_ref
  150.4 8.7 convolution_convert_fusion.2.k_ref.v_ref
  159.2 24.2 %attn_fwd.1 = (bf16[512,1024]{1,0:T(8,128)(2,1)S(1)}, f32[8,512,128]{2,1,0:T(8,128)S(1)}) custom-call(s32[1]{0:T(128)} %bitcast.2.slot_ref, bf16[512,1024]{1,0:T(8,128)(2,1)S(1)} %multiply_convert_fusion.1.q_ref, bf16[1536,2048]{1,0:T(8,128)(2,1)} %convolution_convert_fusion.2.k_ref.v_ref, bf16[1536,2048]{1,0:T(8,128)(2,1)} %convolution_convert_fusion.2.k_ref.v_ref), custom_call_target="tpu_custom_call" | custom-call | flops 3221225472 | bytes 16777216 | tf_op jit(solution)/shard_map/attn_fwd/pallas_call | solution.py:105
  184.7 2.9 fusion.63
  190.7 39.6 %all-gather.11.cloned.1.call-done = bf16[1024,4096]{1,0:T(8,128)(2,1)} async-done(((bf16[256,4096]{1,0:T(8,128)(2,1)}), bf16[1024,4096]{1,0:T(8,128)(2,1)}) %all-gather.11.cloned.1.call-update) | async-done | bytes 8388624 | tf_op jit(solution)/shard_map/all_gather | solution.py:227
  230.3 13.1 %fusion.52 = f32[512,4096]{1,0:T(8,128)} fusion(bf16[1024,4096]{1,0:T(8,128)(2,1)} %all-gather.11.cloned.1.call-done, f32[512,1024]{1,0:T(8,128)} %copy-done.5, f32[1024]{0:T(1024)S(1)} %bitcast.114, f32[1024]{0:T(1024)S(1)} %bitcast.106, f32[512]{0:T(512)S(1)} %fusion.46, f32[512]{0:T(512)S(1)} %broadcast_multiply_fusion.2), kind=kOutput, calls=%fused_computation.113 | convolution fusion | flops 4297588736 | bytes 18886656 | tf_op jit(solution)/shard_map/dot_general | solution.py:256
  243.4 46.6 %all-gather.13.cloned.1.call-done = bf16[4096,1024]{1,0:T(8,128)(2,1)} async-done(((bf16[1024,1024]{1,0:T(8,128)(2,1)}), bf16[4096,1024]{1,0:T(8,128)(2,1)}) %all-gather.13.cloned.1.call-update) | async-done | bytes 8388624 | tf_op jit(solution)/shard_map/all_gather | solution.py:228
  290.0 10.3 %fusion.64 = (f32[512]{0:T(512)S(1)}, f32[512,1024]{1,0:T(8,128)S(1)}) fusion(bf16[4096,1024]{1,0:T(8,128)(2,1)} %all-gather.13.cloned.1.call-done, f32[512,4096]{1,0:T(8,128)} %fusion.52), kind=kOutput, calls=%fused_computation.124 | convolution fusion | flops 4314365440 | bytes 18876416 | tf_op jit(solution)/shard_map/dot_general | solution.py:259
  307.0 15.5 %fusion.6 = bf16[512,4096]{1,0:T(8,128)(2,1)} fusion(f32[512,4096]{1,0:T(8,128)} %fusion.52, bf16[4096,1024]{1,0:T(8,128)(2,1)S(1)} %copy-done.36, f32[512,1024]{1,0:T(8,128)S(1)} %get-tuple-element.46, f32[512]{0:T(512)S(1)} %negate_multiply_fusion.3), kind=kOutput, calls=%fused_computation.8 | convolution fusion | flops 4337958912 | bytes 23070720 | tf_op jit(solution)/shard_map/dot_general | solution.py:37
  322.5 8.7 multiply_reduce_fusion
  336.6 2.7 convolution_convert_fusion.4
  339.3 3.5 convolution_convert_fusion.6.do_ref
  342.8 42.1 %attn_bwd.1 = (bf16[512,1024]{1,0:T(8,128)(2,1)S(1)}, bf16[1024,1536]{1,0:T(8,128)(2,1)}, bf16[1024,1536]{1,0:T(8,128)(2,1)}) custom-call(s32[1]{0:T(128)} %bitcast.2.slot_ref, bf16[512,1024]{1,0:T(8,128)(2,1)S(1)} %multiply_convert_fusion.1.q_ref, bf16[1536,2048]{1,0:T(8,128)(2,1)} %convolution_convert_fusion.2.k_ref.v_ref, ...), custom_call_target="tpu_custom_call" | custom-call | flops 8053063680 | bytes 25165824 | tf_op jit(solution)/shard_map/attn_bwd/pallas_call | solution.py:186
  387.6 2.9 copy.18
  393.5 3.0 copy-done.20
  397.0 7.0 convolution_convert_fusion.3
  404.0 3.3 pad_maximum_fusion
  408.9 9.7 %convolution_convert_fusion.1 = bf16[1024,4096]{1,0:T(8,128)(2,1)} fusion(bf16[512,4096]{1,0:T(8,128)(2,1)} %fusion.6, f32[512,1024]{1,0:T(8,128)S(1)} %copy-done.7, f32[1024]{0:T(1024)S(1)} %bitcast.115, f32[1024]{0:T(1024)S(1)} %bitcast.109, f32[512]{0:T(512)S(1)} %fusion.46, f32[512]{0:T(512)S(1)} %broadcast_multiply_fusion.2), kind=kOutput, calls=%fused_computation.11 | convolution fusion | flops 4301783040 | bytes 14692352 | tf_op jit(solution)/shard_map/dot_general | solution.py:37
  420.3 10.4 %convolution_convert_fusion = bf16[4096,1024]{1,0:T(8,128)(2,1)} fusion(f32[512,1024]{1,0:T(8,128)S(1)} %copy-done.19, f32[512]{0:T(512)S(1)} %negate_multiply_fusion.3, f32[512,4096]{1,0:T(8,128)} %fusion.52), kind=kOutput, calls=%fused_computation.10 | convolution fusion | flops 4319084544 | bytes 18876416 | tf_op jit(solution)/shard_map/dot_general | solution.py:37
  430.8 10.1 %fusion.13 = f32[1536,1024]{1,0:T(8,128)S(1)} fusion(bf16[2048,1536]{1,0:T(8,128)(2,1)} %copy-done.20, bf16[1024,3072]{1,0:T(8,128)(2,1)} %all-gather.7.cloned.1.call-done), kind=kOutput, calls=%fused_computation.24 | convolution fusion | flops 6442450944 | bytes 16777216 | tf_op jit(solution)/shard_map/dot_general | solution.py:37
  445.3 20.6 %reduce-scatter.5.cloned.1.call-done = bf16[256,3072]{1,0:T(8,128)(2,1)} async-done(((bf16[1024,3072]{1,0:T(8,128)(2,1)}), bf16[256,3072]{1,0:T(8,128)(2,1)}) %reduce-scatter.5.cloned.1.call-update) | async-done | bytes 1572880 | tf_op jit(solution)/shard_map/reduce_scatter | solution.py:299
  465.8 74.3 %reduce-scatter.9.cloned.1.call-done = bf16[256,4096]{1,0:T(8,128)(2,1)} async-done(((bf16[1024,4096]{1,0:T(8,128)(2,1)}), bf16[256,4096]{1,0:T(8,128)(2,1)}) %reduce-scatter.9.cloned.1.call-update) | async-done | bytes 2097168 | tf_op jit(solution)/shard_map/reduce_scatter | solution.py:299
  540.1 74.5 %reduce-scatter.11.cloned.1.call-done = bf16[1024,1024]{1,0:T(8,128)(2,1)} async-done(((bf16[4096,1024]{1,0:T(8,128)(2,1)}), bf16[1024,1024]{1,0:T(8,128)(2,1)}) %reduce-scatter.11.cloned.1.call-update) | async-done | bytes 2097168 | tf_op jit(solution)/shard_map/reduce_scatter | solution.py:299
  616.0 87.9 %all-reduce.6.cloned.1.call-done = bf16[2,512,1024]{2,1,0:T(8,128)(2,1)} async-done(((bf16[2,512,1024]{2,1,0:T(8,128)(2,1)}), bf16[2,512,1024]{2,1,0:T(8,128)(2,1)}) %all-reduce.6.cloned.1.call-update) | async-done | bytes 2097168 | tf_op jit(solution)/shard_map/psum | solution.py:282
  704.0 4.2 fusion.54
  710.6 43.6 %all-reduce.1 = (f32[4,1024]{1,0:T(4,128)}, f32[4,1024]{1,0:T(4,128)}) all-reduce(f32[4,1024]{1,0:T(4,128)S(1)} %get-tuple-element.68, f32[4,1024]{1,0:T(4,128)S(1)} %get-tuple-element.69), channel_id=1, replica_groups=mesh['grp'=2,'ctx'=4,'wsh'=4] {'grp','ctx','wsh'}, use_global_device_ids=true, to_apply=%region_33.34 | all-reduce | flops 8192 | bytes 65536 | tf_op jit(solution)/shard_map/psum | solution.py:310
  754.2 4.2 add_bitcast_fusion
  758.5 165.0 %all-reduce.8.cloned.1.call-done = (bf16[256,3072]{1,0:T(8,128)(2,1)}, bf16[256,1024]{1,0:T(8,128)(2,1)}, bf16[256,4096]{1,0:T(8,128)(2,1)}, bf16[1024,1024]{1,0:T(8,128)(2,1)}) async-done(((bf16[256,3072]{1,0:T(8,128)(2,1)}, bf16[256,1024]{1,0:T(8,128)(2,1)}, bf16[256,4096]{1,0:T(8,128)(2,1)}, bf16[1024,1024]{1,0:T(8,128)(2,1)}), (bf16[256,3072]{1,0:T(8,128)(2,1)}, bf16[256,1024]{1,0:T(8,128)(2,1)}, ...) | async-done | bytes 6291472 | tf_op jit(solution)/shard_map/psum | solution.py:300
  923.4 3.6 convert_element_type.104
  (150 shorter events, 54.1 us)
Async XLA Ops:
  7.2 92.7 %all-gather.15.cloned.1.call-start = ((), (), s32[]{:S(2)}) async-start(), calls=%async_computation.13 | async-start | bytes 5406720 | tf_op jit(solution)/shard_map/all_gather | solution.py:224
  14.1 132.3 %all-gather.7.cloned.1.call-start = ((), (), s32[]{:S(2)}) async-start(), calls=%async_computation.4 | async-start | bytes 7864320 | tf_op jit(solution)/shard_map/all_gather | solution.py:223
  14.8 169.8 %all-gather.9.cloned.1.call-start = ((), (), s32[]{:S(2)}) async-start(), calls=%async_computation.5 | async-start | bytes 2621440 | tf_op jit(solution)/shard_map/all_gather | solution.py:226
  15.6 214.7 %all-gather.11.cloned.1.call-start = ((), (), s32[]{:S(2)}) async-start(), calls=%async_computation.6 | async-start | bytes 10485760 | tf_op jit(solution)/shard_map/all_gather | solution.py:227
  16.2 273.8 %all-gather.13.cloned.1.call-start = ((), (), s32[]{:S(2)}) async-start(), calls=%async_computation.7 | async-start | bytes 10485760 | tf_op jit(solution)/shard_map/all_gather | solution.py:228
  16.8 428.5 %reduce-scatter.7.cloned.1.call-start = ((), (), s32[]{:S(2)}) async-start(), calls=%async_computation.10 | async-start | bytes 2621440 | tf_op jit(solution)/shard_map/reduce_scatter | solution.py:299
  17.1 90.8 %copy-start.28 = (f32[512]{0:T(512)}, f32[512]{0:T(512)S(1)}, u32[]{:S(2)}) copy-start(f32[512]{0:T(512)S(1)} %broadcast_multiply_fusion.4) | copy-start | bytes 6148
  18.0 89.8 %copy-start.30 = (f32[512]{0:T(512)}, f32[512]{0:T(512)S(1)}, u32[]{:S(2)}) copy-start(f32[512]{0:T(512)S(1)} %fusion.44) | copy-start | bytes 6148
  18.1 90.9 %copy-start.26 = (f32[1,1024]{1,0:T(1,128)}, f32[1,1024]{1,0:T(1,128)S(1)}, u32[]{:S(2)}) copy-start(f32[1,1024]{1,0:T(1,128)S(1)} %get-tuple-element.54) | copy-start | bytes 12292
  18.5 130.8 %copy-start.21 = (bf16[512,1024]{1,0:T(8,128)(2,1)}, bf16[512,1024]{1,0:T(8,128)(2,1)S(1)}, u32[]{:S(2)}) copy-start(bf16[512,1024]{1,0:T(8,128)(2,1)S(1)} %fusion.28) | copy-start | bytes 3145732
  146.4 3.0 copy-start.15
  146.4 4.1 copy-start.37
  302.5 4.5 copy-start.36
  304.5 18.0 %copy-start.18 = (f32[512,1024]{1,0:T(8,128)}, f32[512,1024]{1,0:T(8,128)S(1)}, u32[]{:S(2)}) copy-start(f32[512,1024]{1,0:T(8,128)S(1)} %get-tuple-element.46) | copy-start | bytes 6291460
  339.3 126.6 %reduce-scatter.5.cloned.1.call-start = ((), (), s32[]{:S(2)}) async-start(), calls=%async_computation.9 | async-start | bytes 7864320 | tf_op jit(solution)/shard_map/reduce_scatter | solution.py:299
  342.8 42.1 %copy-start.22 = (bf16[512,1024]{1,0:T(8,128)(2,1)S(1)}, bf16[512,1024]{1,0:T(8,128)(2,1)}, u32[]{:S(2)}) copy-start(bf16[512,1024]{1,0:T(8,128)(2,1)} %copy-done.21) | copy-start | bytes 3145732
  390.5 2.8 copy-start.12
  393.3 3.2 copy-start.16
  393.3 3.7 copy-start.23
  393.5 3.0 copy-start.20
  407.3 132.8 %reduce-scatter.9.cloned.1.call-start = ((), (), s32[]{:S(2)}) async-start(), calls=%async_computation.11 | async-start | bytes 10485760 | tf_op jit(solution)/shard_map/reduce_scatter | solution.py:299
  418.6 196.0 %reduce-scatter.11.cloned.1.call-start = ((), (), s32[]{:S(2)}) async-start(), calls=%async_computation.12 | async-start | bytes 10485760 | tf_op jit(solution)/shard_map/reduce_scatter | solution.py:299
  430.7 273.3 %all-reduce.6.cloned.1.call-start = ((), (), s32[]{:S(2)}) async-start(), calls=%async_computation.8 | async-start | bytes 4194304 | tf_op jit(solution)/shard_map/psum | solution.py:282
  440.9 2.7 copy-start.24
  445.2 478.2 %all-reduce.8.cloned.1.call-start = ((), (), s32[]{:S(2)}) async-start(), calls=%async_computation.14 | async-start | bytes 12582912 | tf_op jit(solution)/shard_map/psum | solution.py:300
  614.6 89.3 %copy-start.2 = (bf16[1,1,512,1024]{3,2,1,0:T(8,128)(2,1)S(1)}, bf16[1,1,512,1024]{3,2,1,0:T(8,128)(2,1)}, u32[]{:S(2)}) copy-start(bf16[1,1,512,1024]{3,2,1,0:T(8,128)(2,1)} %param.9) | copy-start | bytes 3145732
  614.6 89.3 %copy-start.27 = (f32[1,1024]{1,0:T(1,128)S(1)}, f32[1,1024]{1,0:T(1,128)}, u32[]{:S(2)}) copy-start(f32[1,1024]{1,0:T(1,128)} %copy-done.26) | copy-start | bytes 12292
  614.6 89.3 %copy-start.29 = (f32[512]{0:T(512)S(1)}, f32[512]{0:T(512)}, u32[]{:S(2)}) copy-start(f32[512]{0:T(512)} %copy-done.28) | copy-start | bytes 6148
  616.0 92.2 %copy-start.33 = (f32[512]{0:T(512)S(1)}, f32[512]{0:T(512)}, u32[]{:S(2)}) copy-start(f32[512]{0:T(512)} %copy-done.32) | copy-start | bytes 6148
  616.0 93.5 %copy-start.31 = (f32[512]{0:T(512)S(1)}, f32[512]{0:T(512)}, u32[]{:S(2)}) copy-start(f32[512]{0:T(512)} %copy-done.30) | copy-start | bytes 6148
  923.4 3.6 copy-start.25
  923.4 4.7 copy-start.14
  (17 other events, 25.1 us)
Sparse Core Ops, SparseCore 0:
  14.2 85.6 all-gather.14
  101.4 44.8 all-gather.6
  147.9 22.5 all-gather.8
  172.0 58.2 all-gather.10
  231.7 58.2 all-gather.12
  339.4 31.4 reduce-scatter.6
  407.4 58.3 reduce-scatter.4
  468.4 71.6 reduce-scatter.8
  542.9 71.6 reduce-scatter.10
  617.4 86.4 all-reduce.5
  709.1 214.3 all-reduce.7

commit v2 on v1

--- a/solution.py
+++ b/solution.py
@@ -20,6 +20,7 @@
 NEG = -1e30
 LOG2E = 1.4426950408889634
 C2 = ALPHA * LOG2E
+MESH = pl.DeviceIdType.MESH
 QSCALE = 1.0 / (ALPHA * math.sqrt(DH))
 
 
@@ -212,6 +213,207 @@
     )(own_slot, queries, keys_values, keys_values, attended, grad_out, lse)
 
 
+TILE = 256
+
+
+def piece_parts(n_ctx):
+    row_parts = min(n_ctx, 8)
+    return row_parts, n_ctx // row_parts
+
+
+def reduce_kernel(n_ctx, widths, *refs):
+    count = len(widths)
+    terms, outs = refs[:count], refs[count : 2 * count]
+    (r1, r2, r3, r4, fin, local, stage) = refs[2 * count : 2 * count + 7]
+    (sem_local, sem_out, send1, recv1, send2, recv2, send3, recv3, send4, recv4, send5, recv5, send6, recv6) = refs[
+        2 * count + 7 :
+    ]
+    grp, ctx, wsh = lax.axis_index("grp"), lax.axis_index("ctx"), lax.axis_index("wsh")
+    side, core = wsh // 2, wsh % 2
+    core_peer = (grp, ctx, side * 2 + 1 - core)
+    side_peer = (grp, ctx, (1 - side) * 2 + core)
+    grp_peer = (1 - grp, ctx, wsh)
+    ctx_peers = [(grp, lax.rem(ctx + step, n_ctx), wsh) for step in range(1, n_ctx)]
+
+    barrier = pltpu.get_barrier_semaphore()
+    for peer in [core_peer, side_peer, grp_peer] + ctx_peers:
+        pl.semaphore_signal(barrier, inc=1, device_id=peer, device_id_type=MESH)
+    pl.semaphore_wait(barrier, n_ctx + 2)
+
+    row_parts, col_parts = piece_parts(n_ctx)
+    half = TILE // 2
+    part_rows, part_cols = half // row_parts, TILE // col_parts
+    ranges, first = [], 0
+    for rows, cols in widths:
+        across = cols // TILE
+        ranges.append((first, first + (rows // TILE) * across, across))
+        first = ranges[-1][1]
+    chunks = first
+
+    def block(index, across):
+        return (
+            pl.ds(pl.multiple_of((index // across) * TILE, TILE), TILE),
+            pl.ds(pl.multiple_of((index % across) * TILE, TILE), TILE),
+        )
+
+    def by_range(index, act):
+        for place, (low, high, across) in enumerate(ranges):
+
+            @pl.when((index >= low) & (index < high))
+            def _(place=place, low=low, across=across):
+                act(place, block(index - low, across))
+
+    def part_of(position, offset):
+        return (
+            pl.ds(pl.multiple_of(offset + (position // col_parts) * part_rows, part_rows), part_rows),
+            pl.ds(pl.multiple_of((position % col_parts) * part_cols, part_cols), part_cols),
+        )
+
+    def remote(src, dst, send, recv, peer):
+        return pltpu.make_async_remote_copy(
+            src_ref=src, dst_ref=dst, send_sem=send, recv_sem=recv, device_id=peer, device_id_type=MESH
+        )
+
+    def step_load(index):
+        slot = lax.rem(index, 4)
+
+        def act(place, span):
+            term = terms[place]
+            pltpu.make_async_copy(term.at[:, core, span[0], span[1]], local.at[slot], sem_local.at[slot]).start()
+            remote(
+                term.at[:, 1 - core, span[0], span[1]], r1.at[index], send1.at[slot], recv1.at[index], core_peer
+            ).start()
+
+        by_range(index, act)
+
+    def step_core(index):
+        slot = lax.rem(index, 4)
+        pltpu.make_async_copy(local.at[slot], local.at[slot], sem_local.at[slot]).wait()
+        whole = remote(r1.at[index], r1.at[index], send1.at[slot], recv1.at[index], core_peer)
+        whole.wait_send()
+        whole.wait_recv()
+        r1[index] = r1[index] + local[slot]
+        remote(r1.at[index, 1 - side], r2.at[index], send2.at[slot], recv2.at[index], side_peer).start()
+
+    half_keep = pl.ds(pl.multiple_of(grp * half, half), half)
+    half_give = pl.ds(pl.multiple_of((1 - grp) * half, half), half)
+
+    def step_side(index):
+        slot = lax.rem(index, 4)
+        move = remote(r1.at[index, 1 - side], r2.at[index], send2.at[slot], recv2.at[index], side_peer)
+        move.wait_send()
+        move.wait_recv()
+        r2[index] = r2[index] + r1[index, side]
+        remote(r2.at[index, half_give], r3.at[index], send3.at[slot], recv3.at[index], grp_peer).start()
+
+    def step_grp(index):
+        slot = lax.rem(index, 4)
+        move = remote(r2.at[index, half_give], r3.at[index], send3.at[slot], recv3.at[index], grp_peer)
+        move.wait_send()
+        move.wait_recv()
+        r3[index] = r3[index] + r2[index, half_keep]
+        for place, peer in enumerate(ctx_peers):
+            rows, cols = part_of(peer[1], 0)
+            remote(r3.at[index, rows, cols], r4.at[index, place], send4.at[slot], recv4.at[index], peer).start()
+
+    def step_ctx(index):
+        slot = lax.rem(index, 4)
+        move = remote(r4.at[index], r4.at[index], send4.at[slot], recv4.at[index], ctx_peers[0])
+        move.wait_send()
+        move.wait_recv()
+        rows, cols = part_of(ctx, 0)
+        total = r3[index, rows, cols].astype(jnp.float32)
+        for place in range(n_ctx - 1):
+            total = total + r4[index, place].astype(jnp.float32)
+        rows, cols = part_of(ctx, grp * half)
+        fin[index, rows, cols] = total.astype(jnp.bfloat16)
+        for peer in ctx_peers:
+            here = fin.at[index, rows, cols]
+            remote(here, here, send5.at[slot], recv5.at[index], peer).start()
+
+    def step_back(index):
+        slot = lax.rem(index, 4)
+        move = remote(r4.at[index], r4.at[index], send5.at[slot], recv5.at[index], ctx_peers[0])
+        move.wait_send()
+        move.wait_recv()
+        here = fin.at[index, half_keep]
+        remote(here, here, send6.at[slot], recv6.at[index], grp_peer).start()
+
+    def step_out(index):
+        slot = lax.rem(index, 4)
+        here = fin.at[index, half_give]
+        move = remote(here, here, send6.at[slot], recv6.at[index], grp_peer)
+        move.wait_send()
+        move.wait_recv()
+
+        @pl.when(index >= 4)
+        def _():
+            pltpu.make_async_copy(stage.at[slot], stage.at[slot], sem_out.at[slot]).wait()
+
+        stage[slot] = fin[index].astype(jnp.float32)
+
+        def act(place, span):
+            pltpu.make_async_copy(stage.at[slot], outs[place].at[span[0], span[1]], sem_out.at[slot]).start()
+
+        by_range(index, act)
+
+    stages = (step_core, step_side, step_grp, step_ctx, step_back, step_out)
+
+    step_load(0)
+    step_load(1)
+
+    def body(step, carry):
+        @pl.when(step + 2 < chunks)
+        def _():
+            step_load(step + 2)
+
+        for lag, act in enumerate(stages):
+            index = step - lag
+
+            @pl.when((index >= 0) & (index < chunks))
+            def _(act=act, index=index):
+                act(index)
+
+        return carry
+
+    lax.fori_loop(0, chunks + len(stages) - 1, body, 0)
+    for slot in range(4):
+        pltpu.make_async_copy(stage.at[slot], stage.at[slot], sem_out.at[slot]).wait()
+
+
+def reduce_terms(n_ctx, terms):
+    widths = [(term.shape[0] // 4, term.shape[1]) for term in terms]
+    chunks = sum((rows // TILE) * (cols // TILE) for rows, cols in widths)
+    row_parts, col_parts = piece_parts(n_ctx)
+    part = (TILE // 2 // row_parts, TILE // col_parts)
+    low = jnp.bfloat16
+    dma = pltpu.SemaphoreType.DMA
+    hbm = pl.BlockSpec(memory_space=pl.ANY)
+    return pl.pallas_call(
+        functools.partial(reduce_kernel, n_ctx, widths),
+        out_shape=[jax.ShapeDtypeStruct(width, jnp.float32) for width in widths],
+        in_specs=[hbm] * len(terms),
+        out_specs=[hbm] * len(terms),
+        scratch_shapes=[
+            pltpu.VMEM((chunks, 2, TILE, TILE), low),
+            pltpu.VMEM((chunks, TILE, TILE), low),
+            pltpu.VMEM((chunks, TILE // 2, TILE), low),
+            pltpu.VMEM((chunks, n_ctx - 1) + part, low),
+            pltpu.VMEM((chunks, TILE, TILE), low),
+            pltpu.VMEM((4, 2, TILE, TILE), low),
+            pltpu.VMEM((4, TILE, TILE), jnp.float32),
+            dma((4,)),
+            dma((4,)),
+        ]
+        + [dma((4,)), dma((chunks,))] * 6,
+        compiler_params=pltpu.CompilerParams(
+            collective_id=0, has_side_effects=True, vmem_limit_bytes=60 << 20
+        ),
+        cost_estimate=pl.CostEstimate(flops=1 << 20, bytes_accessed=256 << 20, transcendentals=0),
+        name="reduce_grads",
+    )(*[term.reshape(2, 2, width[0], width[1]) for term, width in zip(terms, widths)])
+
+
 def per_device(n_ctx, inputs, w_qkv, w_out, w_up, w_down, norm_gains, norm_biases, block_map, out_grad):
     slots = n_ctx // 2
     raw = inputs.reshape(BLK, D)
@@ -295,15 +497,8 @@
     grad_tokens, gain_grad0, bias_grad0 = first_back(grad_normed)
     grad_input = (grad_hidden + grad_tokens).reshape(1, 1, BLK, D)
 
-    def reduced(term):
-        shard = lax.psum_scatter(term, "wsh", scatter_dimension=0, tiled=True)
-        return lax.psum(shard, ("grp", "ctx")).astype(jnp.float32)
-
-    summed_down, summed_up, summed_out, summed_qkv = (
-        reduced(term_down),
-        reduced(term_up),
-        reduced(term_out),
-        reduced(term_qkv),
+    summed_down, summed_up, summed_out, summed_qkv = reduce_terms(
+        n_ctx, [term_down, term_up, term_out, term_qkv]
     )
     gain_stack = jnp.stack([gain_grad0, gain_grad1, gain_grad2, gain_grad3])
     bias_stack = jnp.stack([bias_grad0, bias_grad1, bias_grad2, bias_grad3])

time: 948 us -> 723 us (0.76)
  waiting for transfers between devices: 627 us -> 204 us
  Pallas kernels: 66.3 us -> 280 us
    pallas_call x0 -> x1, Pallas kernels: none -> 214 us  [reduce_terms(): pl.pallas_call(functools.partial(reduce_kernel, n_ctx, widths), out_shape...]
    reduce_scatter x4 -> x0, waiting for transfers between devices: 169 us -> none  [reduced(): shard = lax.psum_scatter(term, 'wsh', scatter_dimension=0, tiled=True)]
    psum x1 -> x0, waiting for transfers between devices: 165 us -> none  [reduced(): return lax.psum(shard, ('grp', 'ctx')).astype(jnp.float32)]
    psum x1, waiting for transfers between devices: 87.9 us -> 0.02 us  [per_device(): totals = lax.psum(partial, 'ctx').reshape(slots, BLK, D)]
    convert_element_type x4 -> x0, other arithmetic: 9.65 us -> none  [reduced(): return lax.psum(shard, ('grp', 'ctx')).astype(jnp.float32)]
    unnamed x78 -> x88, local copies, waits for them, and re-layouts: 25.3 us -> 27 us
  transfers between devices with their start and end apart: 11 -> 6, of which waited for: 9 -> 4; matrix products, arithmetic and copies ran while one was open for 11% -> 9% of each run, Pallas kernels for 7% -> 33%
where the time goes in v2:
time: 723 us; the launch traced here: 715 us
  Pallas kernels  280 us (39%)
  waiting for transfers between devices  204 us (28%)
  matrix products  107 us (15%)
  blocking collectives  39.3 us (5%)
  local copies, waits for them, and re-layouts  39.1 us (5%)
  other arithmetic  23.4 us (3%)
  between operations  22.2 us (3%)
    pallas_call x1, Pallas kernels, reduce_terms(): pl.pallas_call(functools.partial(reduce_kernel, n_ctx, widths), out_shape...  214 us
    all_gather x1, waiting for transfers between devices, per_device(): lax.all_gather(jnp.concatenate([raw, tag_rows], axis=0), 'ctx', axis=0)  80.1 us
    dot_general x10, matrix products, dot_dims(): lax.dot_general(left_side, right_side, (((left_dim,), (right_dim,)), ((),...  69.1 us
    all_gather x1, waiting for transfers between devices, per_device(): lax.all_gather(w_down, 'wsh', axis=0, tiled=True)  46.6 us
    pallas_call x1, Pallas kernels, attention_backward(): pl.pallas_call(functools.partial(attn_bwd_kernel, slots), out_shape=(jax....  41.8 us
    all_gather x1, waiting for transfers between devices, per_device(): lax.all_gather(w_up, 'wsh', axis=0, tiled=True)  39.9 us
    psum x1, blocking collectives, per_device(): lax.psum((gain_stack, bias_stack), ('grp', 'ctx', 'wsh'))  39.3 us
    all_gather x1, waiting for transfers between devices, per_device(): full_qkv = lax.all_gather(w_qkv, 'wsh', axis=0, tiled=True)  34.6 us
  transfers between devices with their start and end apart: 6, of which 4 were waited for; matrix products, arithmetic and copies ran while one was open for 9% of the time, Pallas kernels for 33%

profile of v2, /device:TPU:0, one launch (start us, length us, event | category | flops | bytes accessed | tf_op | source)
XLA Modules:
  0.0 714.8 jit_solution(14504264342965780506)
XLA Ops:
  11.8 2.3 concatenate.15
  19.8 80.1 %all-gather.15.cloned.1.call-done = bf16[2112,1024]{1,0:T(8,128)(2,1)} async-done(((bf16[528,1024]{1,0:T(8,128)(2,1)}), bf16[2112,1024]{1,0:T(8,128)(2,1)}) %all-gather.15.cloned.1.call-update) | async-done | bytes 4325392 | tf_op jit(solution)/shard_map/all_gather | solution.py:426
  109.0 2.8 fusion.12
  111.7 34.6 %all-gather.7.cloned.1.call-done = bf16[1024,3072]{1,0:T(8,128)(2,1)} async-done(((bf16[256,3072]{1,0:T(8,128)(2,1)}), bf16[1024,3072]{1,0:T(8,128)(2,1)}) %all-gather.7.cloned.1.call-update) | async-done | bytes 6291472 | tf_op jit(solution)/shard_map/all_gather | solution.py:425
  146.4 3.0 multiply_convert_fusion.1.q_ref
  150.4 8.7 %convolution_convert_fusion.2.k_ref.v_ref = bf16[1536,2048]{1,0:T(8,128)(2,1)} fusion(bf16[1024,3072]{1,0:T(8,128)(2,1)S(1)} %copy-done.35, bf16[1024,1024]{1,0:T(8,128)(2,1)S(1)} %copy-done.14, bf16[512,1024]{1,0:T(8,128)(2,1)S(1)} %fusion.28), kind=kOutput, calls=%fused_computation.12 | convolution fusion | flops 6451888128 | bytes 13631488 | tf_op jit(solution)/shard_map/dot_general | solution.py:448
  159.2 23.9 %attn_fwd.1 = (bf16[512,1024]{1,0:T(8,128)(2,1)S(1)}, f32[8,512,128]{2,1,0:T(8,128)S(1)}) custom-call(s32[1]{0:T(128)} %bitcast.2.slot_ref, bf16[512,1024]{1,0:T(8,128)(2,1)S(1)} %multiply_convert_fusion.1.q_ref, bf16[1536,2048]{1,0:T(8,128)(2,1)} %convolution_convert_fusion.2.k_ref.v_ref, bf16[1536,2048]{1,0:T(8,128)(2,1)} %convolution_convert_fusion.2.k_ref.v_ref), custom_call_target="tpu_custom_call" | custom-call | flops 3221225472 | bytes 16777216 | tf_op jit(solution)/shard_map/attn_fwd/pallas_call | solution.py:106
  184.4 3.0 fusion.63
  190.4 39.9 %all-gather.11.cloned.1.call-done = bf16[1024,4096]{1,0:T(8,128)(2,1)} async-done(((bf16[256,4096]{1,0:T(8,128)(2,1)}), bf16[1024,4096]{1,0:T(8,128)(2,1)}) %all-gather.11.cloned.1.call-update) | async-done | bytes 8388624 | tf_op jit(solution)/shard_map/all_gather | solution.py:429
  230.3 13.1 %fusion.52 = f32[512,4096]{1,0:T(8,128)} fusion(bf16[1024,4096]{1,0:T(8,128)(2,1)} %all-gather.11.cloned.1.call-done, f32[512,1024]{1,0:T(8,128)} %copy-done.5, f32[1024]{0:T(1024)S(1)} %bitcast.122, f32[1024]{0:T(1024)S(1)} %bitcast.114, f32[512]{0:T(512)S(1)} %fusion.46, f32[512]{0:T(512)S(1)} %broadcast_multiply_fusion.2), kind=kOutput, calls=%fused_computation.113 | convolution fusion | flops 4297588736 | bytes 18886656 | tf_op jit(solution)/shard_map/dot_general | solution.py:458
  243.4 46.6 %all-gather.13.cloned.1.call-done = bf16[4096,1024]{1,0:T(8,128)(2,1)} async-done(((bf16[1024,1024]{1,0:T(8,128)(2,1)}), bf16[4096,1024]{1,0:T(8,128)(2,1)}) %all-gather.13.cloned.1.call-update) | async-done | bytes 8388624 | tf_op jit(solution)/shard_map/all_gather | solution.py:430
  290.0 10.3 %fusion.64 = (f32[512]{0:T(512)S(1)}, f32[512,1024]{1,0:T(8,128)S(1)}) fusion(bf16[4096,1024]{1,0:T(8,128)(2,1)} %all-gather.13.cloned.1.call-done, f32[512,4096]{1,0:T(8,128)} %fusion.52), kind=kOutput, calls=%fused_computation.124 | convolution fusion | flops 4314365440 | bytes 18876416 | tf_op jit(solution)/shard_map/dot_general | solution.py:461
  304.4 16.2 %fusion.6 = bf16[512,4096]{1,0:T(8,128)(2,1)} fusion(f32[512,4096]{1,0:T(8,128)} %fusion.52, bf16[4096,1024]{1,0:T(8,128)(2,1)} %all-gather.13.cloned.1.call-done, f32[512,1024]{1,0:T(8,128)S(1)} %get-tuple-element.50, f32[512]{0:T(512)S(1)} %negate_multiply_fusion.3), kind=kOutput, calls=%fused_computation.8 | convolution fusion | flops 4337958912 | bytes 23070720 | tf_op jit(solution)/shard_map/dot_general | solution.py:38
  320.6 9.2 %convolution_convert_fusion = bf16[1024,4096]{1,0:T(8,128)(2,1)} fusion(bf16[512,4096]{1,0:T(8,128)(2,1)} %fusion.6, f32[512,1024]{1,0:T(8,128)S(1)} %copy-done.6, f32[1024]{0:T(1024)S(1)} %bitcast.123, f32[1024]{0:T(1024)S(1)} %bitcast.115, f32[512]{0:T(512)S(1)} %fusion.46, f32[512]{0:T(512)S(1)} %broadcast_multiply_fusion.2), kind=kOutput, calls=%fused_computation.10 | convolution fusion | flops 4301783040 | bytes 14692352 | tf_op jit(solution)/shard_map/dot_general | solution.py:38
  329.8 7.2 %multiply_reduce_fusion = (f32[1024]{0:T(1024)S(1)}, f32[512]{0:T(512)S(1)}, f32[1024]{0:T(1024)S(1)}, f32[512,1024]{1,0:T(8,128)S(1)}) fusion(f32[512,1024]{1,0:T(8,128)S(1)} %copy-done.6, f32[512]{0:T(512)S(1)} %fusion.46, f32[512]{0:T(512)S(1)} %broadcast_multiply_fusion.2, f32[1024]{0:T(1024)S(1)} %bitcast.116, bf16[512,4096]{1,0:T(8,128)(2,1)} %fusion.6, ...), kind=kOutput, calls=%fused_computation.58 | convolution fusion | flops 4299159040 | bytes 16795648 | tf_op jit(solution)/shard_map/dot_general | solution.py:38
  343.6 41.8 %attn_bwd.1 = (bf16[512,1024]{1,0:T(8,128)(2,1)S(1)}, bf16[1024,1536]{1,0:T(8,128)(2,1)}, bf16[1024,1536]{1,0:T(8,128)(2,1)}) custom-call(s32[1]{0:T(128)} %bitcast.2.slot_ref, bf16[512,1024]{1,0:T(8,128)(2,1)S(1)} %multiply_convert_fusion.1.q_ref, bf16[1536,2048]{1,0:T(8,128)(2,1)} %convolution_convert_fusion.2.k_ref.v_ref, ...), custom_call_target="tpu_custom_call" | custom-call | flops 8053063680 | bytes 25165824 | tf_op jit(solution)/shard_map/attn_bwd/pallas_call | solution.py:187
  385.5 2.2 constant_dynamic-update-slice_fusion.1
  390.1 8.5 %convolution_convert_fusion.3 = bf16[1024,2048]{1,0:T(8,128)(2,1)} fusion(bf16[2048,1536]{1,0:T(8,128)(2,1)S(1)} %constant_dynamic-update-slice_fusion, bf16[1024,1024]{1,0:T(8,128)(2,1)S(1)} %copy-done.15, bf16[512,1024]{1,0:T(8,128)(2,1)S(1)} %copy-done.21), kind=kOutput, calls=%fused_computation.23 | convolution fusion | flops 6450839552 | bytes 13631488 | tf_op jit(solution)/shard_map/dot_general | solution.py:38
  398.7 6.8 fusion.13
  405.4 2.7 copy-done.23
  409.8 2.6 convolution_convert_fusion.4
  412.4 4.0 copy.18
  416.4 6.1 pad_maximum_fusion
  422.5 2.7 convolution_convert_fusion.5
  425.1 10.5 %convolution_convert_fusion.1 = bf16[4096,1024]{1,0:T(8,128)(2,1)} fusion(f32[512,1024]{1,0:T(8,128)S(1)} %copy-done.19, f32[512]{0:T(512)S(1)} %negate_multiply_fusion.3, f32[512,4096]{1,0:T(8,128)} %fusion.52), kind=kOutput, calls=%fused_computation.11 | convolution fusion | flops 4319084544 | bytes 18876416 | tf_op jit(solution)/shard_map/dot_general | solution.py:38
  435.6 213.8 %reduce_grads.1 = (f32[1024,1024]{1,0:T(8,128)}, f32[256,4096]{1,0:T(8,128)}, f32[256,1024]{1,0:T(8,128)}, f32[256,3072]{1,0:T(8,128)}) custom-call(bf16[2,2,1024,1024]{3,2,1,0:T(8,128)(2,1)} %bitcast.91, bf16[2,2,256,4096]{3,2,1,0:T(8,128)(2,1)} %bitcast.90, bf16[2,2,256,1024]{3,2,1,0:T(8,128)(2,1)} %bitcast.93, bf16[2,2,256,3072]{3,2,1,0:T(8,128)(2,1)} %bitcast.89), custom_call_target="tpu_custom_call" | custom-call | flops 1048576 | bytes 268435456 | tf_op jit(solution)/shard_map/reduce_grads/pallas_call | solution.py:392
  649.5 4.3 fusion.54
  655.3 2.0 add_bitcast_fusion
  657.4 39.3 %all-reduce.1 = (f32[4,1024]{1,0:T(4,128)}, f32[4,1024]{1,0:T(4,128)}) all-reduce(f32[4,1024]{1,0:T(4,128)S(1)} %get-tuple-element.72, f32[4,1024]{1,0:T(4,128)S(1)} %get-tuple-element.73), channel_id=1, replica_groups=mesh['grp'=2,'ctx'=4,'wsh'=4] {'grp','ctx','wsh'}, use_global_device_ids=true, to_apply=%region_25.26 | all-reduce | flops 8192 | bytes 65536 | tf_op jit(solution)/shard_map/psum | solution.py:505
  696.8 4.0 copy.26
  701.8 2.1 copy.28
  705.5 2.0 copy.29
  (144 shorter events, 36.3 us)
Async XLA Ops:
  7.2 92.7 %all-gather.15.cloned.1.call-start = ((), (), s32[]{:S(2)}) async-start(), calls=%async_computation.5 | async-start | bytes 5406720 | tf_op jit(solution)/shard_map/all_gather | solution.py:426
  14.1 132.3 %all-gather.7.cloned.1.call-start = ((), (), s32[]{:S(2)}) async-start(), calls=%async_computation | async-start | bytes 7864320 | tf_op jit(solution)/shard_map/all_gather | solution.py:425
  14.8 169.6 %all-gather.9.cloned.1.call-start = ((), (), s32[]{:S(2)}) async-start(), calls=%async_computation.1 | async-start | bytes 2621440 | tf_op jit(solution)/shard_map/all_gather | solution.py:428
  15.6 214.7 %all-gather.11.cloned.1.call-start = ((), (), s32[]{:S(2)}) async-start(), calls=%async_computation.2 | async-start | bytes 10485760 | tf_op jit(solution)/shard_map/all_gather | solution.py:429
  16.2 273.8 %all-gather.13.cloned.1.call-start = ((), (), s32[]{:S(2)}) async-start(), calls=%async_computation.3 | async-start | bytes 10485760 | tf_op jit(solution)/shard_map/all_gather | solution.py:430
  16.8 2.5 copy-start.34
  16.8 632.7 %all-reduce.4.cloned.1.call-start = ((), (), s32[]{:S(2)}) async-start(), calls=%async_computation.4 | async-start | bytes 4194304 | tf_op jit(solution)/shard_map/psum | solution.py:484
  18.3 89.6 %copy-start.26 = (f32[512]{0:T(512)}, f32[512]{0:T(512)S(1)}, u32[]{:S(2)}) copy-start(f32[512]{0:T(512)S(1)} %broadcast_multiply_fusion.4) | copy-start | bytes 6148
  19.3 88.6 %copy-start.28 = (f32[512]{0:T(512)}, f32[512]{0:T(512)S(1)}, u32[]{:S(2)}) copy-start(f32[512]{0:T(512)S(1)} %fusion.44) | copy-start | bytes 6148
  19.3 89.6 %copy-start.24 = (f32[1,1024]{1,0:T(1,128)}, f32[1,1024]{1,0:T(1,128)S(1)}, u32[]{:S(2)}) copy-start(f32[1,1024]{1,0:T(1,128)S(1)} %get-tuple-element.58) | copy-start | bytes 12292
  19.8 129.6 %copy-start.20 = (bf16[512,1024]{1,0:T(8,128)(2,1)}, bf16[512,1024]{1,0:T(8,128)(2,1)S(1)}, u32[]{:S(2)}) copy-start(bf16[512,1024]{1,0:T(8,128)(2,1)S(1)} %fusion.28) | copy-start | bytes 3145732
  146.4 3.0 copy-start.14
  146.4 4.1 copy-start.35
  302.5 27.4 %slice-start = ((s8[8388608]{0:T(1024)(128)(4,1)}), s8[4194304]{0:T(1024)(128)(4,1)S(1)}, s32[]{:S(2)}) async-start(s8[8388608]{0:T(1024)(128)(4,1)} %bitcast.124), calls=%async_computation.6 | async-start | bytes 8388608
  304.4 16.2 %copy-start.18 = (f32[512,1024]{1,0:T(8,128)}, f32[512,1024]{1,0:T(8,128)S(1)}, u32[]{:S(2)}) copy-start(f32[512,1024]{1,0:T(8,128)S(1)} %get-tuple-element.50) | copy-start | bytes 6291460
  304.4 25.4 %slice-start.1 = ((s8[8388608]{0:T(1024)(128)(4,1)}), s8[4194304]{0:T(1024)(128)(4,1)S(1)}, s32[]{:S(2)}) async-start(s8[8388608]{0:T(1024)(128)(4,1)} %bitcast.124), calls=%async_computation.7 | async-start | bytes 8388608
  339.8 2.5 copy-start.36
  341.1 2.5 copy-start.16
  385.5 2.8 copy-start.13
  388.3 10.3 %slice-start.2 = ((s8[6291456]{0:T(1024)(128)(4,1)}), s8[4194304]{0:T(1024)(128)(4,1)S(1)}, s32[]{:S(2)}) async-start(s8[6291456]{0:T(1024)(128)(4,1)} %bitcast.126), calls=%async_computation.8 | async-start | bytes 8388608
  390.1 8.5 %slice-start.3 = ((s8[6291456]{0:T(1024)(128)(4,1)}), s8[2097152]{0:T(1024)(128)(4,1)S(1)}, s32[]{:S(2)}) async-start(s8[6291456]{0:T(1024)(128)(4,1)} %bitcast.126), calls=%async_computation.9 | async-start | bytes 4194304
  405.4 2.7 copy-start.23
  416.4 6.1 copy-start.17
  422.5 2.7 copy-start.19
  435.6 213.8 %copy-start.2 = (bf16[1,1,512,1024]{3,2,1,0:T(8,128)(2,1)S(1)}, bf16[1,1,512,1024]{3,2,1,0:T(8,128)(2,1)}, u32[]{:S(2)}) copy-start(bf16[1,1,512,1024]{3,2,1,0:T(8,128)(2,1)} %param.9) | copy-start | bytes 3145732
  435.6 213.8 %copy-start.25 = (f32[1,1024]{1,0:T(1,128)S(1)}, f32[1,1024]{1,0:T(1,128)}, u32[]{:S(2)}) copy-start(f32[1,1024]{1,0:T(1,128)} %copy-done.24) | copy-start | bytes 12292
  435.6 213.8 %copy-start.27 = (f32[512]{0:T(512)S(1)}, f32[512]{0:T(512)}, u32[]{:S(2)}) copy-start(f32[512]{0:T(512)} %copy-done.26) | copy-start | bytes 6148
  649.4 4.3 copy-start.31
  649.4 4.4 copy-start.29
  696.8 4.0 copy-start.22
  696.8 5.0 copy-start.12
  701.8 3.7 copy-start.11
  (15 other events, 22.6 us)
Sparse Core Ops, SparseCore 0:
  14.2 85.6 all-gather.14
  101.4 44.8 all-gather.6
  147.9 22.5 all-gather.8
  172.0 58.2 all-gather.10
  231.7 58.2 all-gather.12
  409.9 122.0 all-reduce.3

commit v3 on v2

--- a/solution.py
+++ b/solution.py
@@ -62,72 +62,432 @@
     return col <= row
 
 
-def attn_fwd_kernel(slots, slot_ref, q_ref, k_ref, v_ref, o_ref, lse_ref):
-    own_slot = slot_ref[0]
+PIECE = 128
+SPAN = 512
+CHAIN = 64
+
+
+def remote(src, dst, send, recv, peer):
+    return pltpu.make_async_remote_copy(
+        src_ref=src, dst_ref=dst, send_sem=send, recv_sem=recv, device_id=peer, device_id_type=MESH
+    )
+
+
+def local_wait(ref, sem):
+    pltpu.make_async_copy(ref, ref, sem).wait()
+
+
+def aligned(start, size):
+    return pl.ds(pl.multiple_of(start, size), size)
+
+
+def softmax_block(q_ref, kv_ref, acc, top_ref, sum_ref, pair, base, own, visible):
+    lanes = aligned(pair * 128, 128)
+    value_lanes = aligned(D + pair * 128, 128)
     causal = causal_tile()
+    first = head_lanes(0, QT)
     for tile in range(BLK // QT):
         rows = pl.ds(tile * QT, QT)
-        own_keys = (tile + 1) * QT
-        q_pair = q_ref[rows, :]
-        outs, lses = [], []
+        q_pair = q_ref[rows, lanes]
+        if own:
+            spans = [(tile * QT, QT, True)] + ([(0, tile * QT, False)] if tile else [])
+        else:
+            spans = [(0, BLK, False)]
+            old_top, old_sum = top_ref[pair, rows, :], sum_ref[pair, rows, :]
+        tops, sums, outs = [], [], []
         for head in range(2):
             q_head = jnp.where(head_lanes(head, QT), q_pair, jnp.zeros_like(q_pair))
-            diag = contract_last(q_head, k_ref[pl.ds(tile * QT, QT), :])
-            diag = jnp.where(causal, diag, NEG)
-            parts = [(diag, tile * QT, QT, None)]
-            top = jnp.max(diag, axis=-1, keepdims=True)
-            if tile:
-                low_part = contract_last(q_head, k_ref[pl.ds(0, tile * QT), :])
-                parts.append((low_part, 0, tile * QT, None))
-                top = jnp.maximum(top, jnp.max(low_part, axis=-1, keepdims=True))
-            for slot in range(slots):
-                visible = slot < own_slot
-                part = contract_last(q_head, k_ref[pl.ds((slot + 1) * BLK, BLK), :])
-                parts.append((part, (slot + 1) * BLK, BLK, visible))
-                slot_top = jnp.max(part, axis=-1, keepdims=True)
-                top = jnp.maximum(top, jnp.where(visible, slot_top, NEG))
-            shift = top * C2
+            parts = []
+            for start, size, diagonal in spans:
+                part = contract_last(q_head, kv_ref[pl.ds(base + start, size), lanes])
+                parts.append(jnp.where(causal, part, NEG) if diagonal else part)
+            top = functools.reduce(
+                jnp.maximum, [jnp.max(part, axis=-1, keepdims=True) for part in parts]
+            )
+            top = top * C2
+            if not own:
+                top = jnp.maximum(
+                    jnp.where(visible, top, NEG), old_top[:, head * DH : head * DH + 1]
+                )
+            shift = top if own else top + jnp.where(visible, 0.0, 1e30)
             total = jnp.zeros((QT, 1), jnp.float32)
-            acc = jnp.zeros((QT, 128), jnp.float32)
-            for part, start, size, visible in parts:
-                row_shift = shift if visible is None else shift + jnp.where(visible, 0.0, 1e30)
-                expo = jnp.exp2(part * C2 - row_shift)
+            out = jnp.zeros((QT, 128), jnp.float32)
+            for part, (start, size, _) in zip(parts, spans):
+                expo = jnp.exp2(part * C2 - shift)
                 total = total + jnp.sum(expo, axis=-1, keepdims=True)
-                acc = acc + dot_dims(expo.astype(jnp.bfloat16), v_ref[pl.ds(start, size), :], 1, 0)
-            outs.append(acc / total)
-            lses.append(jnp.broadcast_to(shift + jnp.log2(total), (QT, 128)))
-        first = head_lanes(0, QT)
-        o_ref[rows, :] = jnp.where(first, outs[0], outs[1]).astype(jnp.bfloat16)
-        lse_ref[0, rows, :] = jnp.where(first, lses[0], lses[1])
-
-
-def attention_forward(own_slot, queries, keys_values, slots):
-    keys = (slots + 1) * BLK
+                out = out + dot_dims(
+                    expo.astype(jnp.bfloat16), kv_ref[pl.ds(base + start, size), value_lanes], 1, 0
+                )
+            tops.append(jnp.broadcast_to(top, (QT, 128)))
+            sums.append(jnp.broadcast_to(total, (QT, 128)))
+            outs.append(out)
+        new_top = jnp.where(first, tops[0], tops[1])
+        new_sum = jnp.where(first, sums[0], sums[1])
+        new_out = jnp.where(first, outs[0], outs[1])
+        if not own:
+            keep = jnp.exp2(old_top - new_top)
+            new_sum = new_sum + old_sum * keep
+            new_out = new_out + acc[rows, lanes] * keep
+        top_ref[pair, rows, :] = new_top
+        sum_ref[pair, rows, :] = new_sum
+        acc[rows, lanes] = new_out
+
+
+def forward_kernel(n_ctx, *refs):
+    slots = n_ctx // 2
+    (slot_ref, gain_ref, bias_ref, x_hbm, w_qkv, w_out, w_up, w_down) = refs[:8]
+    (a_out, q_out, kv_out, o_out, lse_out, full_qkv, full_out, full_up, full_down) = refs[8:17]
+    (x_own, left, right, a_all, q_all, kv_all, weight, acc, low_out, tops, sums) = refs[17:28]
+    (sem_in, sem_out, side_s, side_r, grp_s, grp_r, cs_s, cs_r, cg_s, cg_r, own_s, own_r, left_s, left_r, right_s, right_r) = refs[28:]
+    grp, ctx, wsh = lax.axis_index("grp"), lax.axis_index("ctx"), lax.axis_index("wsh")
+    side, core = wsh // 2, wsh % 2
+    core_peer = (grp, ctx, side * 2 + 1 - core)
+    side_peer = (grp, ctx, (1 - side) * 2 + core)
+    grp_peer = (1 - grp, ctx, wsh)
+    next_ctx = (grp, lax.rem(ctx + 1, n_ctx), wsh)
+    last_ctx = (grp, lax.rem(ctx + n_ctx - 1, n_ctx), wsh)
+
+    load = pltpu.make_async_copy(x_hbm, x_own, sem_in.at[0])
+    load.start()
+    barrier = pltpu.get_barrier_semaphore()
+    for peer in (core_peer, side_peer, grp_peer, next_ctx, last_ctx):
+        pl.semaphore_signal(barrier, inc=1, device_id=peer, device_id_type=MESH)
+    pl.semaphore_wait(barrier, 5)
+
+    shards = (w_qkv, w_out, w_up, w_down)
+    fulls = (weight, full_out, full_up, full_down)
+    ranges, start = [], 0
+    for shard in shards:
+        across = shard.shape[1] // SPAN
+        ranges.append((start, start + across * (shard.shape[0] // (2 * PIECE)), across))
+        start = ranges[-1][1]
+    pieces = start
+
+    def by_range(index, act):
+        for place, (low, high, across) in enumerate(ranges):
+
+            @pl.when((index >= low) & (index < high))
+            def _(place=place, low=low, across=across):
+                act(place, (index - low) // across, aligned(((index - low) % across) * SPAN, SPAN))
+
+    def rows_of(place, owner, half, group):
+        shard_rows = shards[place].shape[0]
+        return aligned(owner * shard_rows + half * (shard_rows // 2) + group * PIECE, PIECE)
+
+    sides_owner = (1 - side) * 2 + core
+
+    def send_piece(index, carry):
+        def act(place, group, cols):
+            remote(
+                shards[place].at[rows_of(place, 0, grp, group), cols],
+                fulls[place].at[rows_of(place, wsh, grp, group), cols],
+                side_s.at[index],
+                side_r.at[index],
+                side_peer,
+            ).start()
+
+        by_range(index, act)
+        return carry
+
+    def own_copies():
+        copies = []
+        across = shards[0].shape[1] // SPAN
+        for place in range(4):
+            shard_rows = shards[place].shape[0]
+            mine = aligned(wsh * shard_rows, shard_rows)
+            steps = range(across) if place == 0 else [None]
+            for step in steps:
+                cols = slice(None) if step is None else pl.ds(step * SPAN, SPAN)
+                number = len(copies)
+                copies.append(
+                    remote(
+                        shards[place].at[:, cols],
+                        fulls[place].at[mine, cols],
+                        own_s.at[number],
+                        own_r.at[number],
+                        core_peer,
+                    )
+                )
+        return copies
+
+    lax.fori_loop(0, pieces, send_piece, 0)
+    for copy in own_copies():
+        copy.start()
+    for place in range(4):
+        shard_rows = shards[place].shape[0]
+        pltpu.make_async_copy(
+            shards[place], fulls[place].at[aligned(wsh * shard_rows, shard_rows), :], sem_in.at[1 + place]
+        ).start()
+    load.wait()
+
+    own_tag = slot_ref[1]
+    chain_chunks = slots * (BLK // CHAIN)
+
+    def chain_step(stream, send, recv, number, is_first, is_last, target):
+        slot = number // (BLK // CHAIN)
+        spot = aligned((number % (BLK // CHAIN)) * CHAIN, CHAIN)
+        mine = jnp.where(own_tag == slot, x_own[spot, :], jnp.zeros((CHAIN, D), jnp.bfloat16))
+        here = stream.at[slot, spot]
+
+        @pl.when(is_first)
+        def _():
+            stream[slot, spot, :] = mine
+
+        @pl.when(jnp.logical_not(is_first))
+        def _():
+            remote(here, here, send.at[number], recv.at[number], target).wait_recv()
+            stream[slot, spot, :] = stream[slot, spot, :] + mine
+
+        @pl.when(jnp.logical_not(is_last))
+        def _():
+            remote(here, here, send.at[number], recv.at[number], target).start()
+
+    def tick(step):
+        number = step - ctx
+
+        @pl.when((number >= 0) & (number < chain_chunks))
+        def _():
+            chain_step(left, left_s, left_r, number, ctx == 0, ctx == n_ctx - 1, next_ctx)
+
+        back = step - (n_ctx - 1 - ctx)
+
+        @pl.when((back >= 0) & (back < chain_chunks))
+        def _():
+            chain_step(right, right_s, right_r, back, ctx == n_ctx - 1, ctx == 0, last_ctx)
+
+        @pl.when(step < pieces)
+        def _():
+            def act(place, group, cols):
+                here = fulls[place].at[rows_of(place, sides_owner, grp, group), cols]
+                remote(here, here, side_s.at[step], side_r.at[step], side_peer).wait_recv()
+                remote(here, here, grp_s.at[step], grp_r.at[step], grp_peer).start()
+                remote(here, here, cs_s.at[step], cs_r.at[step], core_peer).start()
+
+            by_range(step, act)
+
+        @pl.when((step >= 1) & (step <= pieces))
+        def _():
+            def act(place, group, cols):
+                here = fulls[place].at[rows_of(place, sides_owner, 1 - grp, group), cols]
+                remote(here, here, grp_s.at[step - 1], grp_r.at[step - 1], grp_peer).wait_recv()
+                remote(here, here, cg_s.at[step - 1], cg_r.at[step - 1], core_peer).start()
+
+            by_range(step - 1, act)
+
+    def normalise(source, dest):
+        gain, bias = gain_ref[...], bias_ref[...]
+
+        def body(index, carry):
+            rows = aligned(index * 128, 128)
+            values = source(rows).astype(jnp.float32)
+            a_all[aligned(dest + index * 128, 128), :] = layer_norm(values, gain, bias).astype(
+                jnp.bfloat16
+            )
+            return carry
+
+        lax.fori_loop(0, BLK // 128, body, 0)
+
+    def piece_ready(index):
+        here = fulls[0].at[pl.ds(0, PIECE), pl.ds(0, SPAN)]
+        remote(here, here, cs_s.at[index], cs_r.at[index], core_peer).wait_recv()
+        remote(here, here, cg_s.at[index], cg_r.at[index], core_peer).wait_recv()
+        whole = fulls[0].at[pl.ds(0, 2 * PIECE), pl.ds(0, SPAN)]
+        remote(whole, whole, own_s.at[index], own_r.at[index], core_peer).wait_recv()
+
+    tick(0)
+    normalise(lambda rows: x_own[rows, :], 0)
+    tick(1)
+    shard_rows = w_qkv.shape[0]
+    local_wait(weight.at[pl.ds(0, shard_rows), :], sem_in.at[1])
+
+    def project_q(index, carry):
+        tick(index + 2)
+        piece_ready(index)
+        cols = aligned(index * SPAN, SPAN)
+        q_all[:, cols] = (
+            jnp.dot(a_all[pl.ds(0, BLK), :], weight[:, cols], preferred_element_type=jnp.float32) * QSCALE
+        ).astype(jnp.bfloat16)
+        return carry
+
+    lax.fori_loop(0, D // SPAN, project_q, 0)
+    head_ticks = 2 + D // SPAN
+
+    def project_kv(index, base):
+        cols = aligned(index * SPAN, SPAN)
+        rows = aligned(base, BLK)
+        kv_all[rows, cols] = jnp.dot(
+            a_all[rows, :], weight[:, aligned(D + index * SPAN, SPAN)], preferred_element_type=jnp.float32
+        ).astype(jnp.bfloat16)
+
+    def own_kv(index, carry):
+        tick(index + head_ticks)
+        piece_ready(index + D // SPAN)
+        project_kv(index, 0)
+        return carry
+
+    lax.fori_loop(0, 2 * D // SPAN, own_kv, 0)
+    own_ticks = head_ticks + 2 * D // SPAN
+    outputs = [
+        pltpu.make_async_copy(weight, full_qkv, sem_out.at[0]),
+        pltpu.make_async_copy(q_all, q_out, sem_out.at[1]),
+    ]
+    for copy in outputs:
+        copy.start()
+
+    def own_attention(pair, carry):
+        tick(pair + own_ticks)
+        softmax_block(q_all, kv_all, acc, tops, sums, pair, 0, True, None)
+        return carry
+
+    lax.fori_loop(0, PAIRS, own_attention, 0)
+    used = own_ticks + PAIRS
+    per_slot = 2 * D // SPAN + PAIRS
+
+    need = BLK // CHAIN + n_ctx - 1
+    early = max(0, need - used)
+    if early:
+        lax.fori_loop(0, early, lambda index, carry: (tick(used + index), carry)[1], 0)
+
+    def each_slot(slot, carry):
+        base = pl.multiple_of((slot + 1) * BLK, BLK)
+        visible = slot < slot_ref[0]
+        begin = early + used + slot * per_slot
+
+        def total(rows):
+            joined = left[slot, rows, :] + right[slot, rows, :]
+            return jnp.where(own_tag == slot, x_own[rows, :], joined)
+
+        normalise(total, base)
+
+        def slot_kv(index, inner):
+            tick(begin + index)
+            project_kv(index, base)
+            return inner
+
+        lax.fori_loop(0, 2 * D // SPAN, slot_kv, 0)
+
+        def slot_attention(pair, inner):
+            tick(begin + 2 * D // SPAN + pair)
+            softmax_block(q_all, kv_all, acc, tops, sums, pair, base, False, visible)
+            return inner
+
+        lax.fori_loop(0, PAIRS, slot_attention, 0)
+        return carry
+
+    lax.fori_loop(0, slots, each_slot, 0)
+    done_ticks = early + used + slots * per_slot
+
+    def finish(pair, carry):
+        lanes = aligned(pair * 128, 128)
+        low_out[:, lanes] = (acc[:, lanes] / sums[pair]).astype(jnp.bfloat16)
+        tops[pair] = tops[pair] + jnp.log2(sums[pair])
+        return carry
+
+    lax.fori_loop(0, PAIRS, finish, 0)
+    outputs += [
+        pltpu.make_async_copy(a_all, a_out, sem_out.at[2]),
+        pltpu.make_async_copy(kv_all, kv_out, sem_out.at[3]),
+        pltpu.make_async_copy(low_out, o_out, sem_out.at[4]),
+        pltpu.make_async_copy(tops, lse_out, sem_out.at[5]),
+    ]
+    for copy in outputs[2:]:
+        copy.start()
+    all_ticks = max(pieces + 1, chain_chunks + n_ctx - 1)
+    if all_ticks > done_ticks:
+        lax.fori_loop(done_ticks, all_ticks, lambda index, carry: (tick(index), carry)[1], 0)
+
+    def drain(index, carry):
+        here = fulls[0].at[pl.ds(0, PIECE), pl.ds(0, SPAN)]
+
+        @pl.when(index >= ranges[0][1])
+        def _():
+            remote(here, here, cs_s.at[index], cs_r.at[index], core_peer).wait_recv()
+            remote(here, here, cg_s.at[index], cg_r.at[index], core_peer).wait_recv()
+
+        remote(here, here, side_s.at[index], side_r.at[index], side_peer).wait_send()
+        remote(here, here, grp_s.at[index], grp_r.at[index], grp_peer).wait_send()
+        remote(here, here, cs_s.at[index], cs_r.at[index], core_peer).wait_send()
+        remote(here, here, cg_s.at[index], cg_r.at[index], core_peer).wait_send()
+        return carry
+
+    lax.fori_loop(0, pieces, drain, 0)
+    copies = own_copies()
+    for number, copy in enumerate(copies):
+        copy.wait_send()
+        if number >= len(copies) - 3:
+            copy.wait_recv()
+    for place in range(1, 4):
+        rows = shards[place].shape[0]
+        pltpu.make_async_copy(
+            shards[place], fulls[place].at[aligned(wsh * rows, rows), :], sem_in.at[1 + place]
+        ).wait()
+
+    def drain_chain(index, carry):
+        here = left.at[0, pl.ds(0, CHAIN)]
+
+        @pl.when(ctx < n_ctx - 1)
+        def _():
+            remote(here, here, left_s.at[index], left_r.at[index], next_ctx).wait_send()
+
+        @pl.when(ctx > 0)
+        def _():
+            remote(here, here, right_s.at[index], right_r.at[index], last_ctx).wait_send()
+
+        return carry
+
+    lax.fori_loop(0, chain_chunks, drain_chain, 0)
+    for copy in outputs:
+        copy.wait()
+
+
+def forward_part(n_ctx, tags, gain, bias, raw, w_qkv, w_out, w_up, w_down):
+    slots = n_ctx // 2
+    every = (slots + 1) * BLK
+    low, full = jnp.bfloat16, jnp.float32
+    dma = pltpu.SemaphoreType.DMA
+    hbm = pl.BlockSpec(memory_space=pl.ANY)
+    vmem = pl.BlockSpec(memory_space=pltpu.VMEM)
+    shards = (w_qkv, w_out, w_up, w_down)
+    pieces = sum(w.shape[0] * w.shape[1] // (2 * PIECE * SPAN) for w in shards)
+    own = w_qkv.shape[1] // SPAN + 3
+    chain = slots * (BLK // CHAIN)
+    shape = jax.ShapeDtypeStruct
     return pl.pallas_call(
-        functools.partial(attn_fwd_kernel, slots),
-        out_shape=(
-            jax.ShapeDtypeStruct((BLK, D), jnp.bfloat16),
-            jax.ShapeDtypeStruct((PAIRS, BLK, 128), jnp.float32),
+        functools.partial(forward_kernel, n_ctx),
+        out_shape=[
+            shape((every, D), low),
+            shape((BLK, D), low),
+            shape((every, 2 * D), low),
+            shape((BLK, D), low),
+            shape((PAIRS, BLK, 128), full),
+        ]
+        + [shape((4 * w.shape[0], w.shape[1]), low) for w in shards],
+        in_specs=[pl.BlockSpec(memory_space=pltpu.SMEM), vmem, vmem] + [hbm] * 5,
+        out_specs=[hbm] * 9,
+        scratch_shapes=[
+            pltpu.VMEM((BLK, D), low),
+            pltpu.VMEM((slots, BLK, D), low),
+            pltpu.VMEM((slots, BLK, D), low),
+            pltpu.VMEM((every, D), low),
+            pltpu.VMEM((BLK, D), low),
+            pltpu.VMEM((every, 2 * D), low),
+            pltpu.VMEM((D, 3 * D), low),
+            pltpu.VMEM((BLK, D), full),
+            pltpu.VMEM((BLK, D), low),
+            pltpu.VMEM((PAIRS, BLK, 128), full),
+            pltpu.VMEM((PAIRS, BLK, 128), full),
+            dma((5,)),
+            dma((6,)),
+        ]
+        + [dma((pieces,))] * 8
+        + [dma((own,))] * 2
+        + [dma((chain,))] * 4,
+        compiler_params=pltpu.CompilerParams(
+            collective_id=1, has_side_effects=True, vmem_limit_bytes=60 << 20
         ),
-        grid_spec=pltpu.PrefetchScalarGridSpec(
-            num_scalar_prefetch=1,
-            grid=(PAIRS,),
-            in_specs=[
-                pl.BlockSpec((BLK, 128), lambda i, s: (0, i)),
-                pl.BlockSpec((keys, 128), lambda i, s: (0, i)),
-                pl.BlockSpec((keys, 128), lambda i, s: (0, i + PAIRS)),
-            ],
-            out_specs=(
-                pl.BlockSpec((BLK, 128), lambda i, s: (0, i)),
-                pl.BlockSpec((1, BLK, 128), lambda i, s: (i, 0, 0)),
-            ),
-        ),
-        compiler_params=pltpu.CompilerParams(vmem_limit_bytes=48 << 20),
-        cost_estimate=pl.CostEstimate(
-            flops=4 * BLK * keys * D, bytes_accessed=16 << 20, transcendentals=BLK * keys * HEADS
-        ),
-        name="attn_fwd",
-    )(own_slot, queries, keys_values, keys_values)
+        cost_estimate=pl.CostEstimate(flops=20 << 30, bytes_accessed=64 << 20, transcendentals=1 << 24),
+        name="gather_attend",
+    )(tags, gain, bias, raw, *shards)
 
 
 def attn_bwd_kernel(
@@ -269,11 +629,6 @@
             pl.ds(pl.multiple_of((position % col_parts) * part_cols, part_cols), part_cols),
         )
 
-    def remote(src, dst, send, recv, peer):
-        return pltpu.make_async_remote_copy(
-            src_ref=src, dst_ref=dst, send_sem=send, recv_sem=recv, device_id=peer, device_id_type=MESH
-        )
-
     def step_load(index):
         slot = lax.rem(index, 4)
 
@@ -421,34 +776,20 @@
     block_entry = block_map.reshape(2)
     own_slot = block_entry[1] // BLK
     own_tag = jnp.where(block_entry[0] == 0, own_slot, n_ctx)
-    tag_rows = jnp.full((16, D), own_tag.astype(jnp.bfloat16))
-    full_qkv = lax.all_gather(w_qkv, "wsh", axis=0, tiled=True)
-    shared = lax.all_gather(jnp.concatenate([raw, tag_rows], axis=0), "ctx", axis=0)
-    full_out, full_up, full_down = (
-        lax.all_gather(w_out, "wsh", axis=0, tiled=True),
-        lax.all_gather(w_up, "wsh", axis=0, tiled=True),
-        lax.all_gather(w_down, "wsh", axis=0, tiled=True),
+    slot_vec = own_slot.reshape(1)
+    every_low, queries, keys_values, attn_low, lse, full_qkv, full_out, full_up, full_down = forward_part(
+        n_ctx,
+        jnp.stack([own_slot, own_tag]),
+        norm_gains[0:1],
+        norm_biases[0:1],
+        raw,
+        w_qkv,
+        w_out,
+        w_up,
+        w_down,
     )
-    tags = shared[:, BLK, 0].astype(jnp.int32)
-    prompt = [
-        lax.dynamic_index_in_dim(shared, jnp.argmax(tags == slot), 0, keepdims=False)[:BLK]
-        for slot in range(slots)
-    ]
-    slot_vec = own_slot.reshape(1)
-
-    first_norm, first_back = jax.vjp(layer_norm, tokens, norm_gains[0], norm_biases[0])
-    normed_low = first_norm.astype(jnp.bfloat16)
-    prompt_low = layer_norm(
-        jnp.concatenate(prompt, axis=0).astype(jnp.float32), norm_gains[0], norm_biases[0]
-    ).astype(jnp.bfloat16)
-    every_low = jnp.concatenate([normed_low, prompt_low], axis=0)
-    queries = (
-        jnp.dot(normed_low, full_qkv[:, :D], preferred_element_type=jnp.float32) * QSCALE
-    ).astype(jnp.bfloat16)
-    keys_values = jnp.dot(
-        every_low, full_qkv[:, D:], preferred_element_type=jnp.float32
-    ).astype(jnp.bfloat16)
-    attn_low, lse = attention_forward(slot_vec, queries, keys_values, slots)
+    normed_low = every_low[:BLK]
+    _, first_back = jax.vjp(layer_norm, tokens, norm_gains[0], norm_biases[0])
 
     branch = jnp.dot(attn_low, full_out, preferred_element_type=jnp.float32)
     post_attn, attn_back = jax.vjp(layer_norm, branch, norm_gains[1], norm_biases[1])

time: 723 us -> 599 us (0.83)
  waiting for transfers between devices: 204 us -> 0.04 us
  Pallas kernels: 280 us -> 400 us
  matrix products: 107 us -> 89.2 us
  local copies, waits for them, and re-layouts: 39.1 us -> 29.8 us
    all_gather x5 -> x0, waiting for transfers between devices: 201 us -> none  [the longest x1 80.1 us: per_device(): lax.all_gather(jnp.concatenate([raw, tag_rows], axis=0), 'ctx', axis=0)]
    pallas_call x1, Pallas kernels: 23.9 us -> 153 us  [forward_part(): pl.pallas_call(functools.partial(forward_kernel, n_ctx), out_shape=[shape...]
    dot_general x2 -> x0, matrix products: 11.7 us -> none  [the longest x1 8.74 us: per_device(): jnp.dot(every_low, full_qkv[:, D:], preferred_element_type=jnp.float32)]
    pallas_call x1, Pallas kernels: 214 us -> 204 us  [reduce_terms(): pl.pallas_call(functools.partial(reduce_kernel, n_ctx, widths), out_shape...]
    dot_general x1, matrix products: 13.1 us -> 4.68 us  [per_device(): upward = jnp.dot(ffn_low, full_up, preferred_element_type=jnp.float32)]
    unnamed x88 -> x59, local copies, waits for them, and re-layouts: 27 us -> 20.9 us
  transfers between devices with their start and end apart: 6 -> 1, of which waited for: 4 -> 0; matrix products, arithmetic and copies ran while one was open for 9% -> 8% of each run, Pallas kernels for 33% -> 34%
where the time goes in v3:
time: 599 us; the launch traced here: 594 us
  Pallas kernels  400 us (67%)
  matrix products  89.2 us (15%)
  blocking collectives  39.2 us (7%)
  local copies, waits for them, and re-layouts  29.8 us (5%)
  between operations  17.9 us (3%)
  other arithmetic  17.8 us (3%)
    pallas_call x1, Pallas kernels, reduce_terms(): pl.pallas_call(functools.partial(reduce_kernel, n_ctx, widths), out_shape...  204 us
    pallas_call x1, Pallas kernels, forward_part(): pl.pallas_call(functools.partial(forward_kernel, n_ctx), out_shape=[shape...  153 us
    dot_general x10, matrix products, dot_dims(): lax.dot_general(left_side, right_side, (((left_dim,), (right_dim,)), ((),...  69.5 us
    pallas_call x1, Pallas kernels, attention_backward(): pl.pallas_call(functools.partial(attn_bwd_kernel, slots), out_shape=(jax....  42.1 us
    psum x1, blocking collectives, per_device(): lax.psum((gain_stack, bias_stack), ('grp', 'ctx', 'wsh'))  39.2 us
    unnamed x59, local copies, waits for them, and re-layouts  20.9 us
  transfers between devices with their start and end apart: 1, of which 0 were waited for; matrix products, arithmetic and copies ran while one was open for 8% of the time, Pallas kernels for 34%

profile of v3, /device:TPU:0, one launch (start us, length us, event | category | flops | bytes accessed | tf_op | source)
XLA Modules:
  0.0 593.7 jit_solution(9124223493076992806)
XLA Ops:
  7.2 1.3 fusion.47
  12.4 1.5 fusion.45
  13.9 153.2 %gather_attend.1 = (bf16[1536,1024]{1,0:T(8,128)(2,1)}, bf16[512,1024]{1,0:T(8,128)(2,1)}, bf16[1536,2048]{1,0:T(8,128)(2,1)}, bf16[512,1024]{1,0:T(8,128)(2,1)}...) custom-call(s32[2]{0:T(128)} %pad_add_fusion.refs_0_, ...), custom_call_target="tpu_custom_call" | custom-call | flops 21474836480 | bytes 67108864 | tf_op jit(solution)/shard_map/gather_attend/pallas_call | solution.py:455
  167.1 3.4 fusion.48
  173.1 4.7 fusion.37
  177.8 11.7 %fusion.49 = (f32[512]{0:T(512)S(1)}, f32[512,1024]{1,0:T(8,128)S(1)}) fusion(bf16[4096,1024]{1,0:T(8,128)(2,1)} %get-tuple-element.27, f32[512,4096]{1,0:T(8,128)S(1)} %fusion.37), kind=kOutput, calls=%fused_computation.100 | convolution fusion | flops 4314365440 | bytes 18876416 | tf_op jit(solution)/shard_map/dot_general | solution.py:802
  190.7 1.3 fusion.19
  192.0 2.0 fusion.43
  194.0 13.4 %fusion.6 = bf16[512,4096]{1,0:T(8,128)(2,1)} fusion(f32[512,4096]{1,0:T(8,128)S(1)} %fusion.37, bf16[4096,1024]{1,0:T(8,128)(2,1)} %get-tuple-element.27, f32[512,1024]{1,0:T(8,128)S(1)} %get-tuple-element.61, f32[512]{0:T(512)S(1)} %negate_multiply_fusion.3), kind=kOutput, calls=%fused_computation.8 | convolution fusion | flops 4337958912 | bytes 23070720 | tf_op jit(solution)/shard_map/dot_general | solution.py:38
  207.3 8.7 %multiply_reduce_fusion = (f32[1024]{0:T(1024)S(1)}, f32[512]{0:T(512)S(1)}, f32[1024]{0:T(1024)S(1)}, f32[512,1024]{1,0:T(8,128)S(1)}) fusion(f32[512,1024]{1,0:T(8,128)S(1)} %get-tuple-element.63, f32[512]{0:T(512)S(1)} %fusion.32, f32[512]{0:T(512)S(1)} %broadcast_multiply_fusion.2, f32[1024]{0:T(1024)S(1)} %bitcast.99, bf16[512,4096]{1,0:T(8,128)(2,1)} %fusion.6, ...), kind=kOutput, calls=%fused_computation.43 | convolution fusion | flops 4299159040 | bytes 16795648 | tf_op jit(solution)/shard_map/dot_general | solution.py:38
  219.3 1.2 copy-done.20
  220.5 1.3 convolution_convert_fusion.5.do_ref
  222.1 42.1 %attn_bwd.1 = (bf16[512,1024]{1,0:T(8,128)(2,1)S(1)}, bf16[1024,1536]{1,0:T(8,128)(2,1)}, bf16[1024,1536]{1,0:T(8,128)(2,1)}) custom-call(s32[1]{0:T(128)} %bitcast.2.slot_ref, bf16[512,1024]{1,0:T(8,128)(2,1)S(1)} %copy-done.1, bf16[1536,2048]{1,0:T(8,128)(2,1)} %get-tuple-element.29.k_ref.v_ref, bf16[1536,2048]{1,0:T(8,128)(2,1)} %get-tuple-element.29.k_ref.v_ref, ...), custom_call_target="tpu_custom_call" | custom-call | flops 8053063680 | bytes 25165824 | tf_op jit(solution)/shard_map/attn_bwd/pallas_call | solution.py:547
  264.2 2.2 constant_dynamic-update-slice_fusion.1
  267.2 6.8 %fusion.7 = f32[1536,1024]{1,0:T(8,128)S(1)} fusion(bf16[2048,1536]{1,0:T(8,128)(2,1)S(1)} %constant_dynamic-update-slice_fusion, bf16[1024,3072]{1,0:T(8,128)(2,1)S(1)} %bitcast.108), kind=kOutput, calls=%fused_computation.14 | convolution fusion | flops 6442450944 | bytes 16777216 | tf_op jit(solution)/shard_map/dot_general | solution.py:38
  274.0 1.9 slice.78
  275.9 1.4 copy-done.18
  277.4 10.9 %convolution_convert_fusion = bf16[1024,4096]{1,0:T(8,128)(2,1)} fusion(bf16[512,4096]{1,0:T(8,128)(2,1)} %fusion.6, f32[512,1024]{1,0:T(8,128)} %copy-done.2, f32[1024]{0:T(1024)S(1)} %bitcast.103, f32[1024]{0:T(1024)S(1)} %bitcast.101, f32[512]{0:T(512)S(1)} %fusion.32, f32[512]{0:T(512)S(1)} %broadcast_multiply_fusion.2), kind=kOutput, calls=%fused_computation.10 | convolution fusion | flops 4301783040 | bytes 14692352 | tf_op jit(solution)/shard_map/dot_general | solution.py:38
  288.3 2.9 convolution_convert_fusion.4
  292.8 8.2 %convolution_convert_fusion.2 = bf16[1024,2048]{1,0:T(8,128)(2,1)} fusion(bf16[1536,1024]{1,0:T(8,128)(2,1)S(1)} %copy-done.22, bf16[2048,1536]{1,0:T(8,128)(2,1)S(1)} %copy-done.16), kind=kOutput, calls=%fused_computation.16 | convolution fusion | flops 6444548096 | bytes 13631488 | tf_op jit(solution)/shard_map/dot_general | solution.py:38
  301.1 2.6 convolution_convert_fusion.3
  303.7 4.0 copy.17
  307.6 6.1 %pad_maximum_fusion = bf16[1024,3072]{1,0:T(8,128)(2,1)} fusion(bf16[1024,2048]{1,0:T(8,128)(2,1)} %convolution_convert_fusion.2, bf16[1024,1024]{1,0:T(8,128)(2,1)} %copy.17), kind=kLoop, calls=%fused_computation.12 | loop fusion | flops 12582912 | bytes 12582912 | tf_op jit(solution)/shard_map/concatenate | solution.py:831
  313.8 10.3 %convolution_convert_fusion.1 = bf16[4096,1024]{1,0:T(8,128)(2,1)} fusion(f32[512,1024]{1,0:T(8,128)S(1)} %copy-done.14, f32[512]{0:T(512)S(1)} %negate_multiply_fusion.3, f32[512,4096]{1,0:T(8,128)} %copy-done.21), kind=kOutput, calls=%fused_computation.11 | convolution fusion | flops 4319084544 | bytes 18876416 | tf_op jit(solution)/shard_map/dot_general | solution.py:38
  324.0 204.2 %reduce_grads.1 = (f32[1024,1024]{1,0:T(8,128)}, f32[256,4096]{1,0:T(8,128)}, f32[256,1024]{1,0:T(8,128)}, f32[256,3072]{1,0:T(8,128)}) custom-call(bf16[2,2,1024,1024]{3,2,1,0:T(8,128)(2,1)} %bitcast.80, bf16[2,2,256,4096]{3,2,1,0:T(8,128)(2,1)} %bitcast.79, bf16[2,2,256,1024]{3,2,1,0:T(8,128)(2,1)} %bitcast.82, bf16[2,2,256,3072]{3,2,1,0:T(8,128)(2,1)} %bitcast.77), custom_call_target="tpu_custom_call" | custom-call | flops 1048576 | bytes 268435456 | tf_op jit(solution)/shard_map/reduce_grads/pallas_call | solution.py:747
  528.5 4.4 fusion.39
  534.5 2.0 add_bitcast_fusion
  536.6 39.2 %all-reduce = (f32[4,1024]{1,0:T(4,128)}, f32[4,1024]{1,0:T(4,128)}) all-reduce(f32[4,1024]{1,0:T(4,128)S(1)} %pad_maximum_fusion.1, f32[4,1024]{1,0:T(4,128)S(1)} %pad_maximum_fusion.2), channel_id=1, replica_groups=mesh['grp'=2,'ctx'=4,'wsh'=4] {'grp','ctx','wsh'}, use_global_device_ids=true, to_apply=%region_21.22 | all-reduce | flops 8192 | bytes 65536 | tf_op jit(solution)/shard_map/psum | solution.py:846
  575.8 4.0 copy.24
  580.9 2.1 copy.26
  583.0 1.6 copy-done.8
  584.6 2.0 copy.27
  (85 shorter events, 13.1 us)
Async XLA Ops:
  7.2 521.3 %all-reduce.3.cloned.1.call-start = ((), (), s32[]{:S(2)}) async-start(), calls=%async_computation | async-start | bytes 4194304 | tf_op jit(solution)/shard_map/psum | solution.py:825
  167.1 6.0 %slice-start.2 = ((s8[8388608]{0:T(1024)(128)(4,1)}), s8[4194304]{0:T(1024)(128)(4,1)S(1)}, s32[]{:S(2)}) async-start(s8[8388608]{0:T(1024)(128)(4,1)} %bitcast.109), calls=%async_computation.3 | async-start | bytes 8388608
  170.5 1.2 copy-start.6
  170.5 2.5 slice-start.3
  172.7 43.4 %copy-start.2 = (f32[512,1024]{1,0:T(8,128)}, f32[512,1024]{1,0:T(8,128)S(1)}, u32[]{:S(2)}) copy-start(f32[512,1024]{1,0:T(8,128)S(1)} %get-tuple-element.63) | copy-start | bytes 6291460
  177.8 16.2 %copy-start.21 = (f32[512,4096]{1,0:T(8,128)}, f32[512,4096]{1,0:T(8,128)S(1)}, u32[]{:S(2)}) copy-start(f32[512,4096]{1,0:T(8,128)S(1)} %fusion.37) | copy-start | bytes 25165828
  189.5 1.2 copy-start.5
  194.0 13.4 %copy-start.13 = (f32[512,1024]{1,0:T(8,128)}, f32[512,1024]{1,0:T(8,128)S(1)}, u32[]{:S(2)}) copy-start(f32[512,1024]{1,0:T(8,128)S(1)} %get-tuple-element.61) | copy-start | bytes 6291460
  218.0 1.3 copy-start.3
  218.0 2.5 copy-start.20
  219.3 2.5 copy-start.11
  220.5 1.3 copy-start
  220.5 1.5 copy-start.1
  220.5 46.7 %slice-start = ((s8[6291456]{0:T(1024)(128)(4,1)}), s8[2097152]{0:T(1024)(128)(4,1)S(1)}, s32[]{:S(2)}) async-start(s8[6291456]{0:T(1024)(128)(4,1)} %bitcast.107), calls=%async_computation.1 | async-start | bytes 4194304
  222.1 45.2 %slice-start.1 = ((s8[6291456]{0:T(1024)(128)(4,1)}), s8[4194304]{0:T(1024)(128)(4,1)S(1)}, s32[]{:S(2)}) async-start(s8[6291456]{0:T(1024)(128)(4,1)} %bitcast.107), calls=%async_computation.2 | async-start | bytes 8388608
  264.2 2.8 copy-start.10
  267.2 6.8 %copy-start.15 = (bf16[2048,1536]{1,0:T(8,128)(2,1)}, bf16[2048,1536]{1,0:T(8,128)(2,1)S(1)}, u32[]{:S(2)}) copy-start(bf16[2048,1536]{1,0:T(8,128)(2,1)S(1)} %constant_dynamic-update-slice_fusion) | copy-start | bytes 18874372
  274.0 3.3 copy-start.18
  277.3 10.9 %copy-start.12 = (f32[512,1024]{1,0:T(8,128)S(1)}, f32[512,1024]{1,0:T(8,128)}, u32[]{:S(2)}) copy-start(f32[512,1024]{1,0:T(8,128)} %copy-done.11) | copy-start | bytes 6291460
  288.3 3.6 copy-start.16
  288.3 4.6 copy-start.22
  307.6 6.1 %copy-start.14 = (f32[512,1024]{1,0:T(8,128)S(1)}, f32[512,1024]{1,0:T(8,128)}, u32[]{:S(2)}) copy-start(f32[512,1024]{1,0:T(8,128)} %copy-done.13) | copy-start | bytes 6291460
  324.0 204.5 %copy-start.7 = (bf16[1,1,512,1024]{3,2,1,0:T(8,128)(2,1)S(1)}, bf16[1,1,512,1024]{3,2,1,0:T(8,128)(2,1)}, u32[]{:S(2)}) copy-start(bf16[1,1,512,1024]{3,2,1,0:T(8,128)(2,1)} %param.9) | copy-start | bytes 3145732
  324.0 204.5 %copy-start.19 = (f32[1,1024]{1,0:T(1,128)S(1)}, f32[1,1024]{1,0:T(1,128)}, u32[]{:S(2)}) copy-start(f32[1,1024]{1,0:T(1,128)} %get-tuple-element.68.refs_1_) | copy-start | bytes 12292
  532.9 1.6 copy-start.4
  575.8 4.0 copy-start.17
  575.8 5.0 copy-start.9
  580.8 3.7 copy-start.8
Sparse Core Ops, SparseCore 0:
  277.5 111.0 all-reduce.2

commit v4 on v3

v4 whole, which is shorter than its diff:
```python
import functools
import math

import jax
import jax.numpy as jnp
from jax import lax
from jax.experimental import pallas as pl
from jax.experimental.pallas import tpu as pltpu
from jax.sharding import PartitionSpec as P

D = 1024
HEADS = 16
DH = 64
BLK = 512
PAIRS = HEADS // 2
QT = 256

EPS = 1e-05
ALPHA = 32.0
NEG = -1e30
LOG2E = 1.4426950408889634
C2 = ALPHA * LOG2E
MESH = pl.DeviceIdType.MESH
QSCALE = 1.0 / (ALPHA * math.sqrt(DH))


def layer_norm(values, gain_row, bias_row):
    centre = values - jnp.mean(values, axis=-1, keepdims=True)
    spread = jnp.mean(centre * centre, axis=-1, keepdims=True)
    return centre * lax.rsqrt(spread + EPS) * gain_row + bias_row


def gelu_tanh(values):
    return jax.nn.gelu(values, approximate=True)


def dot_dims(left_side, right_side, left_dim, right_dim):
    return lax.dot_general(
        left_side,
        right_side,
        (((left_dim,), (right_dim,)), ((), ())),
        preferred_element_type=jnp.float32,
    )


def contract_last(left_side, right_side):
    return dot_dims(left_side, right_side, 1, 1)


def contract_rows(left_side, right_side):
    return dot_dims(left_side, right_side, 0, 0)


def head_lanes(head, rows):
    lane = lax.broadcasted_iota(jnp.int32, (rows, 128), 1)
    return (lane >= DH) if head else (lane < DH)


def causal_tile():
    row = lax.broadcasted_iota(jnp.int32, (QT, QT), 0)
    col = lax.broadcasted_iota(jnp.int32, (QT, QT), 1)
    return col <= row


PIECE = 128
SPAN = 512
CHAIN = 64
HOP = 2
LAG = 2
GROUP = 4
AHEAD = 4


def remote(src, dst, send, recv, peer):
    return pltpu.make_async_remote_copy(
        src_ref=src, dst_ref=dst, send_sem=send, recv_sem=recv, device_id=peer, device_id_type=MESH
    )


def local_wait(ref, sem):
    pltpu.make_async_copy(ref, ref, sem).wait()


def aligned(start, size):
    return pl.ds(pl.multiple_of(start, size), size)


def softmax_block(q_ref, kv_ref, acc, top_ref, sum_ref, pair, base, own, visible):
    lanes = aligned(pair * 128, 128)
    value_lanes = aligned(D + pair * 128, 128)
    causal = causal_tile()
    first = head_lanes(0, QT)
    count = BLK // QT
    q_pair = q_ref[:, lanes]
    keys = kv_ref[pl.ds(base, BLK), lanes]
    values = kv_ref[pl.ds(base, BLK), value_lanes]
    if not own:
        old_top, old_sum, old_out = top_ref[pair], sum_ref[pair], acc[:, lanes]
        hide = jnp.where(visible, 0.0, 1e30)
    results = []
    work = [(tile, head) for tile in range(count) for head in range(2)]
    parts_of = {}
    for tile, head in work:
        q_tile = q_pair[tile * QT : (tile + 1) * QT]
        q_head = jnp.where(head_lanes(head, QT), q_tile, jnp.zeros_like(q_tile))
        span = (tile + 1) * QT if own else BLK
        parts_of[tile, head] = contract_last(q_head, keys[:span])
    top_of, expo_of, total_of = {}, {}, {}
    for tile, head in work:
        part = parts_of[tile, head]
        if own:
            diag = jnp.where(causal, part[:, tile * QT :], NEG)
            part = jnp.concatenate([part[:, : tile * QT], diag], axis=1) if tile else diag
        top = jnp.max(part, axis=-1, keepdims=True) * C2
        if own:
            shift = top
        else:
            top = jnp.maximum(
                jnp.where(visible, top, NEG), old_top[tile * QT : (tile + 1) * QT, head * DH : head * DH + 1]
            )
            shift = top + hide
        expo = jnp.exp2(part * C2 - shift)
        top_of[tile, head] = jnp.broadcast_to(top, (QT, 128))
        total_of[tile, head] = jnp.broadcast_to(jnp.sum(expo, axis=-1, keepdims=True), (QT, 128))
        expo_of[tile, head] = expo.astype(jnp.bfloat16)
    out_of = {}
    for tile, head in work:
        span = (tile + 1) * QT if own else BLK
        out_of[tile, head] = dot_dims(expo_of[tile, head], values[:span], 1, 0)
    for tile in range(count):
        rows = pl.ds(tile * QT, QT)
        new_top = jnp.where(first, top_of[tile, 0], top_of[tile, 1])
        new_sum = jnp.where(first, total_of[tile, 0], total_of[tile, 1])
        new_out = jnp.where(first, out_of[tile, 0], out_of[tile, 1])
        if not own:
            here = slice(tile * QT, (tile + 1) * QT)
            keep = jnp.exp2(old_top[here] - new_top)
            new_sum = new_sum + old_sum[here] * keep
            new_out = new_out + old_out[here] * keep
        top_ref[pair, rows, :] = new_top
        sum_ref[pair, rows, :] = new_sum
        acc[rows, lanes] = new_out


def forward_kernel(n_ctx, *refs):
    slots = n_ctx // 2
    (slot_ref, gain_ref, bias_ref, x_hbm, w_qkv, w_out, w_up, w_down) = refs[:8]
    (a_out, q_out, kv_out, o_out, lse_out, full_qkv, full_out, full_up, full_down) = refs[8:17]
    (x_own, left, right, a_all, q_all, kv_all, weight, acc, tops, sums, hop) = refs[17:28]
    (sem_in, sem_load, sem_store, sem_out, sem_a, sem_kv, side_s, side_r, grp_s, grp_r, cs_s, cs_r, cg_s, cg_r, own_s, own_r, left_s, left_r, right_s, right_r) = refs[28:]
    grp, ctx, wsh = lax.axis_index("grp"), lax.axis_index("ctx"), lax.axis_index("wsh")
    side, core = wsh // 2, wsh % 2
    core_peer = (grp, ctx, side * 2 + 1 - core)
    side_peer = (grp, ctx, (1 - side) * 2 + core)
    grp_peer = (1 - grp, ctx, wsh)
    next_ctx = (grp, lax.rem(ctx + 1, n_ctx), wsh)
    last_ctx = (grp, lax.rem(ctx + n_ctx - 1, n_ctx), wsh)

    load = pltpu.make_async_copy(x_hbm, x_own, sem_in.at[0])
    load.start()
    barrier = pltpu.get_barrier_semaphore()
    for peer in (core_peer, side_peer, grp_peer, next_ctx, last_ctx):
        pl.semaphore_signal(barrier, inc=1, device_id=peer, device_id_type=MESH)
    pl.semaphore_wait(barrier, 5)

    shards = (w_qkv, w_out, w_up, w_down)
    fulls = (weight, full_out, full_up, full_down)
    ranges, start = [], 0
    for shard in shards:
        across = shard.shape[1] // SPAN
        ranges.append((start, start + across * (shard.shape[0] // (2 * PIECE)), across))
        start = ranges[-1][1]
    pieces = start

    def by_range(index, act):
        for place, (low, high, across) in enumerate(ranges):

            @pl.when((index >= low) & (index < high))
            def _(place=place, low=low, across=across):
                act(place, (index - low) // across, aligned(((index - low) % across) * SPAN, SPAN))

    def rows_of(place, owner, half, group):
        shard_rows = shards[place].shape[0]
        return aligned(owner * shard_rows + half * (shard_rows // 2) + group * PIECE, PIECE)

    sides_owner = (1 - side) * 2 + core

    def send_piece(index, carry):
        def act(place, group, cols):
            remote(
                shards[place].at[rows_of(place, 0, grp, group), cols],
                fulls[place].at[rows_of(place, wsh, grp, group), cols],
                side_s.at[index],
                side_r.at[index],
                side_peer,
            ).start()

        by_range(index, act)
        return carry

    def own_copies():
        copies = []
        across = shards[0].shape[1] // SPAN
        for place in range(4):
            shard_rows = shards[place].shape[0]
            mine = aligned(wsh * shard_rows, shard_rows)
            steps = range(across) if place == 0 else [None]
            for step in steps:
                cols = slice(None) if step is None else pl.ds(step * SPAN, SPAN)
                number = len(copies)
                copies.append(
                    remote(
                        shards[place].at[:, cols],
                        fulls[place].at[mine, cols],
                        own_s.at[number],
                        own_r.at[number],
                        core_peer,
                    )
                )
        return copies

    for index in range(AHEAD):
        send_piece(index, 0)
    for copy in own_copies():
        copy.start()
    own_rows = aligned(wsh * w_qkv.shape[0], w_qkv.shape[0])
    own_weight = pltpu.make_async_copy(w_qkv, weight.at[own_rows, :], sem_in.at[1])
    own_weight.start()
    load.wait()

    bounces, start = [], 0
    for shard in shards[1:]:
        across = shard.shape[1] // SPAN
        bounces.append((start, start + across * (shard.shape[0] // (2 * PIECE)), across))
        start = bounces[-1][1]
    moves = start

    def bounce(index, loading):
        slot = lax.rem(index, 3)
        for place, (low, high, across) in enumerate(bounces):

            @pl.when((index >= low) & (index < high))
            def _(place=place + 1, low=low, across=across):
                group = (index - low) // across
                cols = aligned(((index - low) % across) * SPAN, SPAN)
                if loading:
                    here = shards[place].at[aligned(group * 2 * PIECE, 2 * PIECE), cols]
                    pltpu.make_async_copy(here, hop.at[slot], sem_load.at[slot]).start()
                else:
                    rows = aligned(wsh * shards[place].shape[0] + group * 2 * PIECE, 2 * PIECE)
                    local_wait(hop.at[slot], sem_load.at[slot])
                    pltpu.make_async_copy(
                        hop.at[slot], fulls[place].at[rows, cols], sem_store.at[slot]
                    ).start()

    own_tag = slot_ref[1]
    chain_chunks = slots * (BLK // CHAIN)

    def chain_step(stream, send, recv, number, is_first, is_last, target):
        slot = number // (BLK // CHAIN)
        spot = aligned((number % (BLK // CHAIN)) * CHAIN, CHAIN)
        mine = jnp.where(own_tag == slot, x_own[spot, :], jnp.zeros((CHAIN, D), jnp.bfloat16))
        here = stream.at[slot, spot]

        @pl.when(is_first)
        def _():
            stream[slot, spot, :] = mine

        @pl.when(jnp.logical_not(is_first))
        def _():
            remote(here, here, send.at[number], recv.at[number], target).wait_recv()
            stream[slot, spot, :] = stream[slot, spot, :] + mine

        @pl.when(jnp.logical_not(is_last))
        def _():
            remote(here, here, send.at[number], recv.at[number], target).start()

    def tick(step):
        @pl.when((step >= 1) & (step <= moves))
        def _():
            bounce(step - 1, False)

        @pl.when((step >= 3) & (step < moves))
        def _():
            local_wait(hop.at[lax.rem(step, 3)], sem_store.at[lax.rem(step, 3)])

        @pl.when(step < moves)
        def _():
            bounce(step, True)

        @pl.when(step + AHEAD < pieces)
        def _():
            send_piece(step + AHEAD, 0)

        number = step - HOP * ctx

        @pl.when((number >= 0) & (number < chain_chunks))
        def _():
            chain_step(left, left_s, left_r, number, ctx == 0, ctx == n_ctx - 1, next_ctx)

        back = step - HOP * (n_ctx - 1 - ctx)

        @pl.when((back >= 0) & (back < chain_chunks))
        def _():
            chain_step(right, right_s, right_r, back, ctx == n_ctx - 1, ctx == 0, last_ctx)

        @pl.when(step < pieces)
        def _():
            def act(place, group, cols):
                here = fulls[place].at[rows_of(place, sides_owner, grp, group), cols]
                remote(here, here, side_s.at[step], side_r.at[step], side_peer).wait_recv()
                remote(here, here, grp_s.at[step], grp_r.at[step], grp_peer).start()
                remote(here, here, cs_s.at[step], cs_r.at[step], core_peer).start()

            by_range(step, act)

        late = step - LAG

        @pl.when((late >= 0) & (late < pieces))
        def _():
            def act(place, group, cols):
                here = fulls[place].at[rows_of(place, sides_owner, 1 - grp, group), cols]
                remote(here, here, grp_s.at[late], grp_r.at[late], grp_peer).wait_recv()
                remote(here, here, cg_s.at[late], cg_r.at[late], core_peer).start()

            by_range(late, act)

    def normalise(source, dest):
        gain, bias = gain_ref[...], bias_ref[...]

        def body(index, carry):
            rows = aligned(index * 128, 128)
            values = source(rows).astype(jnp.float32)
            a_all[aligned(dest + index * 128, 128), :] = layer_norm(values, gain, bias).astype(
                jnp.bfloat16
            )
            return carry

        lax.fori_loop(0, BLK // 128, body, 0)

    def piece_ready(index):
        here = fulls[0].at[pl.ds(0, PIECE), pl.ds(0, SPAN)]
        remote(here, here, cs_s.at[index], cs_r.at[index], core_peer).wait_recv()
        remote(here, here, cg_s.at[index], cg_r.at[index], core_peer).wait_recv()
        whole = fulls[0].at[pl.ds(0, 2 * PIECE), pl.ds(0, SPAN)]
        remote(whole, whole, own_s.at[index], own_r.at[index], core_peer).wait_recv()

    tick(0)
    normalise(lambda rows: x_own[rows, :], 0)
    for step in range(1, LAG + 1):
        tick(step)
    own_weight.wait()

    def project_q(index, carry):
        tick(index + LAG + 1)
        piece_ready(index)
        cols = aligned(index * SPAN, SPAN)
        q_all[:, cols] = (
            jnp.dot(a_all[pl.ds(0, BLK), :], weight[:, cols], preferred_element_type=jnp.float32) * QSCALE
        ).astype(jnp.bfloat16)
        return carry

    lax.fori_loop(0, D // SPAN, project_q, 0)
    head_ticks = LAG + 1 + D // SPAN

    def project_kv(index, base):
        cols = aligned(index * SPAN, SPAN)
        rows = aligned(base, BLK)
        kv_all[rows, cols] = jnp.dot(
            a_all[rows, :], weight[:, aligned(D + index * SPAN, SPAN)], preferred_element_type=jnp.float32
        ).astype(jnp.bfloat16)

    def own_kv(index, carry):
        tick(index + head_ticks)
        piece_ready(index + D // SPAN)
        project_kv(index, 0)
        return carry

    lax.fori_loop(0, 2 * D // SPAN, own_kv, 0)
    own_ticks = head_ticks + 2 * D // SPAN

    def send_block(index):
        rows = aligned(index * BLK, BLK)
        pltpu.make_async_copy(a_all.at[rows, :], a_out.at[rows, :], sem_a.at[index]).start()
        pltpu.make_async_copy(kv_all.at[rows, :], kv_out.at[rows, :], sem_kv.at[index]).start()

    outputs = [
        pltpu.make_async_copy(weight, full_qkv, sem_out.at[0]),
        pltpu.make_async_copy(q_all, q_out, sem_out.at[1]),
    ]
    for copy in outputs:
        copy.start()

    send_block(0)

    def own_attention(group, carry):
        tick(own_ticks + 2 * group)
        tick(own_ticks + 2 * group + 1)
        for member in range(GROUP):
            softmax_block(q_all, kv_all, acc, tops, sums, group * GROUP + member, 0, True, None)
        return carry

    groups = PAIRS // GROUP
    lax.fori_loop(0, groups, own_attention, 0)
    used = own_ticks + 2 * groups
    per_slot = 2 * D // SPAN + 2 * groups

    need = BLK // CHAIN + HOP * (n_ctx - 1)
    early = max(0, need - used)
    if early:
        lax.fori_loop(0, early, lambda index, carry: (tick(used + index), carry)[1], 0)

    def each_slot(slot, carry):
        base = pl.multiple_of((slot + 1) * BLK, BLK)
        visible = slot < slot_ref[0]
        begin = early + used + slot * per_slot

        def total(rows):
            joined = left[slot, rows, :] + right[slot, rows, :]
            return jnp.where(own_tag == slot, x_own[rows, :], joined)

        normalise(total, base)

        def slot_kv(index, inner):
            tick(begin + index)
            project_kv(index, base)
            return inner

        lax.fori_loop(0, 2 * D // SPAN, slot_kv, 0)

        send_block(slot + 1)

        def slot_attention(group, inner):
            tick(begin + 2 * D // SPAN + 2 * group)
            tick(begin + 2 * D // SPAN + 2 * group + 1)
            for member in range(GROUP):
                softmax_block(
                    q_all, kv_all, acc, tops, sums, group * GROUP + member, base, False, visible
                )
            return inner

        lax.fori_loop(0, groups, slot_attention, 0)
        return carry

    lax.fori_loop(0, slots, each_slot, 0)
    done_ticks = early + used + slots * per_slot

    def finish(pair, carry):
        lanes = aligned(pair * 128, 128)
        x_own[:, lanes] = (acc[:, lanes] / sums[pair]).astype(jnp.bfloat16)
        tops[pair] = tops[pair] + jnp.log2(sums[pair])
        return carry

    lax.fori_loop(0, PAIRS, finish, 0)
    outputs += [
        pltpu.make_async_copy(x_own, o_out, sem_out.at[2]),
        pltpu.make_async_copy(tops, lse_out, sem_out.at[3]),
    ]
    for copy in outputs[2:]:
        copy.start()
    all_ticks = max(pieces + LAG, chain_chunks + HOP * (n_ctx - 1))
    if all_ticks > done_ticks:
        lax.fori_loop(done_ticks, all_ticks, lambda index, carry: (tick(index), carry)[1], 0)

    def drain(index, carry):
        here = fulls[0].at[pl.ds(0, PIECE), pl.ds(0, SPAN)]

        @pl.when(index >= ranges[0][1])
        def _():
            remote(here, here, cs_s.at[index], cs_r.at[index], core_peer).wait_recv()
            remote(here, here, cg_s.at[index], cg_r.at[index], core_peer).wait_recv()

        remote(here, here, side_s.at[index], side_r.at[index], side_peer).wait_send()
        remote(here, here, grp_s.at[index], grp_r.at[index], grp_peer).wait_send()
        remote(here, here, cs_s.at[index], cs_r.at[index], core_peer).wait_send()
        remote(here, here, cg_s.at[index], cg_r.at[index], core_peer).wait_send()
        return carry

    lax.fori_loop(0, pieces, drain, 0)
    copies = own_copies()
    for number, copy in enumerate(copies):
        copy.wait_send()
        if number >= len(copies) - 3:
            copy.wait_recv()
    for index in range(moves - 3, moves):
        local_wait(hop.at[index % 3], sem_store.at[index % 3])

    def drain_chain(index, carry):
        here = left.at[0, pl.ds(0, CHAIN)]

        @pl.when(ctx < n_ctx - 1)
        def _():
            remote(here, here, left_s.at[index], left_r.at[index], next_ctx).wait_send()

        @pl.when(ctx > 0)
        def _():
            remote(here, here, right_s.at[index], right_r.at[index], last_ctx).wait_send()

        return carry

    lax.fori_loop(0, chain_chunks, drain_chain, 0)
    for copy in outputs:
        copy.wait()

    def drain_blocks(index, carry):
        rows = aligned(index * BLK, BLK)
        local_wait(a_all.at[rows, :], sem_a.at[index])
        local_wait(kv_all.at[rows, :], sem_kv.at[index])
        return carry

    lax.fori_loop(0, slots + 1, drain_blocks, 0)


def forward_part(n_ctx, tags, gain, bias, raw, w_qkv, w_out, w_up, w_down):
    slots = n_ctx // 2
    every = (slots + 1) * BLK
    low, full = jnp.bfloat16, jnp.float32
    dma = pltpu.SemaphoreType.DMA
    hbm = pl.BlockSpec(memory_space=pl.ANY)
    vmem = pl.BlockSpec(memory_space=pltpu.VMEM)
    shards = (w_qkv, w_out, w_up, w_down)
    pieces = sum(w.shape[0] * w.shape[1] // (2 * PIECE * SPAN) for w in shards)
    own = w_qkv.shape[1] // SPAN + 3
    chain = slots * (BLK // CHAIN)
    shape = jax.ShapeDtypeStruct
    return pl.pallas_call(
        functools.partial(forward_kernel, n_ctx),
        out_shape=[
            shape((every, D), low),
            shape((BLK, D), low),
            shape((every, 2 * D), low),
            shape((BLK, D), low),
            shape((PAIRS, BLK, 128), full),
        ]
        + [shape((4 * w.shape[0], w.shape[1]), low) for w in shards],
        in_specs=[pl.BlockSpec(memory_space=pltpu.SMEM), vmem, vmem] + [hbm] * 5,
        out_specs=[hbm] * 9,
        scratch_shapes=[
            pltpu.VMEM((BLK, D), low),
            pltpu.VMEM((slots, BLK, D), low),
            pltpu.VMEM((slots, BLK, D), low),
            pltpu.VMEM((every, D), low),
            pltpu.VMEM((BLK, D), low),
            pltpu.VMEM((every, 2 * D), low),
            pltpu.VMEM((D, 3 * D), low),
            pltpu.VMEM((BLK, D), full),
            pltpu.VMEM((PAIRS, BLK, 128), full),
            pltpu.VMEM((PAIRS, BLK, 128), full),
            pltpu.VMEM((3, 2 * PIECE, SPAN), low),
            dma((2,)),
            dma((3,)),
            dma((3,)),
            dma((4,)),
            dma((slots + 1,)),
            dma((slots + 1,)),
        ]
        + [dma((pieces,))] * 8
        + [dma((own,))] * 2
        + [dma((chain,))] * 4,
        compiler_params=pltpu.CompilerParams(
            collective_id=1, has_side_effects=True, vmem_limit_bytes=63 << 20
        ),
        cost_estimate=pl.CostEstimate(flops=20 << 30, bytes_accessed=64 << 20, transcendentals=1 << 24),
        name="gather_attend",
    )(tags, gain, bias, raw, *shards)


TILE = 256
PAIRED = 2


def grad_block(q_ref, do_ref, o_ref, lse_ref, kv_ref, dq_acc, turned, pair, own, visible):
    lanes = aligned(pair * 128, 128)
    value_lanes = aligned(D + pair * 128, 128)
    size = QT if own else BLK
    count = BLK // size
    q_pair, do_pair, lse_pair = q_ref[:, lanes], do_ref[:, lanes], lse_ref[pair]
    prod = do_pair.astype(jnp.float32) * o_ref[:, lanes].astype(jnp.float32)
    keys, values = kv_ref[:, lanes], kv_ref[:, value_lanes]
    q_turned, do_turned = q_pair.T, do_pair.T
    old_dq = dq_acc[:, lanes]
    causal = causal_tile()
    hide = 0.0 if own else jnp.where(visible, 0.0, 1e30)
    lanes_of = [head_lanes(head, size) for head in range(2)]
    work = [(tile, head) for tile in range(count) for head in range(2)]
    score, dprob, dlogit, prob_low = {}, {}, {}, {}
    for tile, head in work:
        rows = slice(tile * size, (tile + 1) * size)
        span = (tile + 1) * size if own else BLK
        zero = jnp.zeros((size, 128), jnp.bfloat16)
        score[tile, head] = contract_last(jnp.where(lanes_of[head], q_pair[rows], zero), keys[:span])
        dprob[tile, head] = contract_last(jnp.where(lanes_of[head], do_pair[rows], zero), values[:span])
    for tile, head in work:
        rows = slice(tile * size, (tile + 1) * size)
        delta = jnp.sum(jnp.where(lanes_of[head], prod[rows], 0.0), axis=-1, keepdims=True)
        shift = lse_pair[rows, head * DH : head * DH + 1] + hide
        prob = jnp.exp2(score[tile, head] * C2 - shift)
        if own:
            diag = jnp.where(causal, prob[:, tile * size :], 0.0)
            prob = jnp.concatenate([prob[:, : tile * size], diag], axis=1) if tile else diag
        dlogit[tile, head] = (prob * (dprob[tile, head] - delta)).astype(jnp.bfloat16)
        prob_low[tile, head] = prob.astype(jnp.bfloat16)
    for tile in range(count):
        rows = slice(tile * size, (tile + 1) * size)
        span = (tile + 1) * size if own else BLK
        parts = [dot_dims(dlogit[tile, head], keys[:span], 1, 0) for head in range(2)]
        dq_acc[pl.ds(tile * size, size), lanes] = old_dq[rows] + jnp.where(lanes_of[0], parts[0], parts[1])
    for head in range(2):
        for offset, left_side, right_side, scale in (
            (0, q_turned, dlogit, ALPHA),
            (D, do_turned, prob_low, 1.0),
        ):
            spot = aligned(offset + pair * 128 + head * DH, DH)
            left_head = left_side[head * DH : (head + 1) * DH]
            terms = [
                dot_dims(left_head[:, tile * size : (tile + 1) * size], right_side[tile, head], 1, 0)
                for tile in range(count)
            ]
            for tile in range(count):
                cols = slice(tile * size, (tile + 1) * size)
                total = functools.reduce(
                    jnp.add, [terms[other][:, cols] for other in range(tile, count)]
                ) if own else terms[0]
                turned[spot, cols if own else slice(None)] = (total * scale).astype(jnp.bfloat16)


def backward_kernel(n_ctx, widths, *refs):
    slots = n_ctx // 2
    levels = n_ctx.bit_length() - 1
    depth = 8 + levels if levels < 3 else 6 + levels
    (slot_ref, gain_ref, norm_ref, x_hbm, q_hbm, kv_hbm, a_hbm, o_hbm, do_hbm, lse_hbm, w_hbm) = refs[:11]
    terms, outs = list(refs[11:14]), refs[14:18]
    grad_out, norm_out = refs[18:20]
    scratch = list(refs[20:])

    def take(count):
        taken = scratch[:count]
        del scratch[:count]
        return taken

    q_v, o_v, do_v, lse_v, weight, kv_b, a_b, dq_acc, turned, gkv, term, own_part, left, right, norm_v, norm_in = take(16)
    r1, r2, r3, fin, local = take(5)
    zbufs = take(levels)
    sem_in, sem_blk, sem_local, sem_out, sem_res = take(5)
    send1, recv1, send2, recv2, send3, recv3, send6, recv6 = take(8)
    rs_send, rs_recv, ag_send, ag_recv = take(levels), take(levels), take(levels), take(levels)
    left_s, left_r, right_s, right_r, norm_s, norm_r = take(6)
    terms.append(term)

    grp, ctx, wsh = lax.axis_index("grp"), lax.axis_index("ctx"), lax.axis_index("wsh")
    side, core = wsh // 2, wsh % 2
    core_peer = (grp, ctx, side * 2 + 1 - core)
    side_peer = (grp, ctx, (1 - side) * 2 + core)
    grp_peer = (1 - grp, ctx, wsh)
    next_ctx = (grp, lax.rem(ctx + 1, n_ctx), wsh)
    last_ctx = (grp, lax.rem(ctx + n_ctx - 1, n_ctx), wsh)
    bits = [(ctx // (1 << level)) % 2 for level in range(levels)]
    level_peers = [(grp, ctx + (1 - 2 * bits[level]) * (1 << level), wsh) for level in range(levels)]

    loads = [
        pltpu.make_async_copy(source, dest, sem_in.at[place])
        for place, (source, dest) in enumerate(
            ((q_hbm, q_v), (o_hbm, o_v), (do_hbm, do_v), (lse_hbm, lse_v), (w_hbm, weight))
        )
    ]
    for load in loads:
        load.start()

    def block_copies(index):
        rows = aligned(lax.rem(index, slots + 1) * BLK, BLK)
        slot = lax.rem(index, kv_b.shape[0])
        return (
            pltpu.make_async_copy(kv_hbm.at[rows, :], kv_b.at[slot], sem_blk.at[0, slot]),
            pltpu.make_async_copy(a_hbm.at[rows, :], a_b.at[slot], sem_blk.at[1, slot]),
        )

    for copy in block_copies(1):
        copy.start()

    barrier = pltpu.get_barrier_semaphore()
    peers = [core_peer, side_peer, grp_peer, next_ctx, last_ctx] + level_peers
    for peer in peers:
        pl.semaphore_signal(barrier, inc=1, device_id=peer, device_id_type=MESH)
    pl.semaphore_wait(barrier, len(peers))

    half = TILE // 2
    ranges, first = [], 0
    for rows, cols in widths:
        across = cols // TILE
        ranges.append((first, first + (rows // TILE) * across, across))
        first = ranges[-1][1]
    chunks = first

    def by_range(index, act):
        for place, (low, high, across) in enumerate(ranges):

            @pl.when((index >= low) & (index < high))
            def _(place=place, low=low, across=across):
                number = index - low
                act(place, (aligned((number // across) * TILE, TILE), aligned((number % across) * TILE, TILE)))

    def region(level, flip):
        row, rows, col, cols = 0, half, 0, TILE
        for place in range(level):
            bit = 1 - bits[place] if (flip and place == level - 1) else bits[place]
            if rows > 16:
                rows = rows // 2
                row = row + bit * rows
            else:
                cols = cols // 2
                col = col + bit * cols
        return row, rows, col, cols

    def spot(level, flip=False, base=0):
        row, rows, col, cols = region(level, flip)
        return aligned(base + row, rows), aligned(col, cols)

    def step_load(index):
        slot = lax.rem(index, depth)
        near = lax.rem(index, 4)

        def act(place, span):
            source = terms[place]
            pltpu.make_async_copy(source.at[:, core, span[0], span[1]], local.at[near], sem_local.at[near]).start()
            remote(
                source.at[:, 1 - core, span[0], span[1]], r1.at[slot], send1.at[slot], recv1.at[slot], core_peer
            ).start()

        by_range(index, act)

    def finished(move):
        move.wait_send()
        move.wait_recv()

    def step_core(index):
        slot, near = lax.rem(index, depth), lax.rem(index, 4)
        local_wait(local.at[near], sem_local.at[near])
        finished(remote(r1.at[slot], r1.at[slot], send1.at[slot], recv1.at[slot], core_peer))
        r1[slot] = r1[slot] + local[near]
        remote(r1.at[slot, 1 - side], r2.at[slot], send2.at[slot], recv2.at[slot], side_peer).start()

    keep_half = aligned(grp * half, half)
    give_half = aligned((1 - grp) * half, half)

    def step_side(index):
        slot = lax.rem(index, depth)
        finished(remote(r1.at[slot, 1 - side], r2.at[slot], send2.at[slot], recv2.at[slot], side_peer))
        r2[slot] = r2[slot] + r1[slot, side]
        remote(r2.at[slot, give_half], r3.at[slot], send3.at[slot], recv3.at[slot], grp_peer).start()

    def rs_copy(level, slot):
        rows, cols = spot(level + 1, True)
        return remote(
            r3.at[slot, rows, cols], zbufs[level].at[slot], rs_send[level].at[slot], rs_recv[level].at[slot], level_peers[level]
        )

    def ag_copy(level, slot, flip=False):
        rows, cols = spot(level + 1, flip, grp * half)
        here = fin.at[slot, rows, cols]
        return remote(here, here, ag_send[level].at[slot], ag_recv[level].at[slot], level_peers[level])

    def back_copy(slot, rows):
        here = fin.at[slot, rows]
        return remote(here, here, send6.at[slot], recv6.at[slot], grp_peer)

    def step_grp(index):
        slot = lax.rem(index, depth)
        finished(remote(r2.at[slot, give_half], r3.at[slot], send3.at[slot], recv3.at[slot], grp_peer))
        r3[slot] = r3[slot] + r2[slot, keep_half]
        rs_copy(0, slot).start()

    def step_scatter(level):
        def act(index):
            slot = lax.rem(index, depth)
            finished(rs_copy(level, slot))
            rows, cols = spot(level + 1)
            total = r3[slot, rows, cols] + zbufs[level][slot]
            if level + 1 < levels:
                r3[slot, rows, cols] = total
                rs_copy(level + 1, slot).start()
            else:
                rows, cols = spot(level + 1, False, grp * half)
                fin[slot, rows, cols] = total
                ag_copy(level, slot).start()

        return act

    def step_gather(level):
        def act(index):
            slot = lax.rem(index, depth)
            finished(ag_copy(level, slot, True))
            if level:
                ag_copy(level - 1, slot).start()
            else:
                back_copy(slot, keep_half).start()

        return act

    def out_wait(index):
        slot = lax.rem(index, depth)
        local_wait(fin.at[slot], sem_out.at[slot])

    def step_out(index):
        slot = lax.rem(index, depth)
        finished(back_copy(slot, give_half))

        def act(place, span):
            pltpu.make_async_copy(fin.at[slot], outs[place].at[span[0], span[1]], sem_out.at[slot]).start()

        by_range(index, act)

    stages = [(0, step_core), (2, step_side), (4, step_grp)]
    stages += [(5 + level, step_scatter(level)) for level in range(levels)]
    stages += [(5 + 2 * levels - 1 - level, step_gather(level)) for level in reversed(range(levels))]
    stages += [(6 + 2 * levels, step_out), (8 + 2 * levels, out_wait)]
    all_ticks = chunks + stages[-1][0]

    def tick(step):
        @pl.when(step + 2 < chunks)
        def _():
            step_load(step + 2)

        for lag, act in stages:
            index = step - lag

            @pl.when((index >= 0) & (index < chunks))
            def _(act=act, index=index):
                act(index)

    per_slot = BLK // CHAIN
    chain_chunks = slots * per_slot

    def chain_step(stream, send, recv, number, is_first, is_last, target):
        slot = number // per_slot
        rows = aligned((number % per_slot) * CHAIN, CHAIN)
        here = stream.at[slot, rows]

        @pl.when(is_first)
        def _():
            stream[slot, rows, :] = own_part[slot, rows, :]

        @pl.when(jnp.logical_not(is_first))
        def _():
            remote(here, here, send.at[number], recv.at[number], target).wait_recv()
            stream[slot, rows, :] = stream[slot, rows, :] + own_part[slot, rows, :]

        @pl.when(jnp.logical_not(is_last))
        def _():
            remote(here, here, send.at[number], recv.at[number], target).start()

    def chain_tick(step):
        number = step - HOP * ctx

        @pl.when((number >= 0) & (number < chain_chunks))
        def _():
            chain_step(left, left_s, left_r, number, ctx == 0, ctx == n_ctx - 1, next_ctx)

        back = step - HOP * (n_ctx - 1 - ctx)

        @pl.when((back >= 0) & (back < chain_chunks))
        def _():
            chain_step(right, right_s, right_r, back, ctx == n_ctx - 1, ctx == 0, last_ctx)

    chain_ticks = chain_chunks + HOP * (n_ctx - 1)

    step_load(0)
    step_load(1)
    dq_acc[...] = jnp.zeros_like(dq_acc)
    for load in loads:
        load.wait()

    groups = PAIRS // PAIRED

    def attend(kv_ref, own, visible, begin, chained, chain_from):
        def body(group, carry):
            for extra in range(2):
                tick(begin + 2 * group + extra)
            if chained is not None:

                @pl.when(chained)
                def _():
                    for extra in range(2):
                        chain_tick(chain_from + 2 * group + extra)

            for member in range(PAIRED):
                grad_block(
                    q_v, do_v, o_v, lse_v, kv_ref, dq_acc, turned, group * PAIRED + member, own, visible
                )
            return carry

        lax.fori_loop(0, groups, body, 0)

    block_ticks = 2 * groups + 2

    def each_slot(slot, carry):
        visible = slot < slot_ref[0]
        index = slot + 1
        place = lax.rem(index, kv_b.shape[0])
        for copy in block_copies(index):
            copy.wait()
        if kv_b.shape[0] > 1:
            for copy in block_copies(index + 1):
                copy.start()
        begin = slot * block_ticks
        attend(kv_b.at[place], False, visible, begin, slot > 0, (slot - 1) * per_slot)

        def weight_terms(step, inner):
            tick(begin + 2 * groups + step)
            rows = aligned(step * 512, 512)
            for part in range(2):
                cols = pl.ds(part * D, D)
                fresh = dot_dims(a_b[place, :, rows], turned[cols, :], 0, 1)

                @pl.when(slot == 0)
                def _(fresh=fresh, cols=cols):
                    gkv[rows, cols] = fresh.astype(gkv.dtype)

                @pl.when(slot > 0)
                def _(fresh=fresh, cols=cols):
                    gkv[rows, cols] = (gkv[rows, cols] + fresh).astype(gkv.dtype)

            own_part[slot, :, rows] = dot_dims(
                turned[...], weight[rows, pl.ds(D, 2 * D)], 0, 1
            ).astype(jnp.bfloat16)
            return inner

        lax.fori_loop(0, 2, weight_terms, 0)
        if kv_b.shape[0] == 1:
            for copy in block_copies(index + 1):
                copy.start()
        return carry

    lax.fori_loop(0, slots, each_slot, 0)
    begin = slots * block_ticks
    own_place = (slots + 1) % kv_b.shape[0]
    for copy in block_copies(slots + 1):
        copy.wait()
    attend(kv_b.at[own_place], True, None, begin, slots > 0, (slots - 1) * per_slot)
    dq_low = o_v
    dq_low[...] = (dq_acc[...] * ALPHA).astype(jnp.bfloat16) * jnp.bfloat16(QSCALE)
    x_load = pltpu.make_async_copy(x_hbm, do_v, sem_in.at[0])
    x_load.start()

    def last_terms(step, carry):
        tick(begin + 2 * groups + step)
        rows = aligned(step * TILE, TILE)
        a_rows = a_b[own_place, :, rows]
        up, down = step // 2, step % 2
        term[up, down, :, pl.ds(0, D)] = dot_dims(a_rows, dq_low[...], 0, 0).astype(jnp.bfloat16)
        for part in range(2):
            cols = pl.ds(part * D, D)
            term[up, down, :, pl.ds((part + 1) * D, D)] = (
                gkv[rows, cols] + dot_dims(a_rows, turned[cols, :], 0, 1)
            ).astype(jnp.bfloat16)
        return carry

    lax.fori_loop(0, 4, last_terms, 0)
    ready = begin + 2 * groups + 4
    assert ready <= ranges[-1][0] - 2 or n_ctx > 4
    da_acc = dq_acc

    def own_grad(step, carry):
        tick(ready + step)
        chain_tick(chain_chunks + step)
        rows = aligned(step * TILE, TILE)
        da_acc[:, rows] = dot_dims(dq_low[...], weight[rows, pl.ds(0, D)], 1, 1) + dot_dims(
            turned[...], weight[rows, pl.ds(D, 2 * D)], 0, 1
        )
        return carry

    lax.fori_loop(0, 4, own_grad, 0)
    ready = ready + 4

    def flush_chain(step, carry):
        tick(ready + step)
        chain_tick(chain_chunks + 4 + step)
        return carry

    left_over = max(0, chain_ticks - chain_chunks - 4)
    lax.fori_loop(0, left_over, flush_chain, 0)
    ready = ready + left_over
    x_load.wait()
    gain = gain_ref[...]

    def norm_grad(step, carry):
        gain_sum, bias_sum = carry

        @pl.when(step % 2 == 0)
        def _():
            tick(ready + step // 2)

        rows = aligned(step * CHAIN, CHAIN)
        upstream = da_acc[rows, :]
        for slot in range(slots):
            joined = left[slot, rows, :].astype(jnp.float32) + right[slot, rows, :].astype(jnp.float32)
            upstream = upstream + jnp.where(slot_ref[0] == slot, joined, 0.0)
        values = do_v[rows, :].astype(jnp.float32)
        centre = values - jnp.mean(values, axis=-1, keepdims=True)
        scale = lax.rsqrt(jnp.mean(centre * centre, axis=-1, keepdims=True) + EPS)
        centre = centre * scale
        scaled = upstream * gain
        da_acc[rows, :] = scale * (
            scaled
            - jnp.mean(scaled, axis=-1, keepdims=True)
            - centre * jnp.mean(scaled * centre, axis=-1, keepdims=True)
        )
        gain_sum = gain_sum + jnp.sum(upstream * centre, axis=0, keepdims=True)
        bias_sum = bias_sum + jnp.sum(upstream, axis=0, keepdims=True)
        return gain_sum, bias_sum

    zero = jnp.zeros((1, D), jnp.float32)
    gain_sum, bias_sum = lax.fori_loop(0, BLK // CHAIN, norm_grad, (zero, zero))
    ready = ready + BLK // CHAIN // 2
    result = pltpu.make_async_copy(da_acc, grad_out, sem_res.at[0])
    result.start()
    row = lax.broadcasted_iota(jnp.int32, (8, D), 0)
    norm_v[...] = norm_ref[...] + jnp.where(row == 0, gain_sum, 0.0) + jnp.where(row == 4, bias_sum, 0.0)
    for place, peer in enumerate([core_peer, side_peer, grp_peer] + level_peers):
        move = remote(norm_v, norm_in.at[place], norm_s.at[place], norm_r.at[place], peer)
        move.start()
        tick(ready)
        tick(ready + 1)
        ready = ready + 2
        finished(move)
        norm_v[...] = norm_v[...] + norm_in[place]
    norm_result = pltpu.make_async_copy(norm_v, norm_out, sem_res.at[1])
    norm_result.start()
    if all_ticks > ready:
        lax.fori_loop(ready, all_ticks, lambda index, carry: (tick(index), carry)[1], 0)

    def drain_chain(index, carry):
        here = left.at[0, pl.ds(0, CHAIN)]

        @pl.when(ctx < n_ctx - 1)
        def _():
            remote(here, here, left_s.at[index], left_r.at[index], next_ctx).wait_send()

        @pl.when(ctx > 0)
        def _():
            remote(here, here, right_s.at[index], right_r.at[index], last_ctx).wait_send()

        return carry

    lax.fori_loop(0, chain_chunks, drain_chain, 0)
    result.wait()
    norm_result.wait()


def backward_part(n_ctx, slot_vec, gain, norms, raw, q, kv, a, o, do, lse, weight, terms):
    slots = n_ctx // 2
    levels = n_ctx.bit_length() - 1
    depth = 8 + levels if levels < 3 else 6 + levels
    every = (slots + 1) * BLK
    widths = [(term.shape[0] // 4, term.shape[1]) for term in terms] + [(D // 4, 3 * D)]
    low, full = jnp.bfloat16, jnp.float32
    dma = pltpu.SemaphoreType.DMA
    hbm = pl.BlockSpec(memory_space=pl.ANY)
    vmem = pl.BlockSpec(memory_space=pltpu.VMEM)
    shape = jax.ShapeDtypeStruct
    buffers = 2 if slots <= 2 else 1
    chain = slots * (BLK // CHAIN)
    zshapes, rows, cols = [], TILE // 2, TILE
    for _ in range(levels):
        rows, cols = (rows // 2, cols) if rows > 16 else (rows, cols // 2)
        zshapes.append(pltpu.VMEM((depth, rows, cols), low))
    return pl.pallas_call(
        functools.partial(backward_kernel, n_ctx, widths),
        out_shape=[shape(width, low) for width in widths] + [shape((BLK, D), full), shape((8, D), full)],
        in_specs=[pl.BlockSpec(memory_space=pltpu.SMEM), vmem, vmem] + [hbm] * 11,
        out_specs=[hbm] * 6,
        scratch_shapes=[
            pltpu.VMEM((BLK, D), low),
            pltpu.VMEM((BLK, D), low),
            pltpu.VMEM((BLK, D), low),
            pltpu.VMEM((PAIRS, BLK, 128), full),
            pltpu.VMEM((D, 3 * D), low),
            pltpu.VMEM((buffers, BLK, 2 * D), low),
            pltpu.VMEM((buffers, BLK, D), low),
            pltpu.VMEM((BLK, D), full),
            pltpu.VMEM((2 * D, BLK), low),
            pltpu.VMEM((D, 2 * D), full if slots <= 2 else low),
            pltpu.VMEM((2, 2, D // 4, 3 * D), low),
            pltpu.VMEM((slots, BLK, D), low),
            pltpu.VMEM((slots, BLK, D), low),
            pltpu.VMEM((slots, BLK, D), low),
            pltpu.VMEM((8, D), full),
            pltpu.VMEM((3 + levels, 8, D), full),
            pltpu.VMEM((depth, 2, TILE, TILE), low),
            pltpu.VMEM((depth, TILE, TILE), low),
            pltpu.VMEM((depth, TILE // 2, TILE), low),
            pltpu.VMEM((depth, TILE, TILE), low),
            pltpu.VMEM((4, 2, TILE, TILE), low),
        ]
        + zshapes
        + [dma((5,)), dma((2, buffers)), dma((4,)), dma((depth,)), dma((2,))]
        + [dma((depth,))] * (8 + 4 * levels)
        + [dma((chain,))] * 4
        + [dma((3 + levels,))] * 2,
        compiler_params=pltpu.CompilerParams(
            collective_id=2, has_side_effects=True, vmem_limit_bytes=67043328
        ),
        cost_estimate=pl.CostEstimate(flops=40 << 30, bytes_accessed=64 << 20, transcendentals=1 << 24),
        name="attend_back_reduce",
    )(
        slot_vec,
        gain,
        norms,
        raw,
        q,
        kv,
        a,
        o,
        do,
        lse,
        weight,
        *[term.reshape(2, 2, width[0], width[1]) for term, width in zip(terms, widths)],
    )


def per_device(n_ctx, inputs, w_qkv, w_out, w_up, w_down, norm_gains, norm_biases, block_map, out_grad):
    slots = n_ctx // 2
    raw = inputs.reshape(BLK, D)
    tokens = raw.astype(jnp.float32)
    block_entry = block_map.reshape(2)
    own_slot = block_entry[1] // BLK
    own_tag = jnp.where(block_entry[0] == 0, own_slot, n_ctx)
    slot_vec = own_slot.reshape(1)
    every_low, queries, keys_values, attn_low, lse, full_qkv, full_out, full_up, full_down = forward_part(
        n_ctx,
        jnp.stack([own_slot, own_tag]),
        norm_gains[0:1],
        norm_biases[0:1],
        raw,
        w_qkv,
        w_out,
        w_up,
        w_down,
    )

    branch = jnp.dot(attn_low, full_out, preferred_element_type=jnp.float32)
    post_attn, attn_back = jax.vjp(layer_norm, branch, norm_gains[1], norm_biases[1])
    hidden = tokens + post_attn
    pre_ffn, ffn_back = jax.vjp(layer_norm, hidden, norm_gains[2], norm_biases[2])
    ffn_low = pre_ffn.astype(jnp.bfloat16)
    upward = jnp.dot(ffn_low, full_up, preferred_element_type=jnp.float32)
    activated, gelu_back = jax.vjp(gelu_tanh, upward)
    active_low = activated.astype(jnp.bfloat16)
    downward = jnp.dot(active_low, full_down, preferred_element_type=jnp.float32)
    post_ffn, post_back = jax.vjp(layer_norm, downward, norm_gains[3], norm_biases[3])
    result = (hidden + post_ffn).astype(jnp.bfloat16).reshape(1, 1, BLK, D)
    seed_grad = out_grad.reshape(BLK, D).astype(jnp.float32)
    grad_down_in, gain_grad3, bias_grad3 = post_back(seed_grad)
    down_low = grad_down_in.astype(jnp.bfloat16)
    term_down = contract_rows(active_low, down_low).astype(jnp.bfloat16)
    grad_active = contract_last(down_low, full_down)
    up_low = gelu_back(grad_active)[0].astype(jnp.bfloat16)
    term_up = contract_rows(ffn_low, up_low).astype(jnp.bfloat16)
    grad_pre_ffn, gain_grad2, bias_grad2 = ffn_back(contract_last(up_low, full_up))
    grad_hidden = seed_grad + grad_pre_ffn
    grad_branch, gain_grad1, bias_grad1 = attn_back(grad_hidden)
    branch_low = grad_branch.astype(jnp.bfloat16)
    term_out = contract_rows(attn_low, branch_low).astype(jnp.bfloat16)
    grad_out_low = contract_last(branch_low, full_out).astype(jnp.bfloat16)

    zero_row = jnp.zeros((D,), jnp.float32)
    norms = jnp.stack(
        [zero_row, gain_grad1, gain_grad2, gain_grad3, zero_row, bias_grad1, bias_grad2, bias_grad3]
    )
    summed_down, summed_up, summed_out, summed_qkv, grad_tokens, norm_total = backward_part(
        n_ctx,
        slot_vec,
        norm_gains[0:1],
        norms,
        raw,
        queries,
        keys_values,
        every_low,
        attn_low,
        grad_out_low,
        lse,
        full_qkv,
        [term_down, term_up, term_out],
    )
    grad_input = (grad_hidden + grad_tokens).reshape(1, 1, BLK, D)
    summed_down, summed_up, summed_out, summed_qkv = (
        total.astype(jnp.float32) for total in (summed_down, summed_up, summed_out, summed_qkv)
    )
    gain_total, bias_total = norm_total[:4], norm_total[4:]
    return (
        result,
        grad_input,
        summed_qkv,
        summed_out,
        summed_up,
        summed_down,
        gain_total,
        bias_total,
    )


def solution(mesh):
    rows = P("wsh", None)
    blocks = P("grp", "wsh", "ctx", None)
    return jax.shard_map(
        functools.partial(per_device, mesh.shape["ctx"]),
        mesh=mesh,
        in_specs=(blocks, rows, rows, rows, rows, P(), P(), blocks, blocks),
        out_specs=(blocks, blocks, rows, rows, rows, rows, P(), P()),
        check_vma=False,
    )
```

time: 599 us -> 420 us (0.70)
  Pallas kernels: 400 us -> 316 us
  blocking collectives: 39.2 us -> 0 us
  matrix products: 89.2 us -> 64.7 us
  local copies, waits for them, and re-layouts: 29.8 us -> 6.04 us
  between operations: 17.9 us -> 4.74 us
    pallas_call x1, Pallas kernels: 153 us -> 105 us  [forward_part(): pl.pallas_call(functools.partial(forward_kernel, n_ctx), out_shape=[shape...]
    psum x1 -> x0, blocking collectives: 39.2 us -> none  [per_device(): lax.psum((gain_stack, bias_stack), ('grp', 'ctx', 'wsh'))]
    pallas_call x2 -> x1, Pallas kernels: 246 us -> 212 us  [backward_part(): pl.pallas_call(functools.partial(backward_kernel, n_ctx, widths), out_sha...]
    dot_general x10 -> x6, matrix products: 69.5 us -> 44.9 us  [dot_dims(): lax.dot_general(left_side, right_side, (((left_dim,), (right_dim,)), ((),...]
    unnamed x59 -> x34, local copies, waits for them, and re-layouts: 20.9 us -> 1.95 us
    convert_element_type x0 -> x4, other arithmetic: none -> 8.08 us  [per_device(): total.astype(jnp.float32)]
    concatenate x1 -> x0, other arithmetic: 6.1 us -> none  [per_device(): jnp.concatenate([contract_rows(normed_low, grad_q).astype(jnp.bfloat16),...]
  transfers between devices with their start and end apart: 1 -> 0, of which waited for: 0 -> 0; matrix products, arithmetic and copies ran while one was open for 8% -> 0% of each run, Pallas kernels for 34% -> 0%
where the time goes in v4:
time: 420 us; the launch traced here: 415 us
  Pallas kernels  316 us (75%)
  matrix products  64.7 us (15%)
  other arithmetic  23.2 us (6%)
  local copies, waits for them, and re-layouts  6.04 us (1%)
  between operations  4.74 us (1%)
    pallas_call x1, Pallas kernels, backward_part(): pl.pallas_call(functools.partial(backward_kernel, n_ctx, widths), out_sha...  212 us
    pallas_call x1, Pallas kernels, forward_part(): pl.pallas_call(functools.partial(forward_kernel, n_ctx), out_shape=[shape...  105 us
    dot_general x6, matrix products, dot_dims(): lax.dot_general(left_side, right_side, (((left_dim,), (right_dim,)), ((),...  44.9 us
    dot_general x1, matrix products, per_device(): jnp.dot(active_low, full_down, preferred_element_type=jnp.float32)  11.7 us

profile of v4, /device:TPU:0, one launch (start us, length us, event | category | flops | bytes accessed | tf_op | source)
XLA Modules:
  0.0 415.1 jit_solution(1612492537772110315)
XLA Ops:
  0.6 1.3 fusion.29
  5.2 0.6 pad_add_fusion.refs_0_
  5.8 1.5 fusion.27
  7.3 104.8 %gather_attend.1 = (bf16[1536,1024]{1,0:T(8,128)(2,1)}, bf16[512,1024]{1,0:T(8,128)(2,1)}, bf16[1536,2048]{1,0:T(8,128)(2,1)}, bf16[512,1024]{1,0:T(8,128)(2,1)}...) custom-call(s32[2]{0:T(128)} %pad_add_fusion.refs_0_, ...), custom_call_target="tpu_custom_call" | custom-call | flops 21474836480 | bytes 67108864 | tf_op jit(solution)/shard_map/gather_attend/pallas_call | solution.py:526
  112.1 3.4 fusion.30
  115.5 0.3 multiply_reduce_fusion.6
  115.9 0.8 copy-done.8
  116.7 0.7 fusion.25
  117.5 0.3 multiply_reduce_fusion.5
  118.0 4.7 %fusion.19 = f32[512,4096]{1,0:T(8,128)S(1)} fusion(bf16[1024,4096]{1,0:T(8,128)(2,1)S(1)} %bitcast.81, f32[512,1024]{1,0:T(8,128)S(1)} %get-tuple-element.54, f32[1024]{0:T(1024)S(1)} %bitcast.73, f32[1024]{0:T(1024)S(1)} %bitcast.68, f32[512]{0:T(512)S(1)} %fusion.16, f32[512]{0:T(512)S(1)} %broadcast_multiply_fusion.1), kind=kOutput, calls=%fused_computation.57 | convolution fusion | flops 4297588736 | bytes 18886656 | tf_op jit(solution)/shard_map/dot_general | solution.py:1145
  122.7 11.7 %fusion.31 = (f32[512]{0:T(512)S(1)}, f32[512,1024]{1,0:T(8,128)S(1)}) fusion(bf16[4096,1024]{1,0:T(8,128)(2,1)} %get-tuple-element.26, f32[512,4096]{1,0:T(8,128)S(1)} %fusion.19), kind=kOutput, calls=%fused_computation.68 | convolution fusion | flops 4314365440 | bytes 18876416 | tf_op jit(solution)/shard_map/dot_general | solution.py:1148
  134.4 0.3 multiply_reduce_fusion.4
  134.8 0.9 copy-done.2
  135.6 0.9 fusion.13
  136.7 2.0 fusion.24
  138.7 13.4 %fusion.6 = bf16[512,4096]{1,0:T(8,128)(2,1)} fusion(f32[512,4096]{1,0:T(8,128)S(1)} %fusion.19, bf16[4096,1024]{1,0:T(8,128)(2,1)} %get-tuple-element.26, f32[512,1024]{1,0:T(8,128)S(1)} %get-tuple-element.52, f32[512]{0:T(512)S(1)} %negate_multiply_fusion.2), kind=kOutput, calls=%fused_computation.8 | convolution fusion | flops 4337958912 | bytes 23070720 | tf_op jit(solution)/shard_map/dot_general | solution.py:38
  152.0 8.7 %multiply_reduce_fusion.1 = (f32[1024]{0:T(1024)S(1)}, f32[512]{0:T(512)S(1)}, f32[1024]{0:T(1024)S(1)}, f32[512,1024]{1,0:T(8,128)S(1)}) fusion(f32[512,1024]{1,0:T(8,128)S(1)} %get-tuple-element.54, f32[512]{0:T(512)S(1)} %fusion.16, f32[512]{0:T(512)S(1)} %broadcast_multiply_fusion.1, f32[1024]{0:T(1024)S(1)} %bitcast.69, bf16[512,4096]{1,0:T(8,128)(2,1)} %fusion.6, ...), kind=kOutput, calls=%fused_computation.27 | convolution fusion | flops 4299159040 | bytes 16795648 | tf_op jit(solution)/shard_map/dot_general | solution.py:38
  160.8 0.7 fusion.23
  161.5 2.3 multiply_reduce_fusion
  164.0 0.7 stack.21.refs_2_
  164.7 2.4 fusion.21
  167.1 2.3 convolution_convert_fusion.3.refs_8_
  169.4 10.6 %convolution_convert_fusion.1 = bf16[4096,1024]{1,0:T(8,128)(2,1)} fusion(f32[512,1024]{1,0:T(8,128)S(1)} %copy-done.6, f32[512]{0:T(512)S(1)} %negate_multiply_fusion.2, f32[512,4096]{1,0:T(8,128)} %copy-done.13), kind=kOutput, calls=%fused_computation.11 | convolution fusion | flops 4319084544 | bytes 18876416 | tf_op jit(solution)/shard_map/dot_general | solution.py:38
  180.1 7.3 %convolution_convert_fusion = bf16[1024,4096]{1,0:T(8,128)(2,1)} fusion(bf16[512,4096]{1,0:T(8,128)(2,1)S(1)} %copy-done.14, f32[512,1024]{1,0:T(8,128)S(1)} %copy-done.1, f32[1024]{0:T(1024)S(1)} %bitcast.74, f32[1024]{0:T(1024)S(1)} %bitcast.71, f32[512]{0:T(512)S(1)} %fusion.16, f32[512]{0:T(512)S(1)} %broadcast_multiply_fusion.1), kind=kOutput, calls=%fused_computation.10 | convolution fusion | flops 4301783040 | bytes 14692352 | tf_op jit(solution)/shard_map/dot_general | solution.py:38
  187.3 2.7 convolution_convert_fusion.2
  190.0 211.6 %attend_back_reduce.1 = (bf16[1024,1024]{1,0:T(8,128)(2,1)}, bf16[256,4096]{1,0:T(8,128)(2,1)}, bf16[256,1024]{1,0:T(8,128)(2,1)}, bf16[256,3072]{1,0:T(8,128)(2...) custom-call(s32[1]{0:T(128)} %bitcast.2.refs_0_, f32[1,1024]{1,0:T(1,128)} %get-tuple-element.60.refs_1_, ...), custom_call_target="tpu_custom_call" | custom-call | flops 42949672960 | bytes 67108864 | tf_op jit(solution)/shard_map/attend_back_reduce/pallas_call | solution.py:1066
  401.6 4.2 %add_bitcast_fusion = f32[1,1,512,1024]{3,2,1,0:T(8,128)} fusion(f32[512,1024]{1,0:T(8,128)} %get-tuple-element.48, f32[512,1024]{1,0:T(8,128)} %get-tuple-element.32), kind=kLoop, calls=%fused_computation.24 | loop fusion | flops 524288 | bytes 6291456 | tf_op jit(solution)/shard_map/reshape | solution.py:1184
  405.9 2.0 convert_element_type.64
  407.9 1.1 convert_element_type.65
  409.0 2.5 convert_element_type.66
  411.5 2.5 convert_element_type.67
  414.0 0.6 fusion.26
  (47 shorter events, 0.5 us)
Async XLA Ops:
  112.1 5.7 %slice-start = ((s8[8388608]{0:T(1024)(128)(4,1)}), s8[4194304]{0:T(1024)(128)(4,1)S(1)}, s32[]{:S(2)}) async-start(s8[8388608]{0:T(1024)(128)(4,1)} %bitcast.80), calls=%async_computation | async-start | bytes 8388608
  115.5 1.2 copy-start.8
  115.5 2.5 slice-start.1
  117.4 43.4 %copy-start = (f32[512,1024]{1,0:T(8,128)}, f32[512,1024]{1,0:T(8,128)S(1)}, u32[]{:S(2)}) copy-start(f32[512,1024]{1,0:T(8,128)S(1)} %get-tuple-element.54) | copy-start | bytes 6291460
  122.7 16.0 %copy-start.13 = (f32[512,4096]{1,0:T(8,128)}, f32[512,4096]{1,0:T(8,128)S(1)}, u32[]{:S(2)}) copy-start(f32[512,4096]{1,0:T(8,128)S(1)} %fusion.19) | copy-start | bytes 25165828
  134.4 1.2 copy-start.2
  138.7 13.4 %copy-start.5 = (f32[512,1024]{1,0:T(8,128)}, f32[512,1024]{1,0:T(8,128)S(1)}, u32[]{:S(2)}) copy-start(f32[512,1024]{1,0:T(8,128)S(1)} %get-tuple-element.52) | copy-start | bytes 6291460
  164.7 2.4 copy-start.11
  167.1 2.3 copy-start.6
  169.4 10.6 %copy-start.1 = (f32[512,1024]{1,0:T(8,128)S(1)}, f32[512,1024]{1,0:T(8,128)}, u32[]{:S(2)}) copy-start(f32[512,1024]{1,0:T(8,128)} %copy-done) | copy-start | bytes 6291460
  169.4 10.6 %copy-start.14 = (bf16[512,4096]{1,0:T(8,128)(2,1)S(1)}, bf16[512,4096]{1,0:T(8,128)(2,1)}, u32[]{:S(2)}) copy-start(bf16[512,4096]{1,0:T(8,128)(2,1)} %fusion.6) | copy-start | bytes 12582916
  180.0 7.3 %copy-start.12 = (bf16[512,1024]{1,0:T(8,128)(2,1)S(1)}, bf16[512,1024]{1,0:T(8,128)(2,1)}, u32[]{:S(2)}) copy-start(bf16[512,1024]{1,0:T(8,128)(2,1)} %get-tuple-element.23.refs_7_) | copy-start | bytes 3145732
  401.6 4.2 %copy-start.7 = (bf16[256,3072]{1,0:T(8,128)(2,1)S(1)}, bf16[256,3072]{1,0:T(8,128)(2,1)}, u32[]{:S(2)}) copy-start(bf16[256,3072]{1,0:T(8,128)(2,1)} %get-tuple-element.33) | copy-start | bytes 4718596
  405.9 2.0 copy-start.9
  405.9 3.1 copy-start.4
  409.0 2.5 copy-start.3
  411.5 2.5 copy-start.10

commit v5 on v4

--- a/solution.py
+++ b/solution.py
@@ -66,6 +66,10 @@
 SPAN = 512
 CHAIN = 64
 HOP = 2
+YLAG = 2
+XLAG = 2
+BLAG = 2
+PACE = 2
 LAG = 2
 GROUP = 4
 AHEAD = 4
@@ -627,11 +631,13 @@
 def backward_kernel(n_ctx, widths, *refs):
     slots = n_ctx // 2
     levels = n_ctx.bit_length() - 1
-    depth = 8 + levels if levels < 3 else 6 + levels
+    depth = 14 if n_ctx == 4 else 10
     (slot_ref, gain_ref, norm_ref, x_hbm, q_hbm, kv_hbm, a_hbm, o_hbm, do_hbm, lse_hbm, w_hbm) = refs[:11]
-    terms, outs = list(refs[11:14]), refs[14:18]
-    grad_out, norm_out = refs[18:20]
-    scratch = list(refs[20:])
+    fresh = slots <= 2
+    given = 5 if fresh else 3
+    terms, outs = list(refs[11 : 11 + given]), refs[11 + given : 15 + given]
+    grad_out, norm_out = refs[15 + given : 17 + given]
+    scratch = list(refs[17 + given :])
 
     def take(count):
         taken = scratch[:count]
@@ -639,14 +645,13 @@
         return taken
 
     q_v, o_v, do_v, lse_v, weight, kv_b, a_b, dq_acc, turned, gkv, term, own_part, left, right, norm_v, norm_in = take(16)
-    r1, r2, r3, fin, local = take(5)
+    r1, r2, r3, fin, made = take(5)
+    lhs, rhs = take(2) if fresh else (None, None)
     zbufs = take(levels)
-    sem_in, sem_blk, sem_local, sem_out, sem_res = take(5)
+    sem_in, sem_blk, sem_rhs, sem_lhs, sem_out, sem_res = take(6)
     send1, recv1, send2, recv2, send3, recv3, send6, recv6 = take(8)
     rs_send, rs_recv, ag_send, ag_recv = take(levels), take(levels), take(levels), take(levels)
     left_s, left_r, right_s, right_r, norm_s, norm_r = take(6)
-    terms.append(term)
-
     grp, ctx, wsh = lax.axis_index("grp"), lax.axis_index("ctx"), lax.axis_index("wsh")
     side, core = wsh // 2, wsh % 2
     core_peer = (grp, ctx, side * 2 + 1 - core)
@@ -715,18 +720,79 @@
         row, rows, col, cols = region(level, flip)
         return aligned(base + row, rows), aligned(col, cols)
 
-    def step_load(index):
+    last_low = ranges[-1][0]
+    if fresh:
+        set_of = [(0, number) for number in range(widths[0][0] // TILE)] + [(1, 0), (2, 0)]
+        set_first = [number * ranges[0][2] for number in range(widths[0][0] // TILE)]
+        set_first += [ranges[1][0], ranges[2][0]]
+        g_hbm, dz_hbm, f_hbm, du_hbm, datt_hbm = terms
+        left_of, right_of = (g_hbm, f_hbm, o_hbm), (dz_hbm, du_hbm, datt_hbm)
+
+        def set_copies(number):
+            place, group = set_of[number]
+            stride = left_of[place].shape[1] // 4
+            return [
+                pltpu.make_async_copy(
+                    left_of[place].at[:, pl.ds(owner * stride + group * TILE, TILE)],
+                    lhs.at[number % 2, owner],
+                    sem_lhs.at[number % 2, owner],
+                )
+                for owner in range(4)
+            ]
+
+    def step_fetch(index):
+        near = lax.rem(index, 4)
+
+        def act(place, span):
+            if place == 3:
+                return
+            if fresh:
+                pltpu.make_async_copy(
+                    right_of[place].at[:, span[1]], rhs.at[near], sem_rhs.at[near]
+                ).start()
+            else:
+                pltpu.make_async_copy(
+                    terms[place].at[:, :, span[0], span[1]], made.at[near], sem_rhs.at[near]
+                ).start()
+
+        by_range(index, act)
+
+    def step_make(index):
         slot = lax.rem(index, depth)
         near = lax.rem(index, 4)
 
-        def act(place, span):
-            source = terms[place]
-            pltpu.make_async_copy(source.at[:, core, span[0], span[1]], local.at[near], sem_local.at[near]).start()
-            remote(
-                source.at[:, 1 - core, span[0], span[1]], r1.at[slot], send1.at[slot], recv1.at[slot], core_peer
-            ).start()
-
-        by_range(index, act)
+        @pl.when(index < last_low)
+        def _():
+            if fresh:
+                local_wait(rhs.at[near], sem_rhs.at[near])
+                parity = jnp.int32(0)
+                for number, low in enumerate(set_first):
+                    parity = jnp.where(index >= low, number % 2, parity)
+
+                    @pl.when(index == low)
+                    def _(number=number):
+                        for copy in set_copies(number):
+                            copy.wait()
+                        if number + 1 < len(set_first):
+                            for copy in set_copies(number + 1):
+                                copy.start()
+
+                right_side = rhs[near]
+                for owner in range(4):
+                    made[near, owner // 2, owner % 2] = dot_dims(
+                        lhs[parity, owner], right_side, 0, 0
+                    ).astype(jnp.bfloat16)
+            else:
+                local_wait(made.at[near], sem_rhs.at[near])
+
+        @pl.when(index >= last_low)
+        def _():
+            span = aligned((index - last_low) * TILE, TILE)
+            made[near] = term[:, :, :, span]
+
+        remote(
+            made.at[near, :, 1 - core], r1.at[slot], send1.at[slot], recv1.at[slot], core_peer
+        ).start()
 
     def finished(move):
         move.wait_send()
@@ -734,9 +800,8 @@
 
     def step_core(index):
         slot, near = lax.rem(index, depth), lax.rem(index, 4)
-        local_wait(local.at[near], sem_local.at[near])
         finished(remote(r1.at[slot], r1.at[slot], send1.at[slot], recv1.at[slot], core_peer))
-        r1[slot] = r1[slot] + local[near]
+        r1[slot] = r1[slot] + made[near, :, core]
         remote(r1.at[slot, 1 - side], r2.at[slot], send2.at[slot], recv2.at[slot], side_peer).start()
 
     keep_half = aligned(grp * half, half)
@@ -748,6 +813,75 @@
         r2[slot] = r2[slot] + r1[slot, side]
         remote(r2.at[slot, give_half], r3.at[slot], send3.at[slot], recv3.at[slot], grp_peer).start()
 
+    fold = n_ctx == 4
+    if fold:
+        outer = bits[0] == bits[1]
+        inner = bits[0] != bits[1]
+        mate, middle = level_peers[0], (grp, 3 - ctx, wsh)
+        quarter = half // 2
+        mine, other = aligned(bits[1] * quarter, quarter), aligned((1 - bits[1]) * quarter, quarter)
+        fin_mine = aligned(grp * half + bits[1] * quarter, quarter)
+        fin_other = aligned(grp * half + (1 - bits[1]) * quarter, quarter)
+
+        def up_copy(slot):
+            return remote(r3.at[slot], zbufs[0].at[slot], rs_send[0].at[slot], rs_recv[0].at[slot], mate)
+
+        def cross_copy(slot):
+            return remote(
+                r3.at[slot, other], zbufs[1].at[slot], rs_send[1].at[slot], rs_recv[1].at[slot], middle
+            )
+
+        def share_copy(slot, rows):
+            here = fin.at[slot, rows]
+            return remote(here, here, ag_send[1].at[slot], ag_recv[1].at[slot], middle)
+
+        def down_copy(slot):
+            here = fin.at[slot, keep_half]
+            return remote(here, here, ag_send[0].at[slot], ag_recv[0].at[slot], mate)
+
+        def step_up(index):
+            slot = lax.rem(index, depth)
+
+            @pl.when(outer)
+            def _():
+                up_copy(slot).wait_send()
+
+            @pl.when(inner)
+            def _():
+                up_copy(slot).wait_recv()
+                r3[slot] = r3[slot] + zbufs[0][slot]
+                cross_copy(slot).start()
+
+        def step_cross(index):
+            slot = lax.rem(index, depth)
+
+            @pl.when(inner)
+            def _():
+                finished(cross_copy(slot))
+                fin[slot, fin_mine] = r3[slot, mine] + zbufs[1][slot]
+                share_copy(slot, fin_mine).start()
+
+        def step_share(index):
+            slot = lax.rem(index, depth)
+
+            @pl.when(inner)
+            def _():
+                finished(share_copy(slot, fin_other))
+                down_copy(slot).start()
+
+        def step_down(index):
+            slot = lax.rem(index, depth)
+
+            @pl.when(inner)
+            def _():
+                down_copy(slot).wait_send()
+
+            @pl.when(outer)
+            def _():
+                down_copy(slot).wait_recv()
+
+            back_copy(slot, keep_half).start()
+
     def rs_copy(level, slot):
         rows, cols = spot(level + 1, True)
         return remote(
@@ -767,7 +901,13 @@
         slot = lax.rem(index, depth)
         finished(remote(r2.at[slot, give_half], r3.at[slot], send3.at[slot], recv3.at[slot], grp_peer))
         r3[slot] = r3[slot] + r2[slot, keep_half]
-        rs_copy(0, slot).start()
+        if fold:
+
+            @pl.when(outer)
+            def _():
+                up_copy(slot).start()
+        else:
+            rs_copy(0, slot).start()
 
     def step_scatter(level):
         def act(index):
@@ -809,23 +949,18 @@
 
         by_range(index, act)
 
-    stages = [(0, step_core), (2, step_side), (4, step_grp)]
-    stages += [(5 + level, step_scatter(level)) for level in range(levels)]
-    stages += [(5 + 2 * levels - 1 - level, step_gather(level)) for level in reversed(range(levels))]
-    stages += [(6 + 2 * levels, step_out), (8 + 2 * levels, out_wait)]
+    z_lag = 2 if fold else 1
+    order = [(YLAG, step_side), (XLAG, step_grp)]
+    if fold:
+        order += [(z_lag, act) for act in (step_up, step_cross, step_share, step_down)]
+    else:
+        order += [(z_lag, step_scatter(level)) for level in range(levels)]
+        order += [(z_lag, step_gather(level)) for level in reversed(range(levels))]
+    order += [(BLAG, step_out), (2, out_wait)]
+    stages = [(0, step_core)]
+    for lag, act in order:
+        stages.append((stages[-1][0] + lag, act))
     all_ticks = chunks + stages[-1][0]
-
-    def tick(step):
-        @pl.when(step + 2 < chunks)
-        def _():
-            step_load(step + 2)
-
-        for lag, act in stages:
-            index = step - lag
-
-            @pl.when((index >= 0) & (index < chunks))
-            def _(act=act, index=index):
-                act(index)
 
     per_slot = BLK // CHAIN
     chain_chunks = slots * per_slot
@@ -849,39 +984,60 @@
             remote(here, here, send.at[number], recv.at[number], target).start()
 
     def chain_tick(step):
-        number = step - HOP * ctx
+        number = step - ctx
 
         @pl.when((number >= 0) & (number < chain_chunks))
         def _():
             chain_step(left, left_s, left_r, number, ctx == 0, ctx == n_ctx - 1, next_ctx)
 
-        back = step - HOP * (n_ctx - 1 - ctx)
+        back = step - (n_ctx - 1 - ctx)
 
         @pl.when((back >= 0) & (back < chain_chunks))
         def _():
             chain_step(right, right_s, right_r, back, ctx == n_ctx - 1, ctx == 0, last_ctx)
 
-    chain_ticks = chain_chunks + HOP * (n_ctx - 1)
-
-    step_load(0)
-    step_load(1)
+    groups = PAIRS // PAIRED
+    block_ticks = 2 * groups + 2
+    chain_ticks = block_ticks + PACE * (chain_chunks + n_ctx - 1)
+
+    def tick(step):
+        @pl.when(step + 3 < chunks)
+        def _():
+            step_fetch(step + 3)
+
+        @pl.when(step + 2 < chunks)
+        def _():
+            step_make(step + 2)
+
+        for lag, act in stages:
+            index = step - lag
+
+            @pl.when((index >= 0) & (index < chunks))
+            def _(act=act, index=index):
+                act(index)
+
+        beat = step - block_ticks
+
+        @pl.when((beat >= 0) & (beat % PACE == 0))
+        def _():
+            chain_tick(beat // PACE)
+
+
+    for index in range(3):
+        step_fetch(jnp.int32(index))
+    if fresh:
+        for copy in set_copies(0):
+            copy.start()
+    for index in range(2):
+        step_make(jnp.int32(index))
     dq_acc[...] = jnp.zeros_like(dq_acc)
     for load in loads:
         load.wait()
 
-    groups = PAIRS // PAIRED
-
-    def attend(kv_ref, own, visible, begin, chained, chain_from):
+    def attend(kv_ref, own, visible, begin):
         def body(group, carry):
             for extra in range(2):
                 tick(begin + 2 * group + extra)
-            if chained is not None:
-
-                @pl.when(chained)
-                def _():
-                    for extra in range(2):
-                        chain_tick(chain_from + 2 * group + extra)
-
             for member in range(PAIRED):
                 grad_block(
                     q_v, do_v, o_v, lse_v, kv_ref, dq_acc, turned, group * PAIRED + member, own, visible
@@ -889,8 +1045,6 @@
             return carry
 
         lax.fori_loop(0, groups, body, 0)
-
-    block_ticks = 2 * groups + 2
 
     def each_slot(slot, carry):
         visible = slot < slot_ref[0]
@@ -902,22 +1056,28 @@
             for copy in block_copies(index + 1):
                 copy.start()
         begin = slot * block_ticks
-        attend(kv_b.at[place], False, visible, begin, slot > 0, (slot - 1) * per_slot)
+        attend(kv_b.at[place], False, visible, begin)
 
         def weight_terms(step, inner):
             tick(begin + 2 * groups + step)
             rows = aligned(step * 512, 512)
             for part in range(2):
                 cols = pl.ds(part * D, D)
-                fresh = dot_dims(a_b[place, :, rows], turned[cols, :], 0, 1)
-
-                @pl.when(slot == 0)
-                def _(fresh=fresh, cols=cols):
-                    gkv[rows, cols] = fresh.astype(gkv.dtype)
-
-                @pl.when(slot > 0)
-                def _(fresh=fresh, cols=cols):
-                    gkv[rows, cols] = (gkv[rows, cols] + fresh).astype(gkv.dtype)
+                product = dot_dims(a_b[place, :, rows], turned[cols, :], 0, 1)
+                for down in range(2):
+                    if fresh:
+                        target = gkv.at[aligned(step * 512 + down * TILE, TILE), cols]
+                    else:
+                        target = term.at[step, down, :, pl.ds((part + 1) * D, D)]
+                    piece = product[down * TILE : (down + 1) * TILE]
+
+                    @pl.when(slot == 0)
+                    def _(target=target, piece=piece):
+                        target[...] = piece.astype(target.dtype)
+
+                    @pl.when(slot > 0)
+                    def _(target=target, piece=piece):
+                        target[...] = (target[...] + piece).astype(target.dtype)
 
             own_part[slot, :, rows] = dot_dims(
                 turned[...], weight[rows, pl.ds(D, 2 * D)], 0, 1
@@ -935,7 +1095,7 @@
     own_place = (slots + 1) % kv_b.shape[0]
     for copy in block_copies(slots + 1):
         copy.wait()
-    attend(kv_b.at[own_place], True, None, begin, slots > 0, (slots - 1) * per_slot)
+    attend(kv_b.at[own_place], True, None, begin)
     dq_low = o_v
     dq_low[...] = (dq_acc[...] * ALPHA).astype(jnp.bfloat16) * jnp.bfloat16(QSCALE)
     x_load = pltpu.make_async_copy(x_hbm, do_v, sem_in.at[0])
@@ -949,9 +1109,9 @@
         term[up, down, :, pl.ds(0, D)] = dot_dims(a_rows, dq_low[...], 0, 0).astype(jnp.bfloat16)
         for part in range(2):
             cols = pl.ds(part * D, D)
-            term[up, down, :, pl.ds((part + 1) * D, D)] = (
-                gkv[rows, cols] + dot_dims(a_rows, turned[cols, :], 0, 1)
-            ).astype(jnp.bfloat16)
+            target = term.at[up, down, :, pl.ds((part + 1) * D, D)]
+            earlier = gkv[rows, cols] if fresh else target[...]
+            target[...] = (earlier + dot_dims(a_rows, turned[cols, :], 0, 1)).astype(jnp.bfloat16)
         return carry
 
     lax.fori_loop(0, 4, last_terms, 0)
@@ -961,7 +1121,6 @@
 
     def own_grad(step, carry):
         tick(ready + step)
-        chain_tick(chain_chunks + step)
         rows = aligned(step * TILE, TILE)
         da_acc[:, rows] = dot_dims(dq_low[...], weight[rows, pl.ds(0, D)], 1, 1) + dot_dims(
             turned[...], weight[rows, pl.ds(D, 2 * D)], 0, 1
@@ -973,10 +1132,9 @@
 
     def flush_chain(step, carry):
         tick(ready + step)
-        chain_tick(chain_chunks + 4 + step)
         return carry
 
-    left_over = max(0, chain_ticks - chain_chunks - 4)
+    left_over = max(0, chain_ticks - ready)
     lax.fori_loop(0, left_over, flush_chain, 0)
     ready = ready + left_over
     x_load.wait()
@@ -1046,12 +1204,22 @@
     norm_result.wait()
 
 
-def backward_part(n_ctx, slot_vec, gain, norms, raw, q, kv, a, o, do, lse, weight, terms):
+def backward_part(n_ctx, slot_vec, gain, norms, raw, q, kv, a, o, do, lse, weight, pieces):
     slots = n_ctx // 2
     levels = n_ctx.bit_length() - 1
-    depth = 8 + levels if levels < 3 else 6 + levels
+    depth = 14 if n_ctx == 4 else 10
     every = (slots + 1) * BLK
-    widths = [(term.shape[0] // 4, term.shape[1]) for term in terms] + [(D // 4, 3 * D)]
+    if slots > 2:
+        active, dz, ffn, du, datt = pieces
+        terms = [
+            contract_rows(left_side, right_side).astype(jnp.bfloat16)
+            for left_side, right_side in ((active, dz), (ffn, du), (o, datt))
+        ]
+        widths = [(term.shape[0] // 4, term.shape[1]) for term in terms]
+        pieces = [term.reshape(2, 2, width[0], width[1]) for term, width in zip(terms, widths)]
+    else:
+        widths = [(pieces[0].shape[1] // 4, D), (D // 4, pieces[3].shape[1]), (D // 4, D)]
+    widths = widths + [(D // 4, 3 * D)]
     low, full = jnp.bfloat16, jnp.float32
     dma = pltpu.SemaphoreType.DMA
     hbm = pl.BlockSpec(memory_space=pl.ANY)
@@ -1060,13 +1228,15 @@
     buffers = 2 if slots <= 2 else 1
     chain = slots * (BLK // CHAIN)
     zshapes, rows, cols = [], TILE // 2, TILE
-    for _ in range(levels):
+    if n_ctx == 4:
+        zshapes = [pltpu.VMEM((depth, rows, cols), low), pltpu.VMEM((depth, rows // 2, cols), low)]
+    for _ in range(0 if zshapes else levels):
         rows, cols = (rows // 2, cols) if rows > 16 else (rows, cols // 2)
         zshapes.append(pltpu.VMEM((depth, rows, cols), low))
     return pl.pallas_call(
         functools.partial(backward_kernel, n_ctx, widths),
         out_shape=[shape(width, low) for width in widths] + [shape((BLK, D), full), shape((8, D), full)],
-        in_specs=[pl.BlockSpec(memory_space=pltpu.SMEM), vmem, vmem] + [hbm] * 11,
+        in_specs=[pl.BlockSpec(memory_space=pltpu.SMEM), vmem, vmem] + [hbm] * (8 + len(pieces)),
         out_specs=[hbm] * 6,
         scratch_shapes=[
             pltpu.VMEM((BLK, D), low),
@@ -1078,7 +1248,7 @@
             pltpu.VMEM((buffers, BLK, D), low),
             pltpu.VMEM((BLK, D), full),
             pltpu.VMEM((2 * D, BLK), low),
-            pltpu.VMEM((D, 2 * D), full if slots <= 2 else low),
+            pltpu.VMEM((D, 2 * D) if slots <= 2 else (8, 128), full),
             pltpu.VMEM((2, 2, D // 4, 3 * D), low),
             pltpu.VMEM((slots, BLK, D), low),
             pltpu.VMEM((slots, BLK, D), low),
@@ -1089,10 +1259,11 @@
             pltpu.VMEM((depth, TILE, TILE), low),
             pltpu.VMEM((depth, TILE // 2, TILE), low),
             pltpu.VMEM((depth, TILE, TILE), low),
-            pltpu.VMEM((4, 2, TILE, TILE), low),
+            pltpu.VMEM((4, 2, 2, TILE, TILE), low),
         ]
+        + ([pltpu.VMEM((2, 4, BLK, TILE), low), pltpu.VMEM((4, BLK, TILE), low)] if slots <= 2 else [])
         + zshapes
-        + [dma((5,)), dma((2, buffers)), dma((4,)), dma((depth,)), dma((2,))]
+        + [dma((5,)), dma((2, buffers)), dma((4,)), dma((2, 4)), dma((depth,)), dma((2,))]
         + [dma((depth,))] * (8 + 4 * levels)
         + [dma((chain,))] * 4
         + [dma((3 + levels,))] * 2,
@@ -1113,7 +1284,7 @@
         do,
         lse,
         weight,
-        *[term.reshape(2, 2, width[0], width[1]) for term, width in zip(terms, widths)],
+        *pieces,
     )
 
 
@@ -1151,15 +1322,12 @@
     seed_grad = out_grad.reshape(BLK, D).astype(jnp.float32)
     grad_down_in, gain_grad3, bias_grad3 = post_back(seed_grad)
     down_low = grad_down_in.astype(jnp.bfloat16)
-    term_down = contract_rows(active_low, down_low).astype(jnp.bfloat16)
     grad_active = contract_last(down_low, full_down)
     up_low = gelu_back(grad_active)[0].astype(jnp.bfloat16)
-    term_up = contract_rows(ffn_low, up_low).astype(jnp.bfloat16)
     grad_pre_ffn, gain_grad2, bias_grad2 = ffn_back(contract_last(up_low, full_up))
     grad_hidden = seed_grad + grad_pre_ffn
     grad_branch, gain_grad1, bias_grad1 = attn_back(grad_hidden)
     branch_low = grad_branch.astype(jnp.bfloat16)
-    term_out = contract_rows(attn_low, branch_low).astype(jnp.bfloat16)
     grad_out_low = contract_last(branch_low, full_out).astype(jnp.bfloat16)
 
     zero_row = jnp.zeros((D,), jnp.float32)
@@ -1179,7 +1347,7 @@
         grad_out_low,
         lse,
         full_qkv,
-        [term_down, term_up, term_out],
+        [active_low, down_low, ffn_low, up_low, branch_low],
     )
     grad_input = (grad_hidden + grad_tokens).reshape(1, 1, BLK, D)
     summed_down, summed_up, summed_out, summed_qkv = (

time: 420 us -> 366 us (0.87)
  Pallas kernels: 316 us -> 280 us
  matrix products: 64.7 us -> 43.6 us
    pallas_call x1, Pallas kernels: 212 us -> 176 us  [backward_part(): pl.pallas_call(functools.partial(backward_kernel, n_ctx, widths), out_sha...]
    dot_general x6 -> x3, matrix products: 44.9 us -> 24.5 us  [dot_dims(): lax.dot_general(left_side, right_side, (((left_dim,), (right_dim,)), ((),...]
    dot_general x1, matrix products: 11.7 us -> 6.59 us  [per_device(): jnp.dot(active_low, full_down, preferred_element_type=jnp.float32)]
    dot_general x1, matrix products: 4.68 us -> 9.15 us  [per_device(): upward = jnp.dot(ffn_low, full_up, preferred_element_type=jnp.float32)]
where the time goes in v5:
time: 366 us; the launch traced here: 361 us
  Pallas kernels  280 us (77%)
  matrix products  43.6 us (12%)
  other arithmetic  23.8 us (7%)
  local copies, waits for them, and re-layouts  8.87 us (2%)
  between operations  4.31 us (1%)
    pallas_call x1, Pallas kernels, backward_part(): pl.pallas_call(functools.partial(backward_kernel, n_ctx, widths), out_sha...  176 us
    pallas_call x1, Pallas kernels, forward_part(): pl.pallas_call(functools.partial(forward_kernel, n_ctx), out_shape=[shape...  104 us
    dot_general x3, matrix products, dot_dims(): lax.dot_general(left_side, right_side, (((left_dim,), (right_dim,)), ((),...  24.5 us
    dot_general x1, matrix products, per_device(): upward = jnp.dot(ffn_low, full_up, preferred_element_type=jnp.float32)  9.15 us
    convert_element_type x4, other arithmetic, per_device(): total.astype(jnp.float32)  8.08 us

profile of v5, /device:TPU:0, one launch (start us, length us, event | category | flops | bytes accessed | tf_op | source)
XLA Modules:
  0.0 360.9 jit_solution(17295561759157102776)
XLA Ops:
  0.6 1.5 fusion.24
  2.1 1.3 fusion.26
  6.7 0.6 pad_add_fusion.refs_0_
  7.3 104.4 %gather_attend.1 = (bf16[1536,1024]{1,0:T(8,128)(2,1)}, bf16[512,1024]{1,0:T(8,128)(2,1)}, bf16[1536,2048]{1,0:T(8,128)(2,1)}, bf16[512,1024]{1,0:T(8,128)(2,1)}...) custom-call(s32[2]{0:T(128)} %pad_add_fusion.refs_0_, ...), custom_call_target="tpu_custom_call" | custom-call | flops 21474836480 | bytes 67108864 | tf_op jit(solution)/shard_map/gather_attend/pallas_call | solution.py:530
  111.7 3.4 fusion.27
  115.4 0.9 copy-done.5
  116.3 0.7 fusion.22
  117.0 0.4 multiply_reduce_fusion.5
  117.4 0.4 add_convert_fusion.3.refs_13_
  117.8 0.7 slice-done.1
  118.5 9.2 %multiply_convert_fusion = (bf16[512,4096]{1,0:T(8,128)(2,1)}, f32[512,4096]{1,0:T(8,128)}) fusion(bf16[512,1024]{1,0:T(8,128)(2,1)S(1)} %add_convert_fusion.3.refs_13_, bf16[1024,4096]{1,0:T(8,128)(2,1)S(1)} %bitcast.75), kind=kOutput, calls=%fused_computation.9 | convolution fusion | flops 4313841664 | bytes 22020096 | tf_op jit(solution)/shard_map/dot_general | solution.py:1316
  127.7 6.6 %fusion.28 = (f32[512]{0:T(512)S(1)}, f32[512,1024]{1,0:T(8,128)S(1)}) fusion(bf16[512,4096]{1,0:T(8,128)(2,1)} %get-tuple-element.70.refs_11_, bf16[4096,1024]{1,0:T(8,128)(2,1)S(1)} %bitcast.77), kind=kOutput, calls=%fused_computation.62 | convolution fusion | flops 4295491072 | bytes 14682112 | tf_op jit(solution)/shard_map/dot_general | solution.py:1319
  134.3 0.3 multiply_reduce_fusion.4
  134.6 0.8 copy-done
  135.5 0.9 fusion.13
  136.4 2.0 fusion.21
  138.5 1.0 copy-done.6
  139.5 14.8 %fusion.6.refs_14_ = bf16[512,4096]{1,0:T(8,128)(2,1)} fusion(f32[512,4096]{1,0:T(8,128)} %get-tuple-element.71, bf16[512,1024]{1,0:T(8,128)(2,1)S(1)} %add_convert_fusion.1.refs_12_, bf16[4096,1024]{1,0:T(8,128)(2,1)} %get-tuple-element.26), kind=kOutput, calls=%fused_computation.8 | convolution fusion | flops 4336910336 | bytes 22020096 | tf_op jit(solution)/shard_map/dot_general | solution.py:38
  154.3 7.4 %multiply_reduce_fusion.1 = (f32[1024]{0:T(1024)S(1)}, f32[512]{0:T(512)S(1)}, f32[1024]{0:T(1024)S(1)}, f32[512,1024]{1,0:T(8,128)S(1)}) fusion(f32[512,1024]{1,0:T(8,128)S(1)} %get-tuple-element.54, f32[512]{0:T(512)S(1)} %fusion.16, f32[512]{0:T(512)S(1)} %broadcast_multiply_fusion.1, f32[1024]{0:T(1024)S(1)} %bitcast.63, ...), kind=kOutput, calls=%fused_computation.25 | convolution fusion | flops 4299159040 | bytes 16795648 | tf_op jit(solution)/shard_map/dot_general | solution.py:38
  161.7 0.7 fusion.20
  162.4 2.3 multiply_reduce_fusion
  165.0 0.7 stack.21.refs_2_
  165.6 2.3 fusion.18
  168.1 1.4 copy-done.10
  169.5 2.3 convolution_convert_fusion.refs_8_
  171.8 176.0 %attend_back_reduce.1 = (bf16[1024,1024]{1,0:T(8,128)(2,1)}, bf16[256,4096]{1,0:T(8,128)(2,1)}, bf16[256,1024]{1,0:T(8,128)(2,1)}, bf16[256,3072]{1,0:T(8,128)(2...) custom-call(s32[1]{0:T(128)} %bitcast.2.refs_0_, f32[1,1024]{1,0:T(1,128)} %get-tuple-element.60.refs_1_, ...), custom_call_target="tpu_custom_call" | custom-call | flops 42949672960 | bytes 67108864 | tf_op jit(solution)/shard_map/attend_back_reduce/pallas_call | solution.py:1236
  347.7 4.2 %add_bitcast_fusion = f32[1,1,512,1024]{3,2,1,0:T(8,128)} fusion(f32[512,1024]{1,0:T(8,128)} %get-tuple-element.48, f32[512,1024]{1,0:T(8,128)} %get-tuple-element.32), kind=kLoop, calls=%fused_computation.22 | loop fusion | flops 524288 | bytes 6291456 | tf_op jit(solution)/shard_map/reshape | solution.py:1352
  352.0 2.0 convert_element_type.52
  354.0 1.1 convert_element_type.53
  355.1 2.5 convert_element_type.54
  357.6 2.5 convert_element_type.55
  360.1 0.6 fusion.23
  (44 shorter events, 1.0 us)
Async XLA Ops:
  111.7 6.1 %slice-start = ((s8[8388608]{0:T(1024)(128)(4,1)}), s8[4194304]{0:T(1024)(128)(4,1)S(1)}, s32[]{:S(2)}) async-start(s8[8388608]{0:T(1024)(128)(4,1)} %bitcast.74), calls=%async_computation | async-start | bytes 8388608
  115.1 1.2 copy-start.5
  116.3 2.2 slice-start.1
  117.4 10.3 %slice-start.2 = ((s8[8388608]{0:T(1024)(128)(4,1)}), s8[4194304]{0:T(1024)(128)(4,1)S(1)}, s32[]{:S(2)}) async-start(s8[8388608]{0:T(1024)(128)(4,1)} %bitcast.76), calls=%async_computation.2 | async-start | bytes 8388608
  117.8 9.8 %copy-start.4 = (bf16[512,1024]{1,0:T(8,128)(2,1)}, bf16[512,1024]{1,0:T(8,128)(2,1)S(1)}, u32[]{:S(2)}) copy-start(bf16[512,1024]{1,0:T(8,128)(2,1)S(1)} %add_convert_fusion.3.refs_13_) | copy-start | bytes 3145732
  118.5 9.2 %slice-start.3 = ((s8[8388608]{0:T(1024)(128)(4,1)}), s8[4194304]{0:T(1024)(128)(4,1)S(1)}, s32[]{:S(2)}) async-start(s8[8388608]{0:T(1024)(128)(4,1)} %bitcast.76), calls=%async_computation.3 | async-start | bytes 8388608
  134.3 1.2 copy-start
  138.5 1.0 copy-start.6
  167.9 1.6 copy-start.10
  169.5 2.3 copy-start.7
  347.7 4.2 %copy-start.3 = (bf16[256,3072]{1,0:T(8,128)(2,1)S(1)}, bf16[256,3072]{1,0:T(8,128)(2,1)}, u32[]{:S(2)}) copy-start(bf16[256,3072]{1,0:T(8,128)(2,1)} %get-tuple-element.33) | copy-start | bytes 4718596
  352.0 2.0 copy-start.8
  352.0 3.1 copy-start.2
  355.1 2.5 copy-start.1
  357.6 2.5 copy-start.9

commit v6 on v5

--- a/solution.py
+++ b/solution.py
@@ -69,6 +69,9 @@
 YLAG = 2
 XLAG = 2
 BLAG = 2
+FF_TICKS = 13
+GELU_A = 0.044715
+GELU_C = math.sqrt(2.0 / math.pi)
 PACE = 2
 LAG = 2
 GROUP = 4
@@ -632,12 +635,12 @@
     slots = n_ctx // 2
     levels = n_ctx.bit_length() - 1
     depth = 14 if n_ctx == 4 else 10
-    (slot_ref, gain_ref, norm_ref, x_hbm, q_hbm, kv_hbm, a_hbm, o_hbm, do_hbm, lse_hbm, w_hbm) = refs[:11]
-    fresh = slots <= 2
-    given = 5 if fresh else 3
-    terms, outs = list(refs[11 : 11 + given]), refs[11 + given : 15 + given]
-    grad_out, norm_out = refs[15 + given : 17 + given]
-    scratch = list(refs[17 + given :])
+    shallow = slots <= 2
+    (slot_ref, gain_ref, norm_ref, x_hbm, q_hbm, kv_hbm, a_hbm, o_hbm, lse_hbm, w_hbm) = refs[:10]
+    (w_out, w_up, w_down, g_hbm, dz_hbm, f_hbm, u_hbm, hat1_hbm, hat2_hbm, rstd_hbm, dy_hbm) = refs[10:21]
+    outs = refs[21:25]
+    grad_out, norm_out, dh_hbm, du_hbm, datt_hbm = refs[25:30]
+    scratch = list(refs[30:])
 
     def take(count):
         taken = scratch[:count]
@@ -646,9 +649,9 @@
 
     q_v, o_v, do_v, lse_v, weight, kv_b, a_b, dq_acc, turned, gkv, term, own_part, left, right, norm_v, norm_in = take(16)
     r1, r2, r3, fin, made = take(5)
-    lhs, rhs = take(2) if fresh else (None, None)
+    lhs, rhs = take(2)
     zbufs = take(levels)
-    sem_in, sem_blk, sem_rhs, sem_lhs, sem_out, sem_res = take(6)
+    sem_in, sem_blk, sem_rhs, sem_lhs, sem_ff, sem_out, sem_res = take(7)
     send1, recv1, send2, recv2, send3, recv3, send6, recv6 = take(8)
     rs_send, rs_recv, ag_send, ag_recv = take(levels), take(levels), take(levels), take(levels)
     left_s, left_r, right_s, right_r, norm_s, norm_r = take(6)
@@ -662,15 +665,6 @@
     bits = [(ctx // (1 << level)) % 2 for level in range(levels)]
     level_peers = [(grp, ctx + (1 - 2 * bits[level]) * (1 << level), wsh) for level in range(levels)]
 
-    loads = [
-        pltpu.make_async_copy(source, dest, sem_in.at[place])
-        for place, (source, dest) in enumerate(
-            ((q_hbm, q_v), (o_hbm, o_v), (do_hbm, do_v), (lse_hbm, lse_v), (w_hbm, weight))
-        )
-    ]
-    for load in loads:
-        load.start()
-
     def block_copies(index):
         rows = aligned(lax.rem(index, slots + 1) * BLK, BLK)
         slot = lax.rem(index, kv_b.shape[0])
@@ -678,9 +672,6 @@
             pltpu.make_async_copy(kv_hbm.at[rows, :], kv_b.at[slot], sem_blk.at[0, slot]),
             pltpu.make_async_copy(a_hbm.at[rows, :], a_b.at[slot], sem_blk.at[1, slot]),
         )
-
-    for copy in block_copies(1):
-        copy.start()
 
     barrier = pltpu.get_barrier_semaphore()
     peers = [core_peer, side_peer, grp_peer, next_ctx, last_ctx] + level_peers
@@ -721,39 +712,31 @@
         return aligned(base + row, rows), aligned(col, cols)
 
     last_low = ranges[-1][0]
-    if fresh:
-        set_of = [(0, number) for number in range(widths[0][0] // TILE)] + [(1, 0), (2, 0)]
-        set_first = [number * ranges[0][2] for number in range(widths[0][0] // TILE)]
-        set_first += [ranges[1][0], ranges[2][0]]
-        g_hbm, dz_hbm, f_hbm, du_hbm, datt_hbm = terms
-        left_of, right_of = (g_hbm, f_hbm, o_hbm), (dz_hbm, du_hbm, datt_hbm)
-
-        def set_copies(number):
-            place, group = set_of[number]
-            stride = left_of[place].shape[1] // 4
-            return [
-                pltpu.make_async_copy(
-                    left_of[place].at[:, pl.ds(owner * stride + group * TILE, TILE)],
-                    lhs.at[number % 2, owner],
-                    sem_lhs.at[number % 2, owner],
-                )
-                for owner in range(4)
-            ]
+    set_of = [(0, number) for number in range(widths[0][0] // TILE)] + [(1, 0), (2, 0)]
+    set_first = [number * ranges[0][2] for number in range(widths[0][0] // TILE)]
+    set_first += [ranges[1][0], ranges[2][0]]
+    left_of, right_of = (g_hbm, f_hbm, o_hbm), (dz_hbm, du_hbm, datt_hbm)
+
+    def set_copies(number):
+        place, group = set_of[number]
+        stride = left_of[place].shape[1] // 4
+        return [
+            pltpu.make_async_copy(
+                left_of[place].at[:, pl.ds(owner * stride + group * TILE, TILE)],
+                lhs.at[number % 2, owner],
+                sem_lhs.at[number % 2, owner],
+            )
+            for owner in range(4)
+        ]
 
     def step_fetch(index):
         near = lax.rem(index, 4)
 
         def act(place, span):
-            if place == 3:
-                return
-            if fresh:
+            if place < 3:
                 pltpu.make_async_copy(
                     right_of[place].at[:, span[1]], rhs.at[near], sem_rhs.at[near]
                 ).start()
-            else:
-                pltpu.make_async_copy(
-                    terms[place].at[:, :, span[0], span[1]], made.at[near], sem_rhs.at[near]
-                ).start()
 
         by_range(index, act)
 
@@ -763,27 +746,24 @@
 
         @pl.when(index < last_low)
         def _():
-            if fresh:
-                local_wait(rhs.at[near], sem_rhs.at[near])
-                parity = jnp.int32(0)
-                for number, low in enumerate(set_first):
-                    parity = jnp.where(index >= low, number % 2, parity)
-
-                    @pl.when(index == low)
-                    def _(number=number):
-                        for copy in set_copies(number):
-                            copy.wait()
-                        if number + 1 < len(set_first):
-                            for copy in set_copies(number + 1):
-                                copy.start()
-
-                right_side = rhs[near]
-                for owner in range(4):
-                    made[near, owner // 2, owner % 2] = dot_dims(
-                        lhs[parity, owner], right_side, 0, 0
-                    ).astype(jnp.bfloat16)
-            else:
-                local_wait(made.at[near], sem_rhs.at[near])
+            local_wait(rhs.at[near], sem_rhs.at[near])
+            parity = jnp.int32(0)
+            for number, low in enumerate(set_first):
+                parity = jnp.where(index >= low, number % 2, parity)
+
+                @pl.when(index == low)
+                def _(number=number):
+                    for copy in set_copies(number):
+                        copy.wait()
+                    if number + 1 < len(set_first):
+                        for copy in set_copies(number + 1):
+                            copy.start()
+
+            right_side = rhs[near]
+            for owner in range(4):
+                made[near, owner // 2, owner % 2] = dot_dims(
+                    lhs[parity, owner], right_side, 0, 0
+                ).astype(jnp.bfloat16)
 
         @pl.when(index >= last_low)
         def _():
@@ -997,8 +977,10 @@
             chain_step(right, right_s, right_r, back, ctx == n_ctx - 1, ctx == 0, last_ctx)
 
     groups = PAIRS // PAIRED
-    block_ticks = 2 * groups + 2
-    chain_ticks = block_ticks + PACE * (chain_chunks + n_ctx - 1)
+    block_ticks = groups + 2
+    chain_first = FF_TICKS + block_ticks
+    paced = max(0, -(-(chunks - chain_first) // PACE))
+    chain_ticks = max(chunks, chain_first) + max(0, chain_chunks + n_ctx - 1 - paced)
 
     def tick(step):
         @pl.when(step + 3 < chunks)
@@ -1016,28 +998,183 @@
             def _(act=act, index=index):
                 act(index)
 
-        beat = step - block_ticks
-
-        @pl.when((beat >= 0) & (beat % PACE == 0))
+        beat = step - chain_first
+
+        @pl.when((beat >= 0) & (step < chunks) & (beat % PACE == 0))
         def _():
             chain_tick(beat // PACE)
+
+        @pl.when((beat >= 0) & (step >= chunks))
+        def _():
+            chain_tick(paced + step - max(chunks, chain_first))
 
 
     for index in range(3):
         step_fetch(jnp.int32(index))
-    if fresh:
-        for copy in set_copies(0):
-            copy.start()
+    for copy in set_copies(0):
+        copy.start()
+
+    hidden_tiles = u_hbm.shape[1] // SPAN
+    datt_v, dz_v, dy_v, hat1_v, hat2_v = own_part.at[0], do_v, left.at[1], right.at[0], right.at[1]
+
+    def tile_copies(tile, parity):
+        cols = aligned(tile * SPAN, SPAN)
+        return (
+            pltpu.make_async_copy(w_down.at[cols, :], own_part.at[parity], sem_ff.at[0, parity]),
+            pltpu.make_async_copy(
+                w_up.at[:, cols], turned.at[aligned(parity * D, D), :], sem_ff.at[1, parity]
+            ),
+            pltpu.make_async_copy(
+                u_hbm.at[:, cols], left.at[0, :, aligned(parity * SPAN, SPAN)], sem_ff.at[2, parity]
+            ),
+        )
+
+    def du_store(tile, parity):
+        return pltpu.make_async_copy(
+            kv_b.at[0, :, aligned(parity * SPAN, SPAN)],
+            du_hbm.at[:, aligned(tile * SPAN, SPAN)],
+            sem_ff.at[3, parity],
+        )
+
+    dz_load = pltpu.make_async_copy(dz_hbm, dz_v, sem_in.at[0])
+    dz_load.start()
+    for copy in tile_copies(0, 0):
+        copy.start()
+    wide_loads = [
+        pltpu.make_async_copy(source, dest, sem_in.at[place + 1])
+        for place, (source, dest) in enumerate(
+            (
+                (dy_hbm, dy_v),
+                (hat1_hbm, hat1_v),
+                (hat2_hbm, hat2_v),
+                (rstd_hbm, lse_v.at[pl.ds(0, 2)]),
+                (q_hbm, q_v),
+                (o_hbm, o_v),
+                (w_hbm, weight),
+            )
+        )
+    ]
+    out_loads = [
+        pltpu.make_async_copy(
+            w_out.at[pl.ds(place * TILE, TILE), :],
+            term.at[place // 2, place % 2, :, pl.ds(0, D)],
+            sem_in.at[8 + place],
+        )
+        for place in range(4)
+    ]
     for index in range(2):
         step_make(jnp.int32(index))
+    dz_load.wait()
+
+    def ff_tile(tile, carry):
+        start = tile + (tile + 1) // 2
+        tick(start)
+
+        @pl.when(tile % 2 == 0)
+        def _():
+            tick(start + 1)
+
+        parity = tile % 2
+        for copy in tile_copies(tile, parity):
+            copy.wait()
+
+        @pl.when(tile + 1 < hidden_tiles)
+        def _():
+            for copy in tile_copies(tile + 1, 1 - parity):
+                copy.start()
+
+        @pl.when(tile == 0)
+        def _():
+            for copy in wide_loads + out_loads:
+                copy.start()
+
+        @pl.when(tile >= 2)
+        def _():
+            du_store(tile - 2, parity).wait()
+
+        u_cols = aligned(parity * SPAN, SPAN)
+        u_tile = left[0, :, u_cols].astype(jnp.float32)
+        square = u_tile * u_tile
+        bend = jnp.tanh(GELU_C * u_tile * (1.0 + GELU_A * square))
+        slope = 0.5 * (1.0 + bend) + (0.5 * GELU_C) * u_tile * (1.0 - bend * bend) * (
+            1.0 + 3.0 * GELU_A * square
+        )
+        du_tile = (contract_last(dz_v[...], own_part[parity]) * slope).astype(jnp.bfloat16)
+        kv_b[0, :, u_cols] = du_tile
+        du_store(tile, parity).start()
+        fresh = contract_last(du_tile, turned[aligned(parity * D, D), :])
+
+        @pl.when(tile == 0)
+        def _():
+            dq_acc[...] = fresh
+
+        @pl.when(tile > 0)
+        def _():
+            dq_acc[...] = dq_acc[...] + fresh
+
+        return carry
+
+    lax.fori_loop(0, hidden_tiles, ff_tile, 0)
+    for tile in range(hidden_tiles - 2, hidden_tiles):
+        du_store(tile, tile % 2).wait()
+    for copy in wide_loads:
+        copy.wait()
+    for copy in block_copies(1):
+        copy.start()
+
+    def row_back(upstream, hat, scale, gain):
+        scaled = upstream * gain
+        return scale * (
+            scaled
+            - jnp.mean(scaled, axis=-1, keepdims=True)
+            - hat * jnp.mean(scaled * hat, axis=-1, keepdims=True)
+        )
+
+    def column_sum(values):
+        return jnp.sum(values, axis=0, keepdims=True)
+
+    def hidden_back(step, carry):
+        gain1, gain2, bias1, bias2 = carry
+        rows = aligned(step * CHAIN, CHAIN)
+        upstream = dq_acc[rows, :]
+        hat = hat2_v[rows, :].astype(jnp.float32)
+        grad_h = dy_v[rows, :].astype(jnp.float32) + row_back(
+            upstream, hat, lse_v[1, rows, 0:1], gain_ref[2:3, :]
+        )
+        gain2, bias2 = gain2 + column_sum(upstream * hat), bias2 + column_sum(upstream)
+        dq_acc[rows, :] = grad_h
+        hat = hat1_v[rows, :].astype(jnp.float32)
+        datt_v[rows, :] = row_back(grad_h, hat, lse_v[0, rows, 0:1], gain_ref[1:2, :]).astype(
+            jnp.bfloat16
+        )
+        return gain1 + column_sum(grad_h * hat), gain2, bias1 + column_sum(grad_h), bias2
+
+    zero = jnp.zeros((1, D), jnp.float32)
+    sums = lax.fori_loop(0, BLK // CHAIN, hidden_back, (zero,) * 4)
+    row = lax.broadcasted_iota(jnp.int32, (8, D), 0)
+    norm_v[...] = norm_ref[...]
+    for place, value in zip((1, 2, 5, 6), sums):
+        norm_v[...] = norm_v[...] + jnp.where(row == place, value, 0.0)
+    tick(FF_TICKS - 1)
+    stores = [
+        pltpu.make_async_copy(dq_acc, dh_hbm, sem_res.at[0]),
+        pltpu.make_async_copy(datt_v, datt_hbm, sem_res.at[1]),
+    ]
+    lse_load = pltpu.make_async_copy(lse_hbm, lse_v, sem_in.at[0])
+    for copy in stores + [lse_load]:
+        copy.start()
+    for place in range(4):
+        out_loads[place].wait()
+        do_v[:, pl.ds(place * TILE, TILE)] = contract_last(
+            datt_v[...], term[place // 2, place % 2, :, pl.ds(0, D)]
+        ).astype(jnp.bfloat16)
+    for copy in stores + [lse_load]:
+        copy.wait()
     dq_acc[...] = jnp.zeros_like(dq_acc)
-    for load in loads:
-        load.wait()
 
     def attend(kv_ref, own, visible, begin):
         def body(group, carry):
-            for extra in range(2):
-                tick(begin + 2 * group + extra)
+            tick(begin + group)
             for member in range(PAIRED):
                 grad_block(
                     q_v, do_v, o_v, lse_v, kv_ref, dq_acc, turned, group * PAIRED + member, own, visible
@@ -1055,17 +1192,17 @@
         if kv_b.shape[0] > 1:
             for copy in block_copies(index + 1):
                 copy.start()
-        begin = slot * block_ticks
+        begin = FF_TICKS + slot * block_ticks
         attend(kv_b.at[place], False, visible, begin)
 
         def weight_terms(step, inner):
-            tick(begin + 2 * groups + step)
+            tick(begin + groups + step)
             rows = aligned(step * 512, 512)
             for part in range(2):
                 cols = pl.ds(part * D, D)
                 product = dot_dims(a_b[place, :, rows], turned[cols, :], 0, 1)
                 for down in range(2):
-                    if fresh:
+                    if shallow:
                         target = gkv.at[aligned(step * 512 + down * TILE, TILE), cols]
                     else:
                         target = term.at[step, down, :, pl.ds((part + 1) * D, D)]
@@ -1091,7 +1228,7 @@
         return carry
 
     lax.fori_loop(0, slots, each_slot, 0)
-    begin = slots * block_ticks
+    begin = FF_TICKS + slots * block_ticks
     own_place = (slots + 1) % kv_b.shape[0]
     for copy in block_copies(slots + 1):
         copy.wait()
@@ -1102,7 +1239,7 @@
     x_load.start()
 
     def last_terms(step, carry):
-        tick(begin + 2 * groups + step)
+        tick(begin + groups + step)
         rows = aligned(step * TILE, TILE)
         a_rows = a_b[own_place, :, rows]
         up, down = step // 2, step % 2
@@ -1110,12 +1247,12 @@
         for part in range(2):
             cols = pl.ds(part * D, D)
             target = term.at[up, down, :, pl.ds((part + 1) * D, D)]
-            earlier = gkv[rows, cols] if fresh else target[...]
+            earlier = gkv[rows, cols] if shallow else target[...]
             target[...] = (earlier + dot_dims(a_rows, turned[cols, :], 0, 1)).astype(jnp.bfloat16)
         return carry
 
     lax.fori_loop(0, 4, last_terms, 0)
-    ready = begin + 2 * groups + 4
+    ready = begin + groups + 4
     assert ready <= ranges[-1][0] - 2 or n_ctx > 4
     da_acc = dq_acc
 
@@ -1138,7 +1275,7 @@
     lax.fori_loop(0, left_over, flush_chain, 0)
     ready = ready + left_over
     x_load.wait()
-    gain = gain_ref[...]
+    gain = gain_ref[0:1, :]
 
     def norm_grad(step, carry):
         gain_sum, bias_sum = carry
@@ -1156,23 +1293,14 @@
         centre = values - jnp.mean(values, axis=-1, keepdims=True)
         scale = lax.rsqrt(jnp.mean(centre * centre, axis=-1, keepdims=True) + EPS)
         centre = centre * scale
-        scaled = upstream * gain
-        da_acc[rows, :] = scale * (
-            scaled
-            - jnp.mean(scaled, axis=-1, keepdims=True)
-            - centre * jnp.mean(scaled * centre, axis=-1, keepdims=True)
-        )
-        gain_sum = gain_sum + jnp.sum(upstream * centre, axis=0, keepdims=True)
-        bias_sum = bias_sum + jnp.sum(upstream, axis=0, keepdims=True)
-        return gain_sum, bias_sum
-
-    zero = jnp.zeros((1, D), jnp.float32)
+        da_acc[rows, :] = row_back(upstream, centre, scale, gain)
+        return gain_sum + column_sum(upstream * centre), bias_sum + column_sum(upstream)
+
     gain_sum, bias_sum = lax.fori_loop(0, BLK // CHAIN, norm_grad, (zero, zero))
     ready = ready + BLK // CHAIN // 2
     result = pltpu.make_async_copy(da_acc, grad_out, sem_res.at[0])
     result.start()
-    row = lax.broadcasted_iota(jnp.int32, (8, D), 0)
-    norm_v[...] = norm_ref[...] + jnp.where(row == 0, gain_sum, 0.0) + jnp.where(row == 4, bias_sum, 0.0)
+    norm_v[...] = norm_v[...] + jnp.where(row == 0, gain_sum, 0.0) + jnp.where(row == 4, bias_sum, 0.0)
     for place, peer in enumerate([core_peer, side_peer, grp_peer] + level_peers):
         move = remote(norm_v, norm_in.at[place], norm_s.at[place], norm_r.at[place], peer)
         move.start()
@@ -1204,22 +1332,12 @@
     norm_result.wait()
 
 
-def backward_part(n_ctx, slot_vec, gain, norms, raw, q, kv, a, o, do, lse, weight, pieces):
+def backward_part(n_ctx, slot_vec, gains, norms, saved, weights, ffn):
     slots = n_ctx // 2
     levels = n_ctx.bit_length() - 1
     depth = 14 if n_ctx == 4 else 10
-    every = (slots + 1) * BLK
-    if slots > 2:
-        active, dz, ffn, du, datt = pieces
-        terms = [
-            contract_rows(left_side, right_side).astype(jnp.bfloat16)
-            for left_side, right_side in ((active, dz), (ffn, du), (o, datt))
-        ]
-        widths = [(term.shape[0] // 4, term.shape[1]) for term in terms]
-        pieces = [term.reshape(2, 2, width[0], width[1]) for term, width in zip(terms, widths)]
-    else:
-        widths = [(pieces[0].shape[1] // 4, D), (D // 4, pieces[3].shape[1]), (D // 4, D)]
-    widths = widths + [(D // 4, 3 * D)]
+    hidden = weights[1].shape[1]
+    widths = [(hidden // 4, D), (D // 4, hidden), (D // 4, D), (D // 4, 3 * D)]
     low, full = jnp.bfloat16, jnp.float32
     dma = pltpu.SemaphoreType.DMA
     hbm = pl.BlockSpec(memory_space=pl.ANY)
@@ -1235,9 +1353,16 @@
         zshapes.append(pltpu.VMEM((depth, rows, cols), low))
     return pl.pallas_call(
         functools.partial(backward_kernel, n_ctx, widths),
-        out_shape=[shape(width, low) for width in widths] + [shape((BLK, D), full), shape((8, D), full)],
-        in_specs=[pl.BlockSpec(memory_space=pltpu.SMEM), vmem, vmem] + [hbm] * (8 + len(pieces)),
-        out_specs=[hbm] * 6,
+        out_shape=[shape(width, low) for width in widths] + [
+            shape((BLK, D), full),
+            shape((8, D), full),
+            shape((BLK, D), full),
+            shape((BLK, hidden), low),
+            shape((BLK, D), low),
+        ],
+        in_specs=[pl.BlockSpec(memory_space=pltpu.SMEM), vmem, vmem]
+        + [hbm] * (len(saved) + len(weights) + len(ffn)),
+        out_specs=[hbm] * 9,
         scratch_shapes=[
             pltpu.VMEM((BLK, D), low),
             pltpu.VMEM((BLK, D), low),
@@ -1261,9 +1386,9 @@
             pltpu.VMEM((depth, TILE, TILE), low),
             pltpu.VMEM((4, 2, 2, TILE, TILE), low),
         ]
-        + ([pltpu.VMEM((2, 4, BLK, TILE), low), pltpu.VMEM((4, BLK, TILE), low)] if slots <= 2 else [])
+        + [pltpu.VMEM((2, 4, BLK, TILE), low), pltpu.VMEM((4, BLK, TILE), low)]
         + zshapes
-        + [dma((5,)), dma((2, buffers)), dma((4,)), dma((2, 4)), dma((depth,)), dma((2,))]
+        + [dma((12,)), dma((2, buffers)), dma((4,)), dma((2, 4)), dma((4, 2)), dma((depth,)), dma((2,))]
         + [dma((depth,))] * (8 + 4 * levels)
         + [dma((chain,))] * 4
         + [dma((3 + levels,))] * 2,
@@ -1274,17 +1399,11 @@
         name="attend_back_reduce",
     )(
         slot_vec,
-        gain,
+        gains,
         norms,
-        raw,
-        q,
-        kv,
-        a,
-        o,
-        do,
-        lse,
-        weight,
-        *pieces,
+        *saved,
+        *weights,
+        *ffn,
     )
 
 
@@ -1308,47 +1427,43 @@
         w_down,
     )
 
+    def normalised(values):
+        centre = values - jnp.mean(values, axis=-1, keepdims=True)
+        scale = lax.rsqrt(jnp.mean(centre * centre, axis=-1, keepdims=True) + EPS)
+        return centre * scale, jnp.broadcast_to(scale, (BLK, 128))
+
     branch = jnp.dot(attn_low, full_out, preferred_element_type=jnp.float32)
-    post_attn, attn_back = jax.vjp(layer_norm, branch, norm_gains[1], norm_biases[1])
-    hidden = tokens + post_attn
-    pre_ffn, ffn_back = jax.vjp(layer_norm, hidden, norm_gains[2], norm_biases[2])
-    ffn_low = pre_ffn.astype(jnp.bfloat16)
+    hat1, rstd1 = normalised(branch)
+    hidden = tokens + hat1 * norm_gains[1] + norm_biases[1]
+    hat2, rstd2 = normalised(hidden)
+    ffn_low = (hat2 * norm_gains[2] + norm_biases[2]).astype(jnp.bfloat16)
     upward = jnp.dot(ffn_low, full_up, preferred_element_type=jnp.float32)
-    activated, gelu_back = jax.vjp(gelu_tanh, upward)
-    active_low = activated.astype(jnp.bfloat16)
+    active_low = gelu_tanh(upward).astype(jnp.bfloat16)
     downward = jnp.dot(active_low, full_down, preferred_element_type=jnp.float32)
     post_ffn, post_back = jax.vjp(layer_norm, downward, norm_gains[3], norm_biases[3])
     result = (hidden + post_ffn).astype(jnp.bfloat16).reshape(1, 1, BLK, D)
-    seed_grad = out_grad.reshape(BLK, D).astype(jnp.float32)
-    grad_down_in, gain_grad3, bias_grad3 = post_back(seed_grad)
-    down_low = grad_down_in.astype(jnp.bfloat16)
-    grad_active = contract_last(down_low, full_down)
-    up_low = gelu_back(grad_active)[0].astype(jnp.bfloat16)
-    grad_pre_ffn, gain_grad2, bias_grad2 = ffn_back(contract_last(up_low, full_up))
-    grad_hidden = seed_grad + grad_pre_ffn
-    grad_branch, gain_grad1, bias_grad1 = attn_back(grad_hidden)
-    branch_low = grad_branch.astype(jnp.bfloat16)
-    grad_out_low = contract_last(branch_low, full_out).astype(jnp.bfloat16)
-
+    seed_low = out_grad.reshape(BLK, D)
+    grad_down_in, gain_grad3, bias_grad3 = post_back(seed_low.astype(jnp.float32))
     zero_row = jnp.zeros((D,), jnp.float32)
-    norms = jnp.stack(
-        [zero_row, gain_grad1, gain_grad2, gain_grad3, zero_row, bias_grad1, bias_grad2, bias_grad3]
-    )
-    summed_down, summed_up, summed_out, summed_qkv, grad_tokens, norm_total = backward_part(
+    norms = jnp.stack([zero_row] * 3 + [gain_grad3] + [zero_row] * 3 + [bias_grad3])
+    summed_down, summed_up, summed_out, summed_qkv, grad_tokens, norm_total, grad_hidden = backward_part(
         n_ctx,
         slot_vec,
-        norm_gains[0:1],
+        norm_gains,
         norms,
-        raw,
-        queries,
-        keys_values,
-        every_low,
-        attn_low,
-        grad_out_low,
-        lse,
-        full_qkv,
-        [active_low, down_low, ffn_low, up_low, branch_low],
-    )
+        [raw, queries, keys_values, every_low, attn_low, lse, full_qkv],
+        [full_out, full_up, full_down],
+        [
+            active_low,
+            grad_down_in.astype(jnp.bfloat16),
+            ffn_low,
+            upward.astype(jnp.bfloat16),
+            hat1.astype(jnp.bfloat16),
+            hat2.astype(jnp.bfloat16),
+            jnp.stack([rstd1, rstd2]),
+            seed_low,
+        ],
+    )[:7]
     grad_input = (grad_hidden + grad_tokens).reshape(1, 1, BLK, D)
     summed_down, summed_up, summed_out, summed_qkv = (
         total.astype(jnp.float32) for total in (summed_down, summed_up, summed_out, summed_qkv)

time: 366 us -> 361 us (0.986)
  matrix products: 43.6 us -> 18.3 us
  Pallas kernels: 280 us -> 305 us
    dot_general x3 -> x0, matrix products: 24.5 us -> none  [dot_dims(): lax.dot_general(left_side, right_side, (((left_dim,), (right_dim,)), ((),...]
    pallas_call x1, Pallas kernels: 176 us -> 200 us  [backward_part(): pl.pallas_call(functools.partial(backward_kernel, n_ctx, widths), out_sha...]
where the time goes in v6:
time: 361 us; the launch traced here: 356 us
  Pallas kernels  305 us (84%)
  other arithmetic  21.8 us (6%)
  matrix products  18.3 us (5%)
  local copies, waits for them, and re-layouts  6.13 us (2%)
  between operations  4.47 us (1%)
    pallas_call x1, Pallas kernels, backward_part(): pl.pallas_call(functools.partial(backward_kernel, n_ctx, widths), out_sha...  200 us
    pallas_call x1, Pallas kernels, forward_part(): pl.pallas_call(functools.partial(forward_kernel, n_ctx), out_shape=[shape...  104 us
    dot_general x1, matrix products, per_device(): upward = jnp.dot(ffn_low, full_up, preferred_element_type=jnp.float32)  8.59 us
    convert_element_type x4, other arithmetic, per_device(): total.astype(jnp.float32)  8.08 us

profile of v6, /device:TPU:0, one launch (start us, length us, event | category | flops | bytes accessed | tf_op | source)
XLA Modules:
  0.0 355.5 jit_solution(308407006715628989)
XLA Ops:
  0.6 1.3 fusion.20
  5.2 0.6 pad_add_fusion.refs_0_
  5.8 1.5 fusion.18
  7.3 104.4 %gather_attend.1 = (bf16[1536,1024]{1,0:T(8,128)(2,1)}, bf16[512,1024]{1,0:T(8,128)(2,1)}, bf16[1536,2048]{1,0:T(8,128)(2,1)}, bf16[512,1024]{1,0:T(8,128)(2,1)}...) custom-call(s32[2]{0:T(128)} %pad_add_fusion.refs_0_, ...), custom_call_target="tpu_custom_call" | custom-call | flops 21474836480 | bytes 67108864 | tf_op jit(solution)/shard_map/gather_attend/pallas_call | solution.py:533
  111.7 3.3 fusion.21
  115.0 0.0 slice-start.2
  115.0 0.3 multiply_reduce_fusion.2
  115.4 0.1 stack_broadcast_in_dim.4
  115.5 0.7 copy-done.4
  116.2 1.6 fusion.15
  117.9 0.3 multiply_reduce_fusion.1
  118.2 0.1 stack_broadcast_in_dim.5
  118.4 0.8 pad_maximum_fusion.refs_19_
  119.2 1.4 multiply_convert_fusion
  120.6 0.0 slice-start.1
  120.7 8.6 %fusion.16 = (bf16[512,4096]{1,0:T(8,128)(2,1)}, bf16[512,4096]{1,0:T(8,128)(2,1)}) fusion(bf16[512,1024]{1,0:T(8,128)(2,1)S(1)} %get-tuple-element.51.refs_15_, bf16[1024,4096]{1,0:T(8,128)(2,1)S(1)} %bitcast.46), kind=kOutput, calls=%fused_computation.41 | convolution fusion | flops 4315938816 | bytes 17825792 | tf_op jit(solution)/shard_map/dot_general | solution.py:1440
  129.3 6.4 %fusion.22 = (f32[512]{0:T(512)S(1)}, f32[512,1024]{1,0:T(8,128)S(1)}) fusion(bf16[512,4096]{1,0:T(8,128)(2,1)} %get-tuple-element.48.refs_13_, bf16[4096,1024]{1,0:T(8,128)(2,1)S(1)} %bitcast.44), kind=kOutput, calls=%fused_computation.47 | convolution fusion | flops 4295491072 | bytes 14682112 | tf_op jit(solution)/shard_map/dot_general | solution.py:1442
  135.7 0.0 copy-start
  135.7 0.3 multiply_reduce_fusion
  136.1 0.9 copy-done
  136.9 0.9 fusion.10
  137.8 2.0 fusion.14
  139.8 1.2 add_convert_fusion.refs_14_
  140.9 0.6 stack.20.refs_2_
  141.6 200.4 %attend_back_reduce.1 = (bf16[1024,1024]{1,0:T(8,128)(2,1)}, bf16[256,4096]{1,0:T(8,128)(2,1)}, bf16[256,1024]{1,0:T(8,128)(2,1)}, bf16[256,3072]{1,0:T(8,128)(2...) custom-call(s32[1]{0:T(128)} %bitcast.2.refs_0_, ...), custom_call_target="tpu_custom_call" | custom-call | flops 42949672960 | bytes 67108864 | tf_op jit(solution)/shard_map/attend_back_reduce/pallas_call | solution.py:1354
  342.0 4.2 %add_bitcast_fusion = f32[1,1,512,1024]{3,2,1,0:T(8,128)} fusion(f32[512,1024]{1,0:T(8,128)} %get-tuple-element.33, f32[512,1024]{1,0:T(8,128)} %get-tuple-element.34), kind=kLoop, calls=%fused_computation.17 | loop fusion | flops 524288 | bytes 6291456 | tf_op jit(solution)/shard_map/reshape | solution.py:1467
  346.2 0.6 fusion.17
  346.8 1.1 convert_element_type.49
  347.9 2.0 convert_element_type.48
  349.9 0.2 copy-done.2
  350.1 2.5 convert_element_type.50
  352.6 2.5 convert_element_type.51
  (30 shorter events, 0.1 us)
Async XLA Ops:
  115.0 1.2 copy-start.4
  115.0 5.6 %slice-start.2 = ((s8[8388608]{0:T(1024)(128)(4,1)}), s8[4194304]{0:T(1024)(128)(4,1)S(1)}, s32[]{:S(2)}) async-start(s8[8388608]{0:T(1024)(128)(4,1)} %bitcast.45), calls=%async_computation.2 | async-start | bytes 8388608
  116.2 4.4 %slice-start.3 = ((s8[8388608]{0:T(1024)(128)(4,1)}), s8[4194304]{0:T(1024)(128)(4,1)S(1)}, s32[]{:S(2)}) async-start(s8[8388608]{0:T(1024)(128)(4,1)} %bitcast.45), calls=%async_computation.3 | async-start | bytes 8388608
  119.2 10.0 %slice-start = ((s8[8388608]{0:T(1024)(128)(4,1)}), s8[4194304]{0:T(1024)(128)(4,1)S(1)}, s32[]{:S(2)}) async-start(s8[8388608]{0:T(1024)(128)(4,1)} %bitcast.43), calls=%async_computation | async-start | bytes 8388608
  120.6 8.6 %copy-start.5 = (bf16[512,1024]{1,0:T(8,128)(2,1)}, bf16[512,1024]{1,0:T(8,128)(2,1)S(1)}, u32[]{:S(2)}) copy-start(bf16[512,1024]{1,0:T(8,128)(2,1)S(1)} %get-tuple-element.51.refs_15_) | copy-start | bytes 3145732
  120.6 8.6 %slice-start.1 = ((s8[8388608]{0:T(1024)(128)(4,1)}), s8[4194304]{0:T(1024)(128)(4,1)S(1)}, s32[]{:S(2)}) async-start(s8[8388608]{0:T(1024)(128)(4,1)} %bitcast.43), calls=%async_computation.1 | async-start | bytes 8388608
  135.7 1.2 copy-start
  342.0 4.2 %copy-start.7 = (f32[8,1024]{1,0:T(8,128)S(1)}, f32[8,1024]{1,0:T(8,128)}, u32[]{:S(2)}) copy-start(f32[8,1024]{1,0:T(8,128)} %get-tuple-element.39) | copy-start | bytes 98308
  342.0 4.8 %copy-start.6 = (bf16[256,1024]{1,0:T(8,128)(2,1)S(1)}, bf16[256,1024]{1,0:T(8,128)(2,1)}, u32[]{:S(2)}) copy-start(bf16[256,1024]{1,0:T(8,128)(2,1)} %get-tuple-element.36) | copy-start | bytes 1572868
  346.2 1.7 copy-start.3
  347.9 2.2 copy-start.2
  350.1 2.5 copy-start.1
